TPU v7x, 128 devices: a whole 4x4x4 slice. The times are simulated.
128 devices in a mesh: row: 8 (over x, core), col: 16 (over y, z).
Axes of the slice: x: 4, y: 4, z: 4, core: 2. Of those that a mesh axis runs over, the one named last changes fastest.
Arguments:
- parent_front: float32 [16384, 16384], P('row', 'col'), as said below
- child_panels: float32 [8, 4096, 512], P('row', 'col'), may hold values from -6 to 6
- child_inverses: float32 [8, 512, 512], P('row'), as said below
- parent_index: int32 [8, 16], replicated, may hold values from 2 to 63, as said below
Outputs:
- panel: float32 [16384, 512], P('row')
- schur: float32 [16384, 16384], P('row', 'col')
Inputs may be any that keep to these rules, and one draw needn't show every extreme that they name: `parent_index`: entry (g, u) names the parent tile that receives tile row and tile column u of child g's update. Seen in blocks of 4 consecutive tiles, each child names every block exactly once, and at a given u the children name different blocks. No entry names one of the first 2 tiles. `parent_front`: Symmetric. In its leading 2 * 256 rows and columns, each diagonal entry is positive and exceeds the sum of magnitudes of the other entries of its row within that block. `child_inverses`: each matrix is lower triangular with a positive diagonal.
All inputs are finite; a program needn't handle non-finite values.
Results may differ from a plain program's by a relative error of at most 0.0003.
Values sent between devices are 32-bit elements; how exact they have to be, the bound alone decides.
A program may use at most 128 MiB of HBM per device.

v0:
```python
import jax
import jax.numpy as jnp
from jax import lax
from jax.sharding import PartitionSpec as P

TILE = 256
PCT = 4
NSP = 2


def from_root(block, axis, holder):
    block = jnp.where(lax.axis_index(axis) == holder, block, jnp.zeros_like(block))
    return lax.psum(block, axis)


def product(matrix_a, matrix_b):
    return jnp.dot(
        matrix_a, matrix_b, precision=lax.Precision.HIGHEST, preferred_element_type=jnp.float32
    )


def product_rows(matrix_a, matrix_b):
    return lax.dot_general(
        matrix_a,
        matrix_b,
        (((1,), (1,)), ((), ())),
        precision=lax.Precision.HIGHEST,
        preferred_element_type=jnp.float32,
    )


def place_tiles(received, row_tiles, col_tiles, live_mask, tile_count):
    target = row_tiles * PCT + col_tiles
    onehot = (target[None, :] == jnp.arange(tile_count)[:, None]).astype(jnp.float32) * live_mask[
        None, :
    ]
    flat_tiles = received.reshape(received.shape[0], TILE * TILE)
    return product(onehot, flat_tiles)


def per_device(parent_front, child_panels, child_inverses, parent_index):
    row_devices = lax.axis_size("row")
    col_devices = lax.axis_size("col")
    here_row = lax.axis_index("row")
    here_col = lax.axis_index("col")
    per_block = col_devices // row_devices
    row_count = PCT * per_block
    tile_count = row_count * PCT
    own_factor = product_rows(child_panels[0], child_inverses[0])
    my_list = lax.dynamic_index_in_dim(parent_index, here_row, 0, keepdims=False)
    block_of = parent_index // PCT
    update_col = product_rows(lax.all_gather(own_factor, "col", axis=0, tiled=True), own_factor)
    dest_row = my_list // PCT // per_block
    tile_ids = jnp.arange(col_devices, dtype=jnp.int32)
    same_dest = (dest_row[None, :] == dest_row[:, None]) & (tile_ids[None, :] < tile_ids[:, None])
    slot_index = jnp.sum(same_dest.astype(jnp.int32), axis=1)
    position = dest_row * per_block + slot_index
    send_order = jnp.zeros((col_devices,), jnp.int32).at[position].set(tile_ids)
    outgoing = update_col.reshape(col_devices, TILE, TILE)[send_order].reshape(
        row_devices, per_block, TILE, TILE
    )
    arrived = lax.all_to_all(outgoing, "row", split_axis=0, concat_axis=0, tiled=True)
    local_mask = block_of // per_block == here_row
    slot_rank = jnp.cumsum(local_mask.astype(jnp.int32), axis=1) - 1
    slot_ids = jnp.arange(per_block, dtype=jnp.int32)
    slot_pick = (
        local_mask[:, :, None] & (slot_rank[:, :, None] == slot_ids[None, None, :])
    ).astype(jnp.int32)
    row_tile = jnp.sum(parent_index[:, :, None] * slot_pick, axis=1) - here_row * row_count
    sent_to = lax.dynamic_index_in_dim(block_of, here_col, 1, keepdims=False)
    col_route = (sent_to[None, :] == jnp.arange(col_devices)[:, None]).astype(jnp.float32)
    outgoing_cols = product(col_route, arrived.reshape(row_devices, -1)).reshape(
        col_devices, per_block, TILE, TILE
    )
    arrived_cols = lax.all_to_all(outgoing_cols, "col", split_axis=0, concat_axis=0, tiled=True)
    col_match = (block_of == here_col).astype(jnp.int32)
    col_tile = parent_index - here_col * PCT
    rows_from = jnp.sum(row_tile[:, None, :] * col_match[:, :, None], axis=0)
    cols_from = jnp.sum(col_tile * col_match, axis=0)
    live_from = jnp.sum(col_match, axis=0).astype(jnp.float32)
    cols_flat = (cols_from[:, None] + jnp.zeros_like(rows_from)).reshape(-1)
    live_flat = (live_from[:, None] + jnp.zeros(rows_from.shape, jnp.float32)).reshape(-1)
    contrib = place_tiles(
        arrived_cols.reshape(-1, TILE, TILE),
        rows_from.reshape(-1),
        cols_flat,
        live_flat,
        tile_count,
    )
    contrib = (
        contrib.reshape(row_count, PCT, TILE, TILE)
        .transpose(0, 2, 1, 3)
        .reshape(row_count * TILE, PCT * TILE)
    )
    work_matrix = parent_front - contrib
    identity = jnp.eye(TILE, dtype=jnp.float32)
    owner = (here_row == 0) & (here_col == 0)
    row_tile_index = here_row * row_count + jnp.arange(row_count * TILE) // TILE
    columns = []
    for step in range(NSP):
        offset = step * TILE
        diag_tile = jnp.where(
            owner, work_matrix[offset : offset + TILE, offset : offset + TILE], identity
        )
        pivot_tile = jnp.linalg.cholesky(diag_tile)
        inverse = lax.linalg.triangular_solve(pivot_tile, identity, left_side=True, lower=True)
        pivot_pair = from_root(jnp.stack([pivot_tile, inverse]), "row", 0)
        pivot_tile = pivot_pair[0]
        inverse = pivot_pair[1]
        factored = product_rows(work_matrix[:, offset : offset + TILE], inverse)
        factored = jnp.where(row_tile_index[:, None] < step, jnp.zeros_like(factored), factored)
        current = factored[offset : offset + TILE]
        rows_panel, inverse = (
            from_root(
                factored.at[offset : offset + TILE].set(
                    jnp.where(here_row == 0, pivot_tile, current)
                ),
                "col",
                0,
            ),
            from_root(inverse, "col", 0),
        )
        source = from_root(rows_panel, "row", here_col // per_block)
        col_panel = lax.dynamic_slice_in_dim(
            source, here_col % per_block * PCT * TILE, PCT * TILE, 0
        )
        work_matrix = work_matrix - product_rows(rows_panel, col_panel)
        columns.append(rows_panel)
    return (jnp.concatenate(columns, axis=1), work_matrix)


def solution(mesh):
    placed = (P("row", "col"), P("row", "col", None), P("row", None, None), P())
    return jax.shard_map(
        per_device,
        mesh=mesh,
        in_specs=placed,
        out_specs=(P("row", None), P("row", "col")),
        check_vma=False,
    )
```

profile of v0, /device:TPU:0, one launch (start us, length us, event | category | flops | bytes accessed | tf_op | source)
XLA Modules:
  0.0 993.7 jit_solution(9929762409883196764)
XLA Ops:
  7.2 1.2 copy-done
  8.4 2.9 fusion.5
  14.3 70.5 %all-gather.2.cloned.1.call-done = f32[4096,512]{1,0:T(8,128)} async-done(((f32[256,512]{1,0:T(8,128)}), f32[4096,512]{1,0:T(8,128)}) %all-gather.2.cloned.1.call-update) | async-done | bytes 8388624 | tf_op jit(solution)/shard_map/all_gather | solution.py:52
  84.8 10.6 %fusion.69 = f32[4096,256]{1,0:T(8,128)} fusion(f32[4096,512]{1,0:T(8,128)} %all-gather.2.cloned.1.call-done, f32[256,512]{1,0:T(8,128)} %fusion.5), kind=kOutput, calls=%fused_computation.186 | convolution fusion | flops 6442450944 | bytes 13107200 | tf_op jit(solution)/shard_map/dot_general | solution.py:23
  95.4 5.0 gather_fusion
  100.4 4.8 all-to-all-start
  105.5 49.4 %all-to-all-done = f32[8,2,256,256]{3,2,1,0:T(8,128)} async-done(((f32[8,2,256,256]{3,2,1,0:T(8,128)}), f32[8,2,256,256]{3,2,1,0:T(8,128)}, u32[]{:S(2)}, u32[]{:S(2)}) %all-to-all-start) | async-done | bytes 4194336 | tf_op jit(solution)/shard_map/all_to_all | solution.py:62
  155.0 4.6 copy.52
  159.6 3.7 fusion.54
  163.3 8.1 copy.34
  171.3 5.3 all-to-all-start.1
  177.8 9.1 copy.37
  186.9 134.8 %all-to-all-done.1 = f32[16,2,256,256]{3,2,1,0:T(8,128)} async-done(((f32[16,2,256,256]{3,2,1,0:T(8,128)}), f32[16,2,256,256]{3,2,1,0:T(8,128)}, u32[]{:S(2)}, u32[]{:S(2)}) %all-to-all-start.1) | async-done | bytes 8388640 | tf_op jit(solution)/shard_map/all_to_all | solution.py:75
  321.7 17.3 %fusion.2 = f32[8,256,4,256]{3,0,1,2:T(8,128)} fusion(f32[32]{0:T(128)S(1)} %mul.78, s32[8,4]{0,1:T(4,128)S(1)} %multiply_add_fusion, s32[32]{0:T(128)S(1)} %add.154, f32[4,8,256,256]{3,2,1,0:T(8,128)} %bitcast.51), kind=kOutput, calls=%fused_computation.12 | convolution fusion | flops 805308416 | bytes 16777600 | tf_op jit(solution)/shard_map/dot_general | solution.py:17
  339.0 10.8 %copy.36 = f32[8,256,4,256]{1,0,3,2:T(8,128)} copy(f32[8,256,4,256]{3,0,1,2:T(8,128)} %fusion.2) | data formatting | bytes 16777216 | tf_op jit(solution)/shard_map/transpose | solution.py:92
  349.8 10.7 %copy.54 = f32[128,8,8,256]{3,1,2,0:T(8,128)} copy(f32[128,8,8,256]{3,2,1,0:T(8,128)} %bitcast.170) | data formatting | bytes 16777216
  360.5 11.9 %sub.79 = f32[2048,1024]{0,1:T(8,128)} subtract(f32[2048,1024]{0,1:T(8,128)} %copy.37, f32[2048,1024]{0,1:T(8,128)} %bitcast.169) | non-fusion elementwise | flops 2097152 | bytes 25165824 | tf_op jit(solution)/shard_map/sub | solution.py:95
  374.5 11.7 %cholesky.130 = f32[128,128]{1,0:T(8,128)S(1)} custom-call(f32[128,128]{1,0:T(8,128)S(1)} %cholesky.194), custom_call_target="Cholesky" | custom-call | tf_op jit(solution)/shard_map/jit(cholesky)/cholesky | solution.py:105
  386.3 10.0 %custom-call.13 = f32[1,128,128]{1,2,0:T(8,128)S(1)} custom-call(f32[1,128,128]{2,1,0:T(8,128)S(1)} %get-tuple-element.90), custom_call_target="InvertDiagBlocksLowerTriangular" | custom-call | tf_op jit(solution)/shard_map/jit(cholesky)/cholesky | solution.py:105
  396.7 11.7 %cholesky.147 = f32[128,128]{1,0:T(8,128)S(1)} custom-call(f32[128,128]{1,0:T(8,128)S(1)} %convolution_subtract_fusion.5), custom_call_target="Cholesky" | custom-call | tf_op jit(solution)/shard_map/jit(cholesky)/cholesky | solution.py:105
  410.6 4.1 while.6
  411.3 1.3 bitcast_dynamic-update-slice_fusion.4
  413.3 1.3 bitcast_dynamic-update-slice_fusion.4
  414.7 19.7 %custom-call.14 = f32[2,128,128]{1,2,0:T(8,128)S(1)} custom-call(f32[2,128,128]{2,1,0:T(8,128)S(1)} %get-tuple-element.42), custom_call_target="InvertDiagBlocksLowerTriangular" | custom-call | tf_op jit(solution)/shard_map/triangular_solve/custom-call.0 | solution.py:106
  436.3 63.0 %all-reduce.8.cloned.1.call-done = f32[2,256,256]{2,1,0:T(8,128)} async-done(((f32[2,256,256]{2,1,0:T(8,128)}), f32[2,256,256]{2,1,0:T(8,128)}) %all-reduce.8.cloned.1.call-update) | async-done | bytes 524304 | tf_op jit(solution)/shard_map/psum | solution.py:13
  499.3 5.1 convolution_select_fusion.1
  504.6 1.5 broadcast_select_fusion.3
  506.1 89.7 %all-reduce.10.cloned.1.call-done = f32[2048,256]{1,0:T(8,128)} async-done(((f32[2048,256]{1,0:T(8,128)}), f32[2048,256]{1,0:T(8,128)}) %all-reduce.10.cloned.1.call-update) | async-done | bytes 2097168 | tf_op jit(solution)/shard_map/psum | solution.py:13
  595.9 3.2 broadcast_select_fusion.2
  599.1 64.4 %all-reduce.12.cloned.1.call-done = f32[2048,256]{1,0:T(8,128)} async-done(((f32[2048,256]{1,0:T(8,128)}), f32[2048,256]{1,0:T(8,128)}) %all-reduce.12.cloned.1.call-update) | async-done | bytes 2097168 | tf_op jit(solution)/shard_map/psum | solution.py:13
  663.6 10.5 %convolution_subtract_fusion.1 = f32[2048,1024]{0,1:T(8,128)S(1)} fusion(f32[2048,1024]{0,1:T(8,128)} %sub.79, f32[2048,256]{1,0:T(8,128)S(1)} %copy-done.3, f32[2048,256]{1,0:T(8,128)} %all-reduce.12.cloned.1.call-done, s32[]{:T(128)S(6)} %select_n.189), kind=kOutput, calls=%fused_computation.10 | convolution fusion | flops 6444548096 | bytes 19922948 | tf_op jit(solution)/shard_map/dot_general | solution.py:23
  674.0 3.4 copy-done.2
  678.6 11.7 %cholesky.164 = f32[128,128]{1,0:T(8,128)S(1)} custom-call(f32[128,128]{1,0:T(8,128)S(1)} %cholesky.197), custom_call_target="Cholesky" | custom-call | tf_op jit(solution)/shard_map/jit(cholesky)/cholesky | solution.py:105
  691.0 9.8 custom-call.15
  701.3 11.7 %cholesky.181 = f32[128,128]{1,0:T(8,128)S(1)} custom-call(f32[128,128]{1,0:T(8,128)S(1)} %convolution_subtract_fusion.4), custom_call_target="Cholesky" | custom-call | tf_op jit(solution)/shard_map/jit(cholesky)/cholesky | solution.py:105
  715.2 4.1 while.7
  715.8 1.4 bitcast_dynamic-update-slice_fusion.5
  717.9 1.4 bitcast_dynamic-update-slice_fusion.5
  719.3 19.9 %custom-call.16 = f32[2,128,128]{1,2,0:T(8,128)S(1)} custom-call(f32[2,128,128]{2,1,0:T(8,128)S(1)} %get-tuple-element.43), custom_call_target="InvertDiagBlocksLowerTriangular" | custom-call | tf_op jit(solution)/shard_map/triangular_solve/custom-call.0 | solution.py:106
  741.2 60.2 %all-reduce.14.cloned.1.call-done = f32[2,256,256]{2,1,0:T(8,128)} async-done(((f32[2,256,256]{2,1,0:T(8,128)}), f32[2,256,256]{2,1,0:T(8,128)}) %all-reduce.14.cloned.1.call-update) | async-done | bytes 524304 | tf_op jit(solution)/shard_map/psum | solution.py:13
  801.5 5.1 convolution_select_fusion
  806.7 1.5 broadcast_select_fusion.1
  808.2 89.8 %all-reduce.16.cloned.1.call-done = f32[2048,256]{1,0:T(8,128)} async-done(((f32[2048,256]{1,0:T(8,128)}), f32[2048,256]{1,0:T(8,128)}) %all-reduce.16.cloned.1.call-update) | async-done | bytes 2097168 | tf_op jit(solution)/shard_map/psum | solution.py:13
  898.0 3.1 broadcast_select_fusion
  901.1 4.2 pad_maximum_fusion
  905.3 60.0 %all-reduce.18.cloned.1.call-done = f32[2048,256]{1,0:T(8,128)} async-done(((f32[2048,256]{1,0:T(8,128)}), f32[2048,256]{1,0:T(8,128)}) %all-reduce.18.cloned.1.call-update) | async-done | bytes 2097168 | tf_op jit(solution)/shard_map/psum | solution.py:13
  965.3 11.8 %convolution_subtract_fusion = f32[2048,1024]{0,1:T(8,128)} fusion(f32[2048,1024]{0,1:T(8,128)} %copy-done.2, f32[2048,256]{1,0:T(8,128)} %all-reduce.16.cloned.1.call-done, f32[2048,256]{1,0:T(8,128)} %all-reduce.18.cloned.1.call-done, s32[]{:T(128)S(6)} %select_n.189), kind=kOutput, calls=%fused_computation.9 | convolution fusion | flops 6444548096 | bytes 19922948 | tf_op jit(solution)/shard_map/dot_general | solution.py:23
  977.1 9.3 copy.44
  (100 shorter events, 17.7 us)
Async XLA Ops:
  7.2 1.2 copy-start
  7.2 77.6 %all-gather.2.cloned.1.call-start = ((), (), s32[]{:S(2)}) async-start(), calls=%async_computation.2 | async-start | bytes 8912896 | tf_op jit(solution)/shard_map/all_gather | solution.py:52
  100.4 4.9 copy-start.6
  100.4 54.5 %all-to-all-start = ((f32[8,2,256,256]{3,2,1,0:T(8,128)}), f32[8,2,256,256]{3,2,1,0:T(8,128)}, u32[]{:S(2)}, u32[]{:S(2)}) async-start(f32[8,2,256,256]{3,2,1,0:T(8,128)} %bitcast.172), calls=%async_computation | async-start | bytes 8388608 | tf_op jit(solution)/shard_map/all_to_all | solution.py:62
  171.3 150.4 %all-to-all-start.1 = ((f32[16,2,256,256]{3,2,1,0:T(8,128)}), f32[16,2,256,256]{3,2,1,0:T(8,128)}, u32[]{:S(2)}, u32[]{:S(2)}) async-start(f32[16,2,256,256]{3,2,1,0:T(8,128)} %copy.34), calls=%async_computation.1 | async-start | bytes 16777216 | tf_op jit(solution)/shard_map/all_to_all | solution.py:75
  176.7 322.7 %all-reduce.8.cloned.1.call-start = ((), (), s32[]{:S(2)}) async-start(), calls=%async_computation.3 | async-start | bytes 1048576 | tf_op jit(solution)/shard_map/psum | solution.py:13
  436.3 159.6 %all-reduce.10.cloned.1.call-start = ((), (), s32[]{:S(2)}) async-start(), calls=%async_computation.4 | async-start | bytes 4194304 | tf_op jit(solution)/shard_map/psum | solution.py:13
  499.3 5.2 copy-start.5
  506.0 157.5 %all-reduce.12.cloned.1.call-start = ((), (), s32[]{:S(2)}) async-start(), calls=%async_computation.5 | async-start | bytes 4194304 | tf_op jit(solution)/shard_map/psum | solution.py:13
  595.8 67.7 %copy-start.3 = (f32[2048,256]{1,0:T(8,128)S(1)}, f32[2048,256]{1,0:T(8,128)}, u32[]{:S(2)}) copy-start(f32[2048,256]{1,0:T(8,128)} %all-reduce.10.cloned.1.call-done) | copy-start | bytes 6291460
  599.1 202.4 %all-reduce.14.cloned.1.call-start = ((), (), s32[]{:S(2)}) async-start(), calls=%async_computation.6 | async-start | bytes 1048576 | tf_op jit(solution)/shard_map/psum | solution.py:13
  674.0 3.4 copy-start.2
  741.2 156.8 %all-reduce.16.cloned.1.call-start = ((), (), s32[]{:S(2)}) async-start(), calls=%async_computation.7 | async-start | bytes 4194304 | tf_op jit(solution)/shard_map/psum | solution.py:13
  801.5 5.2 copy-start.4
  808.2 157.1 %all-reduce.18.cloned.1.call-start = ((), (), s32[]{:S(2)}) async-start(), calls=%async_computation.8 | async-start | bytes 4194304 | tf_op jit(solution)/shard_map/psum | solution.py:13
  977.1 9.3 copy-start.1
Sparse Core Ops, SparseCore 0:
  11.4 73.3 all-gather.1
  436.4 62.9 all-reduce.7
  506.2 89.6 all-reduce.9
  599.2 64.3 all-reduce.11
  741.3 60.1 all-reduce.13
  808.3 89.6 all-reduce.15
  901.2 64.0 all-reduce.17
where the time goes:
time: 999 us; the launch traced here: 994 us
  waiting for transfers between devices  682 us (68%)
  other arithmetic  141 us (14%)
  local copies, waits for them, and re-layouts  71.9 us (7%)
  matrix products  70 us (7%)
  between operations  17.6 us (2%)
  starting transfers between devices  10.7 us (1%)
    psum x6, waiting for transfers between devices, from_root(): return lax.psum(block, axis)  427 us
    all_to_all x1, waiting for transfers between devices, per_device(): lax.all_to_all(outgoing_cols, 'col', split_axis=0, concat_axis=0, tiled=T...  135 us
    all_gather x1, waiting for transfers between devices, per_device(): lax.all_gather(own_factor, 'col', axis=0, tiled=True)  70.5 us
    another operation x13, other arithmetic, per_device(): pivot_tile = jnp.linalg.cholesky(diag_tile)  68.8 us
    all_to_all x1, waiting for transfers between devices, per_device(): lax.all_to_all(outgoing, 'row', split_axis=0, concat_axis=0, tiled=True)  49.4 us
    dot_general x6, matrix products, product_rows(): lax.dot_general(matrix_a, matrix_b, (((1,), (1,)), ((), ())), precision=l...  46 us
    another operation x3, other arithmetic, per_device(): lax.linalg.triangular_solve(pivot_tile, identity, left_side=True, lower=T...  39.6 us
    unnamed x18, local copies, waits for them, and re-layouts  38.4 us
  transfers between devices with their start and end apart: 9, of which 9 were waited for; matrix products, arithmetic and copies ran while one was open for 2% of the time, Pallas kernels for 0%

commit v1 on v0

v1 whole, which is shorter than its diff:
```python
import jax
import jax.numpy as jnp
from jax import lax
from jax.experimental import pallas as pl
from jax.experimental.pallas import tpu as pltpu
from jax.sharding import PartitionSpec as P

TILE = 256
CW = 512
PCT = 4
NSP = 2
ROWS = 8
COLS = 16
SIDE = 4
RT = 8
LEAD = NSP * TILE
PANEL_ROWS = RT * TILE
COL_WIDTH = PCT * TILE
TREE_CHUNKS = 8
MESH = pl.DeviceIdType.MESH
F32 = jnp.float32
BF16 = jnp.bfloat16


def product(matrix_a, matrix_b):
    return jnp.dot(
        matrix_a, matrix_b, precision=lax.Precision.HIGHEST, preferred_element_type=F32
    )


def product_rows(matrix_a, matrix_b):
    return lax.dot_general(
        matrix_a,
        matrix_b,
        (((1,), (1,)), ((), ())),
        precision=lax.Precision.HIGHEST,
        preferred_element_type=F32,
    )


def halves(value):
    high = value.astype(BF16)
    low = (value - high.astype(F32)).astype(BF16)
    return high, low


def three_pass(pair_a, pair_b, contract):
    def one(left, right):
        return lax.dot_general(left, right, (contract, ((), ())), preferred_element_type=F32)

    return one(pair_a[0], pair_b[0]) + (one(pair_a[0], pair_b[1]) + one(pair_a[1], pair_b[0]))


def wrap(value):
    return lax.rem(value + 2 * SIDE, SIDE)


def gather_kernel(
    own_ref, front_ref, all_ref, pan_ref, top_ref, lead_ref, send_sem, recv_sem, local_sem
):
    row = lax.axis_index("row")
    col = lax.axis_index("col")
    place_y = col // SIDE
    place_z = lax.rem(col, SIDE)
    chip = row // 2
    core = lax.rem(row, 2)
    counter = [0]

    def fresh():
        counter[0] += 1
        return counter[0] - 1

    def at(step_y, step_z):
        return wrap(place_y + step_y) * SIDE + wrap(place_z + step_z)

    def remote(src, dst, send, recv, to_row, to_col):
        return pltpu.make_async_remote_copy(
            src_ref=src,
            dst_ref=dst,
            send_sem=send_sem.at[send],
            recv_sem=recv_sem.at[recv],
            device_id=(to_row, to_col),
            device_id_type=MESH,
        )

    barrier = pltpu.get_barrier_semaphore()
    greeted = [
        (row, at(1, 0)),
        (row, at(-1, 0)),
        (row, at(0, 1)),
        (row, at(0, -1)),
        (row + 1 - 2 * core, col),
        (lax.rem(row + 2, ROWS), col),
        (lax.rem(row + 6, ROWS), col),
    ]
    for who in greeted:
        pl.semaphore_signal(barrier, inc=1, device_id=who, device_id_type=MESH)
    pl.semaphore_wait(barrier, len(greeted))

    started = []
    keep_own = pltpu.make_async_copy(own_ref, all_ref.at[col], local_sem.at[0])
    keep_own.start()

    def ring_events(half):
        if half == 0:
            place = lambda i, j: at(j, i)
        else:
            place = lambda i, j: at(i, j)
        base = half * 128
        sem = {}

        def key(*name):
            if name not in sem:
                sem[name] = fresh()
            return sem[name]

        def rows_of(part):
            if part == 0:
                return pl.ds(base, 128)
            return pl.ds(base, 64) if part == 1 else pl.ds(base + 64, 64)

        def make(i, j, part, to_i, to_j, name):
            source = own_ref if (i, j) == (0, 0) else all_ref.at[place(i, j)]
            return remote(
                source.at[rows_of(part)],
                all_ref.at[place(i, j), rows_of(part)],
                key(*name),
                key(*name),
                row,
                place(to_i, to_j),
            )

        pending = {}

        def go(name, *args):
            copy = make(*args, name)
            copy.start()
            pending[name] = copy
            started.append((copy, None))

        def arrived(name):
            pending[name].wait_recv()

        def quarter(d):
            return 1 if d == 1 else 2

        def first():
            for d in (1, -1):
                go(("a", d), 0, 0, 0, d, 0)

        def second():
            for e in (1, -1):
                go(("b", 0, e), 0, 0, 0, 0, e)

        def near(d):
            arrived(("a", d))
            go(("af", d), -d, 0, quarter(d), d, 0)
            for e in (1, -1):
                go(("b", -d, e), -d, 0, 0, 0, e)

        def far():
            arrived(("af", 1))
            arrived(("af", -1))
            for e in (1, -1):
                go(("b", 2, e), 2, 0, 0, 0, e)

        def cross(i):
            for e in (1, -1):
                arrived(("b", i, e))
                go(("bf", i, e), i, -e, quarter(e), 0, e)

        def last(i):
            for e in (1, -1):
                arrived(("bf", i, e))

        return first, second, near, far, cross, last

    root = col == 0
    trees = []
    for along_z, sign in ((True, 1), (True, -1), (False, 1), (False, -1)):
        place_a = wrap(sign * (place_z if along_z else place_y))
        place_b = wrap(sign * (place_y if along_z else place_z))
        to_a = at(0, sign) if along_z else at(sign, 0)
        to_b = at(sign, 0) if along_z else at(0, sign)
        send_a = ((place_b == 0) & (place_a < 3)) | ((place_b >= 1) & (place_a == 3))
        send_b = (place_a >= 1) & (place_b < 3)
        trees.append((to_a, to_b, send_a, send_b))

    def tree_event(tree, chunk):
        to_a, to_b, send_a, send_b = trees[tree]
        index_a, index_b = fresh(), fresh()
        size = LEAD // TREE_CHUNKS
        block = pan_ref.at[pl.ds(tree * LEAD + chunk * size, size)]
        copy_a = remote(block, block, index_a, index_a, row, to_a)
        copy_b = remote(block, block, index_b, index_a, row, to_b)

        def run():
            @pl.when(jnp.logical_not(root))
            def _():
                copy_a.wait_recv()

            @pl.when(send_a)
            def _():
                copy_a.start()

            @pl.when(send_b)
            def _():
                copy_b.start()

        started.append((copy_a, send_a))
        started.append((copy_b, send_b))
        return run

    def row_event(block):
        index_p, index_u, index_d = fresh(), fresh(), fresh()

        def build(part):
            return (
                remote(block, block, index_p, index_p, row + 1, col),
                remote(block, block, index_u, index_p, lax.rem(row + 2, ROWS), col),
                remote(block, block, index_d, index_p, lax.rem(row + 6, ROWS), col),
            )

        def run(part):
            partner, up, down = build(part)
            send_p = core == 0
            send_u = (core == 0) & ((chip == 0) | ((chip == 1) if part == 0 else (chip < 0)))
            send_d = (core == 0) & ((chip == 0) | ((chip == 3) if part == 1 else (chip < 0)))

            @pl.when(row != 0)
            def _():
                partner.wait_recv()

            for copy, flag in ((up, send_u), (down, send_d), (partner, send_p)):

                @pl.when(flag)
                def _(copy=copy):
                    copy.start()

                started.append((copy, flag))

        return run

    load_panel = pltpu.make_async_copy(
        front_ref.at[:, pl.ds(0, LEAD)], pan_ref, local_sem.at[1]
    )
    load_top = pltpu.make_async_copy(front_ref.at[pl.ds(0, LEAD)], top_ref, local_sem.at[2])

    @pl.when(root)
    def _():
        load_panel.start()

    @pl.when(row == 0)
    def _():
        load_top.start()

    z_ring = ring_events(0)
    y_ring = ring_events(1)
    for ring in (z_ring, y_ring):
        ring[0]()
    for ring in (z_ring, y_ring):
        ring[1]()

    @pl.when(root)
    def _():
        load_panel.wait()

    @pl.when(row == 0)
    def _():
        load_top.wait()

    tops = [row_event(top_ref.at[pl.ds(h * TILE, TILE)]) for h in range(2)]
    leads = [row_event(lead_ref.at[pl.ds(h * TILE, TILE)]) for h in range(2)]
    chunk_events = [
        [tree_event(tree, chunk) for tree in range(4)] for chunk in range(TREE_CHUNKS)
    ]

    def tree_round(chunk):
        for run in chunk_events[chunk]:
            run()

    ring_steps = []
    for d in (1, -1):
        for ring in (z_ring, y_ring):
            ring_steps.append((ring[2], d))
    for i in (0,):
        for ring in (z_ring, y_ring):
            ring_steps.append((ring[4], i))
    for ring in (z_ring, y_ring):
        ring_steps.append((ring[3],))
    for i in (1, -1, 2):
        for ring in (z_ring, y_ring):
            ring_steps.append((ring[4], i))
    for i in (0, 1, -1, 2):
        for ring in (z_ring, y_ring):
            ring_steps.append((ring[5], i))
    done_top = [False, False]

    def run_top(h):
        tops[h](h)

    for number, step in enumerate(ring_steps):
        if number == 0:
            run_top(0)
        if number == 6:
            run_top(1)
        step[0](*step[1:])
        if number >= 2 and number % 2 == 0 and (number - 2) // 2 < TREE_CHUNKS:
            tree_round((number - 2) // 2)
    for chunk in range(TREE_CHUNKS):
        if 2 + 2 * chunk >= len(ring_steps):
            tree_round(chunk)
    move_lead = pltpu.make_async_copy(pan_ref.at[pl.ds(0, LEAD)], lead_ref, local_sem.at[3])

    @pl.when(row == 0)
    def _():
        move_lead.start()
        move_lead.wait()

    for h in range(2):
        leads[h](h)
    keep_own.wait()
    for copy, flag in started:
        if flag is None:
            copy.wait_send()
        else:

            @pl.when(flag)
            def _(copy=copy):
                copy.wait_send()


def gather_all(own_factor, front):
    anywhere = pl.BlockSpec(memory_space=pl.ANY)
    vmem = pl.BlockSpec(memory_space=pltpu.VMEM)
    return pl.pallas_call(
        gather_kernel,
        out_shape=(
            jax.ShapeDtypeStruct((COLS, TILE, CW), F32),
            jax.ShapeDtypeStruct((PANEL_ROWS, LEAD), F32),
            jax.ShapeDtypeStruct((LEAD, COL_WIDTH), F32),
            jax.ShapeDtypeStruct((LEAD, LEAD), F32),
        ),
        in_specs=[vmem, anywhere],
        out_specs=(vmem, vmem, vmem, vmem),
        scratch_shapes=[
            pltpu.SemaphoreType.DMA((128,)),
            pltpu.SemaphoreType.DMA((128,)),
            pltpu.SemaphoreType.DMA((4,)),
        ],
        compiler_params=pltpu.CompilerParams(
            collective_id=0, has_side_effects=True, vmem_limit_bytes=40 * 2**20
        ),
        name="gather",
    )(own_factor, front)


def tiles_kernel(order_ref, left_ref, right_ref, out_ref):
    out_ref[0] = three_pass(halves(left_ref[0]), halves(right_ref[0]), ((1,), (1,)))


def update_tiles(order, factors):
    return pl.pallas_call(
        tiles_kernel,
        out_shape=jax.ShapeDtypeStruct((COLS, TILE, TILE), F32),
        grid_spec=pltpu.PrefetchScalarGridSpec(
            num_scalar_prefetch=1,
            grid=(COLS,),
            in_specs=[
                pl.BlockSpec((1, TILE, CW), lambda i, order: (order[i], 0, 0)),
                pl.BlockSpec((1, TILE, CW), lambda i, order: (order[COLS], 0, 0)),
            ],
            out_specs=pl.BlockSpec((1, TILE, TILE), lambda i, order: (i, 0, 0)),
        ),
        cost_estimate=pl.CostEstimate(
            flops=6 * COLS * TILE * TILE * CW, bytes_accessed=12 * 2**20, transcendentals=0
        ),
        name="tiles",
    )(order, factors, factors)


def schur_kernel(rows_ref, cols_ref, front_ref, panel_ref, top_ref, tiles_ref, out_ref):
    step = pl.program_id(0)
    out_ref[...] = front_ref[...] - three_pass(
        halves(panel_ref[...]), halves(top_ref[...]), ((1,), (0,))
    )
    block = step // PCT
    for child in range(ROWS):

        @pl.when(rows_ref[child, block] == step)
        def _(child=child):
            start = pl.multiple_of(cols_ref[child] * TILE, TILE)
            out_ref[:, pl.ds(start, TILE)] -= tiles_ref[child, 0]


def schur_update(row_places, col_places, front, panel, top, tiles):
    return pl.pallas_call(
        schur_kernel,
        out_shape=jax.ShapeDtypeStruct((PANEL_ROWS, COL_WIDTH), F32),
        grid_spec=pltpu.PrefetchScalarGridSpec(
            num_scalar_prefetch=2,
            grid=(RT,),
            in_specs=[
                pl.BlockSpec((TILE, COL_WIDTH), lambda i, *_: (i, 0)),
                pl.BlockSpec((TILE, LEAD), lambda i, *_: (i, 0)),
                pl.BlockSpec((LEAD, COL_WIDTH), lambda i, *_: (0, 0)),
                pl.BlockSpec((ROWS, 1, TILE, TILE), lambda i, *_: (0, i // PCT, 0, 0)),
            ],
            out_specs=pl.BlockSpec((TILE, COL_WIDTH), lambda i, *_: (i, 0)),
        ),
        cost_estimate=pl.CostEstimate(
            flops=6 * PANEL_ROWS * COL_WIDTH * LEAD,
            bytes_accessed=26 * 2**20,
            transcendentals=0,
        ),
        name="schur",
    )(row_places, col_places, front, panel, top, tiles)


def per_device(parent_front, child_panels, child_inverses, parent_index):
    here_row = lax.axis_index("row")
    here_col = lax.axis_index("col")
    own_factor = product_rows(child_panels[0], child_inverses[0])
    factors, panel, top, lead = gather_all(own_factor, parent_front)

    block_of = parent_index // PCT
    my_blocks = lax.dynamic_index_in_dim(block_of, here_row, 0, keepdims=False)
    ids = jnp.arange(COLS, dtype=jnp.int32)
    wanted = jnp.concatenate([ids, here_col[None].astype(jnp.int32)])
    order = jnp.sum(jnp.where(my_blocks[None, :] == wanted[:, None], ids[None, :], 0), axis=1)
    outgoing = update_tiles(order, factors).reshape(ROWS, 2, TILE, TILE)
    tiles = lax.all_to_all(outgoing, "row", split_axis=0, concat_axis=0, tiled=True)

    row_blocks = 2 * here_row + jnp.arange(2, dtype=jnp.int32)
    row_places = (
        jnp.sum(
            jnp.where(
                block_of[:, None, :] == row_blocks[None, :, None], parent_index[:, None, :], 0
            ),
            axis=2,
        )
        - here_row * RT
    )
    col_places = (
        jnp.sum(jnp.where(block_of == here_col, parent_index, 0), axis=1) - here_col * PCT
    )

    identity = jnp.eye(TILE, dtype=F32)
    pivot_0 = jnp.linalg.cholesky(lead[:TILE, :TILE])
    inverse_0 = lax.linalg.triangular_solve(pivot_0, identity, left_side=True, lower=True)
    below = product_rows(lead[TILE:, :TILE], inverse_0)
    pivot_1 = jnp.linalg.cholesky(lead[TILE:, TILE:] - product_rows(below, below))
    inverse_1 = lax.linalg.triangular_solve(pivot_1, identity, left_side=True, lower=True)

    tile_row = here_row * RT + jnp.arange(PANEL_ROWS) // TILE
    panel_0 = product_rows(panel[:, :TILE], inverse_0)
    panel_1 = product_rows(panel[:, TILE:] - product_rows(panel_0, below), inverse_1)
    first = here_row == 0
    panel_0 = panel_0.at[:TILE].set(jnp.where(first, pivot_0, panel_0[:TILE]))
    panel_1 = panel_1.at[:TILE].set(jnp.where(first, 0.0, panel_1[:TILE]))
    panel_1 = panel_1.at[TILE:LEAD].set(jnp.where(first, pivot_1, panel_1[TILE:LEAD]))
    panel_out = jnp.concatenate([panel_0, panel_1], axis=1)

    top_0 = product(inverse_0, top[:TILE])
    top_1 = product(inverse_1, top[TILE:] - product(below, top_0))
    first = here_col == 0
    top_0 = top_0.at[:, :TILE].set(jnp.where(first, pivot_0.T, top_0[:, :TILE]))
    top_1 = top_1.at[:, :TILE].set(jnp.where(first, 0.0, top_1[:, :TILE]))
    top_1 = top_1.at[:, TILE:LEAD].set(jnp.where(first, pivot_1.T, top_1[:, TILE:LEAD]))
    top_out = jnp.concatenate([top_0, top_1], axis=0)

    schur = schur_update(
        row_places.astype(jnp.int32),
        col_places.astype(jnp.int32),
        parent_front,
        panel_out,
        top_out,
        tiles,
    )
    return (panel_out, schur)


def solution(mesh):
    placed = (P("row", "col"), P("row", "col", None), P("row", None, None), P())
    return jax.shard_map(
        per_device,
        mesh=mesh,
        in_specs=placed,
        out_specs=(P("row", None), P("row", "col")),
        check_vma=False,
    )
```

time: 999 us -> 828 us (0.83)
  the two profiles are of different devices: /device:TPU:0 before, /device:TPU:35 now
where the time goes in v1:
time: 828 us; the launch traced here: 824 us
  Pallas kernels  615 us (74%)
  other arithmetic  129 us (16%)
  local copies, waits for them, and re-layouts  32.8 us (4%)
  matrix products  25 us (3%)
  starting transfers between devices  16.9 us (2%)
    pallas_call x1, Pallas kernels, gather_all(): pl.pallas_call(gather_kernel, out_shape=(jax.ShapeDtypeStruct((COLS, TILE...  584 us
    another operation x7, other arithmetic, per_device(): jnp.linalg.cholesky(lead[TILE:, TILE:] - product_rows(below, below))  34.6 us
    another operation x6, other arithmetic, per_device(): pivot_0 = jnp.linalg.cholesky(lead[:TILE, :TILE])  34 us
    another operation x3, other arithmetic, per_device(): lax.linalg.triangular_solve(pivot_0, identity, left_side=True, lower=True)  20.7 us
    another operation x2, other arithmetic, per_device(): lax.linalg.triangular_solve(pivot_1, identity, left_side=True, lower=True)  20.4 us
    all_to_all x1, starting transfers between devices, per_device(): lax.all_to_all(outgoing, 'row', split_axis=0, concat_axis=0, tiled=True)  16.9 us
    pallas_call x1, Pallas kernels, schur_update(): pl.pallas_call(schur_kernel, out_shape=jax.ShapeDtypeStruct((PANEL_ROWS,...  16.7 us
  transfers between devices with their start and end apart: 1, of which 0 were waited for; matrix products, arithmetic and copies ran while one was open for 22% of the time, Pallas kernels for 0%

profile of v1, /device:TPU:35, one launch (start us, length us, event | category | flops | bytes accessed | tf_op | source)
XLA Modules:
  0.0 823.6 jit_solution(11845607676316791184)
XLA Ops:
  0.7 1.2 copy-done
  1.9 2.1 fusion.2.own_ref
  4.0 583.9 %gather.4 = (f32[16,256,512]{2,1,0:T(8,128)}, f32[2048,512]{1,0:T(8,128)S(1)}, f32[512,1024]{1,0:T(8,128)S(1)}, f32[512,512]{1,0:T(8,128)S(1)}) custom-call(f32[256,512]{1,0:T(8,128)S(1)} %fusion.2.own_ref, f32[2048,1024]{1,0:T(8,128)} %front_ref.3), custom_call_target="tpu_custom_call" | custom-call | tf_op jit(solution)/shard_map/gather/pallas_call | solution.py:336
  587.9 2.0 copy-done.2
  591.2 14.8 %tiles.1 = f32[16,256,256]{2,1,0:T(8,128)} custom-call(s32[17]{0:T(128)} %select_reduce_fusion.4.order_ref, f32[16,256,512]{2,1,0:T(8,128)} %get-tuple-element.83.left_ref.right_ref, f32[16,256,512]{2,1,0:T(8,128)} %get-tuple-element.83.left_ref.right_ref), custom_call_target="tpu_custom_call" | custom-call | flops 3221225472 | bytes 12582912 | tf_op jit(solution)/shard_map/tiles/pallas_call | solution.py:363
  606.1 16.9 %all-to-all-start = ((f32[8,2,256,256]{3,2,1,0:T(8,128)}), f32[8,2,256,256]{3,2,1,0:T(8,128)}, u32[]{:S(2)}, u32[]{:S(2)}) async-start(f32[8,2,256,256]{3,2,1,0:T(8,128)} %bitcast.84), calls=%async_computation | async-start | bytes 8388608 | tf_op jit(solution)/shard_map/all_to_all | solution.py:432
  623.0 1.3 copy.23
  624.3 1.7 slice.220
  626.0 1.1 copy.24
  627.0 1.0 fusion.13
  628.7 11.7 %cholesky.130 = f32[128,128]{1,0:T(8,128)S(1)} custom-call(f32[128,128]{1,0:T(8,128)S(1)} %cholesky.194), custom_call_target="Cholesky" | custom-call | tf_op jit(solution)/shard_map/jit(cholesky)/cholesky | solution.py:449
  640.6 9.8 %custom-call.13 = f32[1,128,128]{1,2,0:T(8,128)S(1)} custom-call(f32[1,128,128]{2,1,0:T(8,128)S(1)} %get-tuple-element.143), custom_call_target="InvertDiagBlocksLowerTriangular" | custom-call | tf_op jit(solution)/shard_map/jit(cholesky)/cholesky | solution.py:449
  650.4 1.1 constant_dynamic-update-slice_fusion.1
  651.6 1.1 convolution_subtract_fusion.6
  652.7 11.7 %cholesky.147 = f32[128,128]{1,0:T(8,128)S(1)} custom-call(f32[128,128]{1,0:T(8,128)S(1)} %convolution_subtract_fusion.6), custom_call_target="Cholesky" | custom-call | tf_op jit(solution)/shard_map/jit(cholesky)/cholesky | solution.py:449
  668.2 5.8 while.10
  668.8 2.2 dynamic-slice.60
  671.7 2.1 dynamic-slice.60
  674.0 19.8 %custom-call.14 = f32[2,128,128]{1,2,0:T(8,128)S(1)} custom-call(f32[2,128,128]{2,1,0:T(8,128)S(1)} %get-tuple-element.98), custom_call_target="InvertDiagBlocksLowerTriangular" | custom-call | tf_op jit(solution)/shard_map/triangular_solve/custom-call.0 | solution.py:450
  693.8 1.2 fusion.24
  695.1 1.3 convolution_subtract_fusion.4
  697.3 1.4 convolution_subtract_fusion.2
  698.8 11.7 %cholesky.164 = f32[128,128]{1,0:T(8,128)S(1)} custom-call(f32[128,128]{1,0:T(8,128)S(1)} %cholesky.197), custom_call_target="Cholesky" | custom-call | tf_op jit(solution)/shard_map/jit(cholesky)/cholesky | solution.py:452
  710.7 9.8 %custom-call.15 = f32[1,128,128]{1,2,0:T(8,128)S(1)} custom-call(f32[1,128,128]{2,1,0:T(8,128)S(1)} %get-tuple-element.141), custom_call_target="InvertDiagBlocksLowerTriangular" | custom-call | tf_op jit(solution)/shard_map/jit(cholesky)/cholesky | solution.py:452
  721.1 11.7 %cholesky.181 = f32[128,128]{1,0:T(8,128)S(1)} custom-call(f32[128,128]{1,0:T(8,128)S(1)} %convolution_subtract_fusion.5), custom_call_target="Cholesky" | custom-call | tf_op jit(solution)/shard_map/jit(cholesky)/cholesky | solution.py:452
  736.3 6.2 while.11
  737.2 2.2 dynamic-slice.62
  740.2 2.2 dynamic-slice.62
  742.5 19.7 %custom-call.16 = f32[2,128,128]{1,2,0:T(8,128)S(1)} custom-call(f32[2,128,128]{2,1,0:T(8,128)S(1)} %get-tuple-element.99), custom_call_target="InvertDiagBlocksLowerTriangular" | custom-call | tf_op jit(solution)/shard_map/triangular_solve/custom-call.0 | solution.py:453
  762.5 1.2 convolution_subtract_fusion.3
  764.0 3.8 fusion
  767.8 3.6 convolution_subtract_fusion
  771.4 3.3 fusion.21
  774.7 1.7 slice.231
  776.4 1.8 copy.44
  778.2 1.7 broadcast_select_fusion
  779.9 1.8 copy.36
  781.7 1.7 constant_dynamic-update-slice_fusion.2
  783.3 1.7 fusion.11
  785.0 1.7 fusion.10
  786.7 4.7 pad_maximum_fusion
  791.5 5.3 copy.40.panel_ref
  797.8 0.9 compare_reduce_fusion.4
  798.6 1.0 fusion.4
  799.7 1.0 convolution_subtract_fusion.1
  800.7 1.0 fusion.20
  803.9 1.5 pad_maximum_fusion.1.top_ref
  806.6 16.7 %schur.1 = f32[2048,1024]{1,0:T(8,128)} custom-call(s32[8,2]{1,0:T(8,128)} %broadcast_subtract_fusion.rows_ref, s32[8]{0:T(128)} %broadcast_subtract_fusion.1.cols_ref, f32[2048,1024]{1,0:T(8,128)} %front_ref.3, f32[2048,512]{1,0:T(8,128)} %copy.40.panel_ref, f32[512,1024]{1,0:T(8,128)} %pad_maximum_fusion.1.top_ref, f32[8,2,256,256]{3,2,1,0:T(8,128)} %all-to-all-done.tiles_ref), custom_call_target="tpu_custom_call" | custom-call | flops 6442450944 | bytes 27262976 | tf_op jit(solution)/shard_map/schur/pallas_call | solution.py:397
  (87 shorter events, 16.4 us)
Async XLA Ops:
  0.6 1.2 copy-start
  4.0 585.9 %copy-start.11 = (s32[8,16]{1,0:T(8,128)S(1)}, s32[8,16]{1,0:T(8,128)}, u32[]{:S(2)}) copy-start(s32[8,16]{1,0:T(8,128)} %param.22) | copy-start | bytes 1540
  587.8 2.0 copy-start.2
  606.1 200.6 %all-to-all-start = ((f32[8,2,256,256]{3,2,1,0:T(8,128)}), f32[8,2,256,256]{3,2,1,0:T(8,128)}, u32[]{:S(2)}, u32[]{:S(2)}) async-start(f32[8,2,256,256]{3,2,1,0:T(8,128)} %bitcast.84), calls=%async_computation | async-start | bytes 8388608 | tf_op jit(solution)/shard_map/all_to_all | solution.py:432
  628.0 0.7 copy-start.10
  667.2 0.9 copy-start.5
  696.6 0.6 copy-start.8
  710.7 51.5 %copy-start.7 = (f32[256,256]{1,0:T(8,128)S(1)}, f32[256,256]{1,0:T(8,128)}, u32[]{:S(2)}) copy-start(f32[256,256]{1,0:T(8,128)} %fusion.19) | copy-start | bytes 786436
  732.9 31.1 %copy-start.9 = (f32[128,256]{1,0:T(8,128)S(1)}, f32[128,256]{1,0:T(8,128)}, u32[]{:S(2)}) copy-start(f32[128,256]{1,0:T(8,128)} %copy-done.8) | copy-start | bytes 393220
  764.0 3.8 copy-start.3
  767.7 3.6 copy-start.4
  774.7 8.6 %copy-start.6 = (f32[256,256]{0,1:T(8,128)S(1)}, f32[256,256]{0,1:T(8,128)}, u32[]{:S(2)}) copy-start(f32[256,256]{0,1:T(8,128)} %copy-done.5) | copy-start | bytes 786436
  803.9 1.5 copy-start.12
  806.6 16.7 %copy-start.1 = (f32[1,512,512]{2,1,0:T(8,128)S(1)}, f32[1,512,512]{2,1,0:T(8,128)}, u32[]{:S(2)}) copy-start(f32[1,512,512]{2,1,0:T(8,128)} %param.21) | copy-start | bytes 3145732

commit v2 on v1

v2 whole, which is shorter than its diff:
```python
import jax
import jax.numpy as jnp
from jax import lax
from jax.experimental import pallas as pl
from jax.experimental.pallas import tpu as pltpu
from jax.sharding import PartitionSpec as P

TILE = 256
CW = 512
PCT = 4
NSP = 2
ROWS = 8
COLS = 16
SIDE = 4
RT = 8
LEAD = NSP * TILE
PANEL_ROWS = RT * TILE
COL_WIDTH = PCT * TILE
SLICE = LEAD // COLS
TOP_PIECES = 8
TOP_OVERLAP = 8
MESH = pl.DeviceIdType.MESH
F32 = jnp.float32
BF16 = jnp.bfloat16


def product(matrix_a, matrix_b):
    return jnp.dot(
        matrix_a, matrix_b, precision=lax.Precision.HIGHEST, preferred_element_type=F32
    )


def product_rows(matrix_a, matrix_b):
    return lax.dot_general(
        matrix_a,
        matrix_b,
        (((1,), (1,)), ((), ())),
        precision=lax.Precision.HIGHEST,
        preferred_element_type=F32,
    )


def halves(value):
    high = value.astype(BF16)
    low = (value - high.astype(F32)).astype(BF16)
    return high, low


def three_pass(pair_a, pair_b, contract):
    def one(left, right):
        return lax.dot_general(left, right, (contract, ((), ())), preferred_element_type=F32)

    return one(pair_a[0], pair_b[0]) + (one(pair_a[0], pair_b[1]) + one(pair_a[1], pair_b[0]))


def wrap(value):
    return lax.rem(value + 2 * SIDE, SIDE)


def gather_kernel(own_ref, front_ref, all_ref, pan_ref, top_ref, send_sem, recv_sem, local_sem):
    row = lax.axis_index("row")
    col = lax.axis_index("col")
    place_y = col // SIDE
    place_z = lax.rem(col, SIDE)
    chip = row // 2
    core = lax.rem(row, 2)
    counter = [0]

    def fresh(count=1):
        counter[0] += count
        return counter[0] - count

    def at(step_y, step_z):
        return wrap(place_y + step_y) * SIDE + wrap(place_z + step_z)

    def remote(src, dst, send, recv, to_row, to_col):
        return pltpu.make_async_remote_copy(
            src_ref=src,
            dst_ref=dst,
            send_sem=send_sem.at[send],
            recv_sem=recv_sem.at[recv],
            device_id=(to_row, to_col),
            device_id_type=MESH,
        )

    load_top = pltpu.make_async_copy(front_ref.at[pl.ds(0, LEAD)], top_ref, local_sem.at[0])

    @pl.when(row == 0)
    def _():
        load_top.start()

    keep_own = pltpu.make_async_copy(own_ref, all_ref.at[col], local_sem.at[1])
    keep_own.start()

    barrier = pltpu.get_barrier_semaphore()
    greeted = [(row, lax.rem(col + k, COLS)) for k in range(1, COLS)]
    greeted += [
        (row + 1 - 2 * core, col),
        (lax.rem(row + 2, ROWS), col),
        (lax.rem(row + 6, ROWS), col),
    ]
    for who in greeted:
        pl.semaphore_signal(barrier, inc=1, device_id=who, device_id_type=MESH)
    pl.semaphore_wait(barrier, len(greeted))

    started = []

    def ring(half, piece, own):
        if half == 0:
            place = lambda i, j: at(j, i)
        else:
            place = lambda i, j: at(i, j)
        sem = {}

        def key(name):
            if name not in sem:
                sem[name] = fresh()
            return sem[name]

        pending = {}

        def go(name, i, j, part, to_i, to_j):
            source = own if (i, j) == (0, 0) else piece(place(i, j), half, part)
            copy = remote(
                source,
                piece(place(i, j), half, part),
                key(name),
                key(name),
                row,
                place(to_i, to_j),
            )
            copy.start()
            pending[name] = copy
            started.append((copy, None))

        def arrived(name):
            pending[name].wait_recv()

        def quarter(d):
            return 1 if d == 1 else 2

        def first():
            for d in (1, -1):
                go(("a", d), 0, 0, 0, d, 0)

        def second():
            for e in (1, -1):
                go(("b", 0, e), 0, 0, 0, 0, e)

        def near(d):
            arrived(("a", d))
            go(("af", d), -d, 0, quarter(d), d, 0)
            for e in (1, -1):
                go(("b", -d, e), -d, 0, 0, 0, e)

        def far():
            arrived(("af", 1))
            arrived(("af", -1))
            for e in (1, -1):
                go(("b", 2, e), 2, 0, 0, 0, e)

        def cross(i):
            for e in (1, -1):
                arrived(("b", i, e))
                go(("bf", i, e), i, -e, quarter(e), 0, e)

        def last(i):
            for e in (1, -1):
                arrived(("bf", i, e))

        return first, second, near, far, cross, last

    def ring_steps(rings):
        def each(index, *args):
            return [lambda r=r: r[index](*args) for r in rings]

        steps = each(0) + each(1) + each(2, 1) + each(2, -1) + each(4, 0) + each(3)
        for i in (1, -1, 2):
            steps += each(4, i)
        for i in (0, 1, -1, 2):
            steps += each(5, i)
        return steps

    def factor_piece(slot, half, part):
        if part == 0:
            return all_ref.at[slot, pl.ds(half * 128, 128)]
        return all_ref.at[slot, pl.ds(half * 128 + 64 * (part - 1), 64)]

    def panel_piece(slot, half, part):
        if part == 0:
            return pan_ref.at[half, pl.ds(slot * SLICE, SLICE)]
        size = SLICE // 2
        return pan_ref.at[half, pl.ds(slot * SLICE + size * (part - 1), size)]

    factor_rings = [ring(h, factor_piece, own_ref.at[pl.ds(h * 128, 128)]) for h in range(2)]
    panel_rings = [ring(h, panel_piece, panel_piece(col, h, 0)) for h in range(2)]

    top_size = LEAD // TOP_PIECES
    half_pieces = TOP_PIECES // 2
    top_recv = fresh(TOP_PIECES)
    top_next = fresh(TOP_PIECES)
    top_side = fresh(TOP_PIECES)

    def top_copies(piece, way):
        block = top_ref.at[pl.ds(piece * top_size, top_size)]
        onward = lax.rem(row + (2 if way == 1 else 6), ROWS)
        return (
            remote(block, block, top_next + piece, top_recv + piece, onward, col),
            remote(block, block, top_side + piece, top_recv + piece, row + 1 - 2 * core, col),
        )

    def top_step(number):
        for way in (1, -1):
            depth = chip if way == 1 else lax.rem(SIDE - chip, SIDE)
            count = number - depth - core
            piece = 2 * count + (0 if way == 1 else 1)

            @pl.when((count >= 0) & (count < half_pieces))
            def _(piece=piece, way=way, depth=depth):
                onward, side = top_copies(piece, way)

                @pl.when(row != 0)
                def _():
                    side.wait_recv()

                @pl.when((core == 0) & (depth < SIDE - 1))
                def _():
                    onward.start()

                @pl.when(core == 0)
                def _():
                    side.start()

    def top_drain(number):
        for way in (1, -1):
            depth = chip if way == 1 else lax.rem(SIDE - chip, SIDE)
            onward, side = top_copies(2 * number + (0 if way == 1 else 1), way)

            @pl.when((core == 0) & (depth < SIDE - 1))
            def _():
                onward.wait_send()

            @pl.when(core == 0)
            def _():
                side.wait_send()

    spread = []
    for half in range(2):
        spread.append((half, 2 * row + half, pl.ds(0, COL_WIDTH), pl.ds(0, COL_WIDTH)))
        spread.append((half, 0, pl.ds(half * TILE, TILE), pl.ds(COL_WIDTH, TILE)))
    spread_recv = [fresh() for _ in spread]
    spread_send = [fresh(COLS) for _ in spread]

    def spread_copy(index, step):
        half, _, lanes, to_lanes = spread[index]
        to_col = lax.rem(col + step, COLS)
        rows = pl.ds(to_col * SLICE, SLICE)
        return remote(
            top_ref.at[rows, lanes],
            pan_ref.at[half, rows, to_lanes],
            spread_send[index] + step,
            spread_recv[index],
            row,
            to_col,
        )

    def spread_start(index):
        half, holder, lanes, to_lanes = spread[index]
        rows = pl.ds(col * SLICE, SLICE)

        @pl.when(col == holder)
        def _():
            keep = pltpu.make_async_copy(
                top_ref.at[rows, lanes], pan_ref.at[half, rows, to_lanes], local_sem.at[2 + index]
            )
            keep.start()

            @pl.loop(1, COLS)
            def _(step):
                spread_copy(index, step).start()

            keep.wait()

    def spread_wait(index):
        @pl.when(col != spread[index][1])
        def _():
            spread_copy(index, 1).wait_recv()

    def spread_drain(index):
        @pl.when(col == spread[index][1])
        def _():
            @pl.loop(1, COLS)
            def _(step):
                spread_copy(index, step).wait_send()

    factor_steps = ring_steps(factor_rings)
    panel_steps = ring_steps(panel_rings)
    for run in factor_steps[:4]:
        run()

    @pl.when(row == 0)
    def _():
        load_top.wait()

    top_steps = half_pieces + SIDE
    for number in range(top_steps):
        top_step(number)
        if 4 + number < TOP_OVERLAP:
            factor_steps[4 + number]()
    for number in (1, 3, 0, 2):
        spread_start(number)
    for run in factor_steps[TOP_OVERLAP:]:
        run()
    for number in range(len(spread)):
        spread_wait(number)
    for run in panel_steps:
        run()
    keep_own.wait()
    for copy, _ in started:
        copy.wait_send()
    for number in range(half_pieces):
        top_drain(number)
    for number in range(len(spread)):
        spread_drain(number)


def gather_all(own_factor, front):
    anywhere = pl.BlockSpec(memory_space=pl.ANY)
    vmem = pl.BlockSpec(memory_space=pltpu.VMEM)
    return pl.pallas_call(
        gather_kernel,
        out_shape=(
            jax.ShapeDtypeStruct((COLS, TILE, CW), F32),
            jax.ShapeDtypeStruct((2, LEAD, COL_WIDTH + TILE), F32),
            jax.ShapeDtypeStruct((LEAD, COL_WIDTH), F32),
        ),
        in_specs=[vmem, anywhere],
        out_specs=(vmem, vmem, vmem),
        scratch_shapes=[
            pltpu.SemaphoreType.DMA((192,)),
            pltpu.SemaphoreType.DMA((192,)),
            pltpu.SemaphoreType.DMA((6,)),
        ],
        compiler_params=pltpu.CompilerParams(
            collective_id=0, has_side_effects=True, vmem_limit_bytes=40 * 2**20
        ),
        name="gather",
    )(own_factor, front)


BLOCK = 128
GROUP = 8
GROUPS = BLOCK // GROUP


def eliminate(block_ref, upper_ref, inverse_ref):
    lanes = lax.broadcasted_iota(jnp.int32, (GROUP, BLOCK), 1)
    sublanes = lax.broadcasted_iota(jnp.int32, (GROUP, BLOCK), 0)
    left = [block_ref[GROUP * g : GROUP * (g + 1), :] for g in range(GROUPS)]
    right = [jnp.where(lanes == sublanes + GROUP * g, 1.0, 0.0) for g in range(GROUPS)]
    for j in range(BLOCK):
        g, s = j // GROUP, j % GROUP
        pivot_row = jnp.broadcast_to(left[g][s : s + 1, :], (GROUP, BLOCK))
        right_row = jnp.broadcast_to(right[g][s : s + 1, :], (GROUP, BLOCK))
        recip = 1.0 / jnp.broadcast_to(pivot_row[:, j : j + 1], (GROUP, BLOCK))
        for i in range(g, GROUPS):
            ratio = jnp.broadcast_to(left[i][:, j : j + 1], (GROUP, BLOCK)) * recip
            if i == g:
                if s == GROUP - 1:
                    continue
                ratio = jnp.where(sublanes > s, ratio, 0.0)
            left[i] = left[i] - ratio * pivot_row
            right[i] = right[i] - ratio * right_row
    for g in range(GROUPS):
        on_diag = lanes == sublanes + GROUP * g
        scale = 1.0 / jnp.sqrt(jnp.sum(jnp.where(on_diag, left[g], 0.0), axis=1, keepdims=True))
        upper = jnp.where(lanes >= sublanes + GROUP * g, left[g] * scale, 0.0)
        upper_ref[GROUP * g : GROUP * (g + 1), :] = upper
        inverse_ref[GROUP * g : GROUP * (g + 1), :] = right[g] * scale


def panel_kernel(
    pan_ref, top_ref, panel_ref, cols_ref, block_ref, upper_ref, inv_ref, side_ref, low_ref,
    work_ref, full_ref,
):
    row = lax.axis_index("row")
    col = lax.axis_index("col")
    lead = [pan_ref.at[h, :, pl.ds(COL_WIDTH, TILE)] for h in range(2)]
    near = slice(0, BLOCK)
    away = slice(BLOCK, TILE)

    def join_inverse(tile):
        first, second, side = inv_ref[2 * tile], inv_ref[2 * tile + 1], side_ref[tile]
        full_ref[tile, near, near] = first
        full_ref[tile, near, away] = jnp.zeros((BLOCK, BLOCK), F32)
        full_ref[tile, away, near] = -product(second, product(side, first))
        full_ref[tile, away, away] = second

    def second_half(tile, below, corner):
        side = product_rows(below, inv_ref[2 * tile])
        side_ref[tile] = side
        block_ref[...] = corner - product_rows(side, side)

    def body(number, carry):
        @pl.when(number == 0)
        def _():
            block_ref[...] = lead[0][near, near]

        @pl.when(number == 1)
        def _():
            second_half(0, lead[0][away, near], lead[0][away, away])

        @pl.when(number == 2)
        def _():
            join_inverse(0)
            low = product_rows(lead[0][TILE:, :], full_ref[0])
            low_ref[...] = low
            work_ref[...] = lead[1][TILE:, :] - product_rows(low, low)
            block_ref[...] = work_ref[near, near]

        @pl.when(number == 3)
        def _():
            second_half(1, work_ref[away, near], work_ref[away, away])

        eliminate(block_ref, upper_ref.at[number], inv_ref.at[number])
        return carry

    lax.fori_loop(0, 4, body, 0)
    join_inverse(1)

    inverses = [halves(full_ref[t]) for t in range(2)]
    low = halves(low_ref[...])

    def chunk(source, lanes):
        first = three_pass(inverses[0], halves(source[:TILE, lanes]), ((1,), (0,)))
        rest = source[TILE:, lanes] - three_pass(low, halves(first), ((1,), (0,)))
        return first, three_pass(inverses[1], halves(rest), ((1,), (0,)))

    @pl.loop(0, PCT)
    def _(part):
        lanes = pl.ds(pl.multiple_of(part * TILE, TILE), TILE)
        first, second = chunk(top_ref, lanes)
        cols_ref[:TILE, lanes] = first
        cols_ref[TILE:, lanes] = second

    @pl.loop(0, RT)
    def _(part):
        lanes = pl.ds(pl.multiple_of(lax.rem(part, PCT) * TILE, TILE), TILE)
        rows = pl.ds(pl.multiple_of(part * TILE, TILE), TILE)
        first, second = chunk(pan_ref.at[part // PCT], lanes)
        panel_ref[rows, :TILE] = first.T
        panel_ref[rows, TILE:] = second.T

    blank = jnp.zeros((BLOCK, BLOCK), F32)

    @pl.when(col == 0)
    def _():
        for t in range(2):
            for r, c, value in (
                (0, 0, upper_ref[2 * t]),
                (0, 1, side_ref[t].T),
                (1, 0, blank),
                (1, 1, upper_ref[2 * t + 1]),
            ):
                r0, c0 = t * TILE + r * BLOCK, t * TILE + c * BLOCK
                cols_ref[r0 : r0 + BLOCK, c0 : c0 + BLOCK] = value
        cols_ref[TILE:, :TILE] = jnp.zeros((TILE, TILE), F32)

    @pl.when(row == 0)
    def _():
        for t in range(2):
            for r, c, value in (
                (0, 0, upper_ref[2 * t].T),
                (0, 1, blank),
                (1, 0, side_ref[t]),
                (1, 1, upper_ref[2 * t + 1].T),
            ):
                r0, c0 = t * TILE + r * BLOCK, t * TILE + c * BLOCK
                panel_ref[r0 : r0 + BLOCK, c0 : c0 + BLOCK] = value
        panel_ref[:TILE, TILE:] = jnp.zeros((TILE, TILE), F32)


def factor_panel(pan, top):
    vmem = pl.BlockSpec(memory_space=pltpu.VMEM)
    return pl.pallas_call(
        panel_kernel,
        out_shape=(
            jax.ShapeDtypeStruct((PANEL_ROWS, LEAD), F32),
            jax.ShapeDtypeStruct((LEAD, COL_WIDTH), F32),
        ),
        in_specs=[vmem, vmem],
        out_specs=(vmem, vmem),
        scratch_shapes=[
            pltpu.VMEM((BLOCK, BLOCK), F32),
            pltpu.VMEM((4, BLOCK, BLOCK), F32),
            pltpu.VMEM((4, BLOCK, BLOCK), F32),
            pltpu.VMEM((2, BLOCK, BLOCK), F32),
            pltpu.VMEM((TILE, TILE), F32),
            pltpu.VMEM((TILE, TILE), F32),
            pltpu.VMEM((2, TILE, TILE), F32),
        ],
        compiler_params=pltpu.CompilerParams(vmem_limit_bytes=40 * 2**20),
        cost_estimate=pl.CostEstimate(
            flops=60 * 10**9, bytes_accessed=14 * 2**20, transcendentals=0
        ),
        name="panel",
    )(pan, top)


def tiles_kernel(order_ref, left_ref, right_ref, out_ref):
    out_ref[0] = three_pass(halves(left_ref[0]), halves(right_ref[0]), ((1,), (1,)))


def update_tiles(order, factors):
    return pl.pallas_call(
        tiles_kernel,
        out_shape=jax.ShapeDtypeStruct((COLS, TILE, TILE), F32),
        grid_spec=pltpu.PrefetchScalarGridSpec(
            num_scalar_prefetch=1,
            grid=(COLS,),
            in_specs=[
                pl.BlockSpec((1, TILE, CW), lambda i, order: (order[i], 0, 0)),
                pl.BlockSpec((1, TILE, CW), lambda i, order: (order[COLS], 0, 0)),
            ],
            out_specs=pl.BlockSpec((1, TILE, TILE), lambda i, order: (i, 0, 0)),
        ),
        cost_estimate=pl.CostEstimate(
            flops=6 * COLS * TILE * TILE * CW, bytes_accessed=12 * 2**20, transcendentals=0
        ),
        name="tiles",
    )(order, factors, factors)


def schur_kernel(rows_ref, cols_ref, front_ref, panel_ref, top_ref, tiles_ref, out_ref):
    step = pl.program_id(0)
    out_ref[...] = front_ref[...] - three_pass(
        halves(panel_ref[...]), halves(top_ref[...]), ((1,), (0,))
    )
    block = step // PCT
    for child in range(ROWS):

        @pl.when(rows_ref[child, block] == step)
        def _(child=child):
            start = pl.multiple_of(cols_ref[child] * TILE, TILE)
            out_ref[:, pl.ds(start, TILE)] -= tiles_ref[child, 0]


def schur_update(row_places, col_places, front, panel, top, tiles):
    return pl.pallas_call(
        schur_kernel,
        out_shape=jax.ShapeDtypeStruct((PANEL_ROWS, COL_WIDTH), F32),
        grid_spec=pltpu.PrefetchScalarGridSpec(
            num_scalar_prefetch=2,
            grid=(RT,),
            in_specs=[
                pl.BlockSpec((TILE, COL_WIDTH), lambda i, *_: (i, 0)),
                pl.BlockSpec((TILE, LEAD), lambda i, *_: (i, 0)),
                pl.BlockSpec((LEAD, COL_WIDTH), lambda i, *_: (0, 0)),
                pl.BlockSpec((ROWS, 1, TILE, TILE), lambda i, *_: (0, i // PCT, 0, 0)),
            ],
            out_specs=pl.BlockSpec((TILE, COL_WIDTH), lambda i, *_: (i, 0)),
        ),
        cost_estimate=pl.CostEstimate(
            flops=6 * PANEL_ROWS * COL_WIDTH * LEAD,
            bytes_accessed=26 * 2**20,
            transcendentals=0,
        ),
        name="schur",
    )(row_places, col_places, front, panel, top, tiles)


def per_device(parent_front, child_panels, child_inverses, parent_index):
    here_row = lax.axis_index("row")
    here_col = lax.axis_index("col")
    own_factor = product_rows(child_panels[0], child_inverses[0])
    factors, panel, top = gather_all(own_factor, parent_front)

    block_of = parent_index // PCT
    my_blocks = lax.dynamic_index_in_dim(block_of, here_row, 0, keepdims=False)
    ids = jnp.arange(COLS, dtype=jnp.int32)
    wanted = jnp.concatenate([ids, here_col[None].astype(jnp.int32)])
    order = jnp.sum(jnp.where(my_blocks[None, :] == wanted[:, None], ids[None, :], 0), axis=1)
    outgoing = update_tiles(order, factors).reshape(ROWS, 2, TILE, TILE)
    tiles = lax.all_to_all(outgoing, "row", split_axis=0, concat_axis=0, tiled=True)

    row_blocks = 2 * here_row + jnp.arange(2, dtype=jnp.int32)
    row_places = (
        jnp.sum(
            jnp.where(
                block_of[:, None, :] == row_blocks[None, :, None], parent_index[:, None, :], 0
            ),
            axis=2,
        )
        - here_row * RT
    )
    col_places = (
        jnp.sum(jnp.where(block_of == here_col, parent_index, 0), axis=1) - here_col * PCT
    )

    panel_out, top_out = factor_panel(panel, top)
    schur = schur_update(
        row_places.astype(jnp.int32),
        col_places.astype(jnp.int32),
        parent_front,
        panel_out,
        top_out,
        tiles,
    )
    return (panel_out, schur)


def solution(mesh):
    placed = (P("row", "col"), P("row", "col", None), P("row", None, None), P())
    return jax.shard_map(
        per_device,
        mesh=mesh,
        in_specs=placed,
        out_specs=(P("row", None), P("row", "col")),
        check_vma=False,
    )
```

time: 828 us -> 246 us (0.30)
  the two profiles are of different devices: /device:TPU:35 before, /device:TPU:0 now
where the time goes in v2:
time: 246 us; the launch traced here: 244 us
  Pallas kernels  227 us (92%)
  local copies, waits for them, and re-layouts  6.26 us (3%)
  starting transfers between devices  4.67 us (2%)
  other arithmetic  2.99 us (1%)
    pallas_call x1, Pallas kernels, gather_all(): pl.pallas_call(gather_kernel, out_shape=(jax.ShapeDtypeStruct((COLS, TILE...  111 us
    pallas_call x1, Pallas kernels, factor_panel(): pl.pallas_call(panel_kernel, out_shape=(jax.ShapeDtypeStruct((PANEL_ROWS,...  85 us
    pallas_call x1, Pallas kernels, schur_update(): pl.pallas_call(schur_kernel, out_shape=jax.ShapeDtypeStruct((PANEL_ROWS,...  16.5 us
    pallas_call x1, Pallas kernels, update_tiles(): pl.pallas_call(tiles_kernel, out_shape=jax.ShapeDtypeStruct((COLS, TILE,...  15 us
    unnamed x10, local copies, waits for them, and re-layouts  6.17 us
  transfers between devices with their start and end apart: 1, of which 0 were waited for; matrix products, arithmetic and copies ran while one was open for 1% of the time, Pallas kernels for 35%

profile of v2, /device:TPU:0, one launch (start us, length us, event | category | flops | bytes accessed | tf_op | source)
XLA Modules:
  0.0 243.9 jit_solution(16013996496770339567)
XLA Ops:
  0.6 0.0 copy-start
  0.7 0.9 select_reduce_fusion.2
  1.6 0.1 pad_add_fusion
  1.6 0.7 select_reduce_fusion.order_ref
  2.3 0.0 copy-done
  2.3 2.1 fusion.own_ref
  4.4 110.7 %gather.1 = (f32[16,256,512]{2,1,0:T(8,128)}, f32[2,512,1280]{2,1,0:T(8,128)S(1)}, f32[512,1024]{1,0:T(8,128)S(1)}) custom-call(f32[256,512]{1,0:T(8,128)S(1)} %fusion.own_ref, f32[2048,1024]{1,0:T(8,128)} %front_ref.3), custom_call_target="tpu_custom_call" | custom-call | tf_op jit(solution)/shard_map/gather/pallas_call | solution.py:330
  115.1 0.0 copy-start.2
  115.1 2.3 copy-done.2
  117.5 15.0 %tiles.1 = f32[16,256,256]{2,1,0:T(8,128)} custom-call(s32[17]{0:T(128)} %select_reduce_fusion.order_ref, f32[16,256,512]{2,1,0:T(8,128)} %get-tuple-element.11.left_ref.right_ref, f32[16,256,512]{2,1,0:T(8,128)} %get-tuple-element.11.left_ref.right_ref), custom_call_target="tpu_custom_call" | custom-call | flops 3221225472 | bytes 12582912 | tf_op jit(solution)/shard_map/tiles/pallas_call | solution.py:515
  132.5 0.0 copy-start.4
  132.5 4.7 %all-to-all-start = ((f32[8,2,256,256]{3,2,1,0:T(8,128)}), f32[8,2,256,256]{3,2,1,0:T(8,128)}, u32[]{:S(2)}, u32[]{:S(2)}) async-start(f32[8,2,256,256]{3,2,1,0:T(8,128)} %bitcast.10), calls=%async_computation | async-start | bytes 8388608 | tf_op jit(solution)/shard_map/all_to_all | solution.py:584
  137.2 0.0 copy-done.4
  137.2 0.2 select_reduce_fusion.1
  137.4 0.1 copy.6
  137.5 0.6 broadcast_subtract_fusion.rows_ref
  138.1 0.5 broadcast_subtract_fusion.1.cols_ref
  138.6 0.0 copy-start.3
  138.6 2.5 %copy-done.3 = f32[2,512,1280]{2,1,0:T(8,128)S(1)} copy-done((f32[2,512,1280]{2,1,0:T(8,128)S(1)}, f32[2,512,1280]{2,1,0:T(8,128)}, u32[]{:S(2)}) %copy-start.3) | copy-done | bytes 5242904
  141.1 85.0 %panel.1 = (f32[2048,512]{1,0:T(8,128)}, f32[512,1024]{1,0:T(8,128)S(1)}) custom-call(f32[2,512,1280]{2,1,0:T(8,128)S(1)} %copy-done.3, f32[512,1024]{1,0:T(8,128)S(1)} %get-tuple-element.8.top_ref), custom_call_target="tpu_custom_call" | custom-call | flops 60000002048 | bytes 14680064 | tf_op jit(solution)/shard_map/panel/pallas_call | solution.py:485
  226.1 0.0 copy-start.1
  226.1 1.3 copy-done.1
  227.4 0.0 all-to-all-done.tiles_ref
  227.4 16.5 %schur.1 = f32[2048,1024]{1,0:T(8,128)} custom-call(s32[8,2]{1,0:T(8,128)} %broadcast_subtract_fusion.rows_ref, s32[8]{0:T(128)} %broadcast_subtract_fusion.1.cols_ref, f32[2048,1024]{1,0:T(8,128)} %front_ref.3, f32[2048,512]{1,0:T(8,128)} %get-tuple-element.5.panel_ref, f32[512,1024]{1,0:T(8,128)} %copy-done.1, f32[8,2,256,256]{3,2,1,0:T(8,128)} %all-to-all-done.tiles_ref), custom_call_target="tpu_custom_call" | custom-call | flops 6442450944 | bytes 27262976 | tf_op jit(solution)/shard_map/schur/pallas_call | solution.py:549
  (3 shorter events, 0.0 us)
Async XLA Ops:
  0.6 1.7 copy-start
  115.1 2.4 copy-start.2
  132.5 4.7 %copy-start.4 = (s32[8,16]{1,0:T(8,128)S(1)}, s32[8,16]{1,0:T(8,128)}, u32[]{:S(2)}) copy-start(s32[8,16]{1,0:T(8,128)} %param.7) | copy-start | bytes 1540
  132.5 94.9 %all-to-all-start = ((f32[8,2,256,256]{3,2,1,0:T(8,128)}), f32[8,2,256,256]{3,2,1,0:T(8,128)}, u32[]{:S(2)}, u32[]{:S(2)}) async-start(f32[8,2,256,256]{3,2,1,0:T(8,128)} %bitcast.10), calls=%async_computation | async-start | bytes 8388608 | tf_op jit(solution)/shard_map/all_to_all | solution.py:584
  138.6 2.5 %copy-start.3 = (f32[2,512,1280]{2,1,0:T(8,128)S(1)}, f32[2,512,1280]{2,1,0:T(8,128)}, u32[]{:S(2)}) copy-start(f32[2,512,1280]{2,1,0:T(8,128)} %copy-done.2) | copy-start | bytes 15728644
  226.1 1.3 copy-start.1

commit v3 on v2

--- a/solution.py
+++ b/solution.py
@@ -354,29 +354,53 @@
 
 
 def eliminate(block_ref, upper_ref, inverse_ref):
-    lanes = lax.broadcasted_iota(jnp.int32, (GROUP, BLOCK), 1)
-    sublanes = lax.broadcasted_iota(jnp.int32, (GROUP, BLOCK), 0)
+    shape = (GROUP, BLOCK)
+    lanes = lax.broadcasted_iota(jnp.int32, shape, 1)
+    sublanes = lax.broadcasted_iota(jnp.int32, shape, 0)
     left = [block_ref[GROUP * g : GROUP * (g + 1), :] for g in range(GROUPS)]
     right = [jnp.where(lanes == sublanes + GROUP * g, 1.0, 0.0) for g in range(GROUPS)]
-    for j in range(BLOCK):
-        g, s = j // GROUP, j % GROUP
-        pivot_row = jnp.broadcast_to(left[g][s : s + 1, :], (GROUP, BLOCK))
-        right_row = jnp.broadcast_to(right[g][s : s + 1, :], (GROUP, BLOCK))
-        recip = 1.0 / jnp.broadcast_to(pivot_row[:, j : j + 1], (GROUP, BLOCK))
-        for i in range(g, GROUPS):
-            ratio = jnp.broadcast_to(left[i][:, j : j + 1], (GROUP, BLOCK)) * recip
-            if i == g:
-                if s == GROUP - 1:
-                    continue
-                ratio = jnp.where(sublanes > s, ratio, 0.0)
-            left[i] = left[i] - ratio * pivot_row
-            right[i] = right[i] - ratio * right_row
     for g in range(GROUPS):
-        on_diag = lanes == sublanes + GROUP * g
-        scale = 1.0 / jnp.sqrt(jnp.sum(jnp.where(on_diag, left[g], 0.0), axis=1, keepdims=True))
-        upper = jnp.where(lanes >= sublanes + GROUP * g, left[g] * scale, 0.0)
-        upper_ref[GROUP * g : GROUP * (g + 1), :] = upper
-        inverse_ref[GROUP * g : GROUP * (g + 1), :] = right[g] * scale
+        base = GROUP * g
+        row_l = [jnp.broadcast_to(left[g][s : s + 1, :], shape) for s in range(GROUP)]
+        row_r = [jnp.broadcast_to(right[g][s : s + 1, :], shape) for s in range(GROUP)]
+        entry = {}
+        for s in range(GROUP):
+            for t in range(s, GROUP):
+                entry[s, t] = jnp.broadcast_to(row_l[s][:, base + t : base + t + 1], shape)
+        recip = []
+        ratio = {}
+        for s in range(GROUP):
+            recip.append(1.0 / entry[s, s])
+            for t in range(s + 1, GROUP):
+                ratio[t, s] = entry[s, t] * recip[s]
+            for t in range(s + 1, GROUP):
+                for u in range(t, GROUP):
+                    entry[t, u] = entry[t, u] - ratio[t, s] * entry[s, u]
+        for s in range(GROUP):
+            for t in range(s):
+                row_l[s] = row_l[s] - ratio[s, t] * row_l[t]
+                row_r[s] = row_r[s] - ratio[s, t] * row_r[t]
+        new_l, new_r, scale = row_l[0], row_r[0], recip[0]
+        for s in range(1, GROUP):
+            pick = sublanes == s
+            new_l = jnp.where(pick, row_l[s], new_l)
+            new_r = jnp.where(pick, row_r[s], new_r)
+            scale = jnp.where(pick, recip[s], scale)
+        for i in range(g + 1, GROUPS):
+            plain = []
+            for s in range(GROUP):
+                value = jnp.broadcast_to(left[i][:, base + s : base + s + 1], shape)
+                for t in range(s):
+                    value = value - plain[t] * ratio[s, t]
+                plain.append(value)
+            for s in range(GROUP):
+                scaled = plain[s] * recip[s]
+                left[i] = left[i] - scaled * row_l[s]
+                right[i] = right[i] - scaled * row_r[s]
+        scale = jnp.sqrt(scale)
+        upper = jnp.where(lanes >= sublanes + base, new_l * scale, 0.0)
+        upper_ref[base : base + GROUP, :] = upper
+        inverse_ref[base : base + GROUP, :] = new_r * scale
 
 
 def panel_kernel(
@@ -507,8 +531,17 @@
     )(pan, top)
 
 
-def tiles_kernel(order_ref, left_ref, right_ref, out_ref):
-    out_ref[0] = three_pass(halves(left_ref[0]), halves(right_ref[0]), ((1,), (1,)))
+PAIRS = COLS // 2
+
+
+def tiles_kernel(order_ref, first_ref, second_ref, right_ref, out_ref, high_ref, low_ref):
+    @pl.when(pl.program_id(0) == 0)
+    def _():
+        high_ref[...], low_ref[...] = halves(right_ref[0])
+
+    right = (high_ref[...], low_ref[...])
+    out_ref[0] = three_pass(halves(first_ref[0]), right, ((1,), (1,)))
+    out_ref[1] = three_pass(halves(second_ref[0]), right, ((1,), (1,)))
 
 
 def update_tiles(order, factors):
@@ -517,25 +550,36 @@
         out_shape=jax.ShapeDtypeStruct((COLS, TILE, TILE), F32),
         grid_spec=pltpu.PrefetchScalarGridSpec(
             num_scalar_prefetch=1,
-            grid=(COLS,),
+            grid=(PAIRS,),
             in_specs=[
-                pl.BlockSpec((1, TILE, CW), lambda i, order: (order[i], 0, 0)),
+                pl.BlockSpec((1, TILE, CW), lambda i, order: (order[2 * i], 0, 0)),
+                pl.BlockSpec((1, TILE, CW), lambda i, order: (order[2 * i + 1], 0, 0)),
                 pl.BlockSpec((1, TILE, CW), lambda i, order: (order[COLS], 0, 0)),
             ],
-            out_specs=pl.BlockSpec((1, TILE, TILE), lambda i, order: (i, 0, 0)),
+            out_specs=pl.BlockSpec((2, TILE, TILE), lambda i, order: (i, 0, 0)),
+            scratch_shapes=[pltpu.VMEM((TILE, CW), BF16), pltpu.VMEM((TILE, CW), BF16)],
         ),
         cost_estimate=pl.CostEstimate(
             flops=6 * COLS * TILE * TILE * CW, bytes_accessed=12 * 2**20, transcendentals=0
         ),
         name="tiles",
-    )(order, factors, factors)
-
-
-def schur_kernel(rows_ref, cols_ref, front_ref, panel_ref, top_ref, tiles_ref, out_ref):
+    )(order, factors, factors, factors)
+
+
+def schur_kernel(
+    rows_ref, cols_ref, front_ref, panel_ref, top_ref, tiles_ref, out_ref, high_ref, low_ref
+):
     step = pl.program_id(0)
-    out_ref[...] = front_ref[...] - three_pass(
-        halves(panel_ref[...]), halves(top_ref[...]), ((1,), (0,))
-    )
+
+    @pl.when(step == 0)
+    def _():
+        high_ref[...], low_ref[...] = halves(top_ref[...])
+
+    left = halves(panel_ref[...])
+    for part in range(PCT):
+        lanes = slice(part * TILE, (part + 1) * TILE)
+        right = (high_ref[:, lanes], low_ref[:, lanes])
+        out_ref[:, lanes] = front_ref[:, lanes] - three_pass(left, right, ((1,), (0,)))
     block = step // PCT
     for child in range(ROWS):
 
@@ -559,6 +603,10 @@
                 pl.BlockSpec((ROWS, 1, TILE, TILE), lambda i, *_: (0, i // PCT, 0, 0)),
             ],
             out_specs=pl.BlockSpec((TILE, COL_WIDTH), lambda i, *_: (i, 0)),
+            scratch_shapes=[
+                pltpu.VMEM((LEAD, COL_WIDTH), BF16),
+                pltpu.VMEM((LEAD, COL_WIDTH), BF16),
+            ],
         ),
         cost_estimate=pl.CostEstimate(
             flops=6 * PANEL_ROWS * COL_WIDTH * LEAD,

time: 246 us -> 200 us (0.81)
  Pallas kernels: 227 us -> 172 us
  waiting for transfers between devices: 0.01 us -> 10.6 us
    pallas_call x1, Pallas kernels: 85 us -> 33.8 us  [factor_panel(): pl.pallas_call(panel_kernel, out_shape=(jax.ShapeDtypeStruct((PANEL_ROWS,...]
    all_to_all x1, waiting for transfers between devices: 0.01 us -> 10.6 us  [per_device(): lax.all_to_all(outgoing, 'row', split_axis=0, concat_axis=0, tiled=True)]
    pallas_call x1, Pallas kernels: 15 us -> 10.8 us  [update_tiles(): pl.pallas_call(tiles_kernel, out_shape=jax.ShapeDtypeStruct((COLS, TILE,...]
  transfers between devices with their start and end apart: 1 -> 1, of which waited for: 0 -> 1; matrix products, arithmetic and copies ran while one was open for 1% -> 1% of each run, Pallas kernels for 35% -> 17%
where the time goes in v3:
time: 200 us; the launch traced here: 199 us
  Pallas kernels  172 us (86%)
  waiting for transfers between devices  10.6 us (5%)
  local copies, waits for them, and re-layouts  6.26 us (3%)
  starting transfers between devices  4.67 us (2%)
  other arithmetic  2.99 us (1%)
  matrix products  2.1 us (1%)
    pallas_call x1, Pallas kernels, gather_all(): pl.pallas_call(gather_kernel, out_shape=(jax.ShapeDtypeStruct((COLS, TILE...  111 us
    pallas_call x1, Pallas kernels, factor_panel(): pl.pallas_call(panel_kernel, out_shape=(jax.ShapeDtypeStruct((PANEL_ROWS,...  33.8 us
    pallas_call x1, Pallas kernels, schur_update(): pl.pallas_call(schur_kernel, out_shape=jax.ShapeDtypeStruct((PANEL_ROWS,...  16.9 us
    pallas_call x1, Pallas kernels, update_tiles(): pl.pallas_call(tiles_kernel, out_shape=jax.ShapeDtypeStruct((COLS, TILE,...  10.8 us
    all_to_all x1, waiting for transfers between devices, per_device(): lax.all_to_all(outgoing, 'row', split_axis=0, concat_axis=0, tiled=True)  10.6 us
    unnamed x10, local copies, waits for them, and re-layouts  6.17 us
    all_to_all x1, starting transfers between devices, per_device(): lax.all_to_all(outgoing, 'row', split_axis=0, concat_axis=0, tiled=True)  4.67 us
  transfers between devices with their start and end apart: 1, of which 1 were waited for; matrix products, arithmetic and copies ran while one was open for 1% of the time, Pallas kernels for 17%

profile of v3, /device:TPU:0, one launch (start us, length us, event | category | flops | bytes accessed | tf_op | source)
XLA Modules:
  0.0 199.5 jit_solution(15146639482257103009)
XLA Ops:
  0.6 0.0 copy-start
  0.7 0.9 select_reduce_fusion.2
  1.6 0.1 pad_add_fusion
  1.6 0.7 select_reduce_fusion.order_ref
  2.3 0.0 copy-done
  2.3 2.1 %fusion.own_ref = f32[256,512]{1,0:T(8,128)S(1)} fusion(f32[1,512,512]{2,1,0:T(8,128)S(1)} %copy-done, f32[1,256,512]{2,1,0:T(8,128)} %param.5), kind=kOutput, calls=%fused_computation | convolution fusion | flops 805306368 | bytes 2097152 | tf_op jit(solution)/shard_map/dot_general | solution.py:34
  4.4 110.7 %gather.1 = (f32[16,256,512]{2,1,0:T(8,128)}, f32[2,512,1280]{2,1,0:T(8,128)S(1)}, f32[512,1024]{1,0:T(8,128)S(1)}) custom-call(f32[256,512]{1,0:T(8,128)S(1)} %fusion.own_ref, f32[2048,1024]{1,0:T(8,128)} %front_ref.3), custom_call_target="tpu_custom_call" | custom-call | tf_op jit(solution)/shard_map/gather/pallas_call | solution.py:330
  115.1 0.0 copy-start.2
  115.1 2.3 %copy-done.2 = f32[2,512,1280]{2,1,0:T(8,128)} copy-done((f32[2,512,1280]{2,1,0:T(8,128)}, f32[2,512,1280]{2,1,0:T(8,128)S(1)}, u32[]{:S(2)}) %copy-start.2) | copy-done | bytes 5242904
  117.5 10.8 %tiles.1 = f32[16,256,256]{2,1,0:T(8,128)} custom-call(s32[17]{0:T(128)} %select_reduce_fusion.order_ref, f32[16,256,512]{2,1,0:T(8,128)} %get-tuple-element.11.first_ref.second_ref.right_ref, f32[16,256,512]{2,1,0:T(8,128)} %get-tuple-element.11.first_ref.second_ref.right_ref, f32[16,256,512]{2,1,0:T(8,128)} %get-tuple-element.11.first_ref.second_ref.right_ref), custom_call_target="tpu_custom_call" | custom-call | flops 3221225472 | bytes 12582912 | tf_op jit(solution)/shard_map/tiles/pallas_call | solution.py:548
  128.2 0.0 copy-start.4
  128.2 4.7 %all-to-all-start = ((f32[8,2,256,256]{3,2,1,0:T(8,128)}), f32[8,2,256,256]{3,2,1,0:T(8,128)}, u32[]{:S(2)}, u32[]{:S(2)}) async-start(f32[8,2,256,256]{3,2,1,0:T(8,128)} %bitcast.10), calls=%async_computation | async-start | bytes 8388608 | tf_op jit(solution)/shard_map/all_to_all | solution.py:632
  132.9 0.0 copy-done.4
  132.9 0.2 select_reduce_fusion.1
  133.1 0.1 copy.6
  133.2 0.6 broadcast_subtract_fusion.rows_ref
  133.8 0.5 broadcast_subtract_fusion.1.cols_ref
  134.4 0.0 copy-start.3
  134.4 2.5 %copy-done.3 = f32[2,512,1280]{2,1,0:T(8,128)S(1)} copy-done((f32[2,512,1280]{2,1,0:T(8,128)S(1)}, f32[2,512,1280]{2,1,0:T(8,128)}, u32[]{:S(2)}) %copy-start.3) | copy-done | bytes 5242904
  136.9 33.8 %panel.1 = (f32[2048,512]{1,0:T(8,128)}, f32[512,1024]{1,0:T(8,128)S(1)}) custom-call(f32[2,512,1280]{2,1,0:T(8,128)S(1)} %copy-done.3, f32[512,1024]{1,0:T(8,128)S(1)} %get-tuple-element.8.top_ref), custom_call_target="tpu_custom_call" | custom-call | flops 60000002048 | bytes 14680064 | tf_op jit(solution)/shard_map/panel/pallas_call | solution.py:509
  170.7 0.0 copy-start.1
  170.7 1.3 copy-done.1
  172.0 10.6 %all-to-all-done.tiles_ref = f32[8,2,256,256]{3,2,1,0:T(8,128)} async-done(((f32[8,2,256,256]{3,2,1,0:T(8,128)}), f32[8,2,256,256]{3,2,1,0:T(8,128)}, u32[]{:S(2)}, u32[]{:S(2)}) %all-to-all-start) | async-done | bytes 4194336 | tf_op jit(solution)/shard_map/all_to_all | solution.py:632
  182.6 16.9 %schur.1 = f32[2048,1024]{1,0:T(8,128)} custom-call(s32[8,2]{1,0:T(8,128)} %broadcast_subtract_fusion.rows_ref, s32[8]{0:T(128)} %broadcast_subtract_fusion.1.cols_ref, f32[2048,1024]{1,0:T(8,128)} %front_ref.3, f32[2048,512]{1,0:T(8,128)} %get-tuple-element.5.panel_ref, f32[512,1024]{1,0:T(8,128)} %copy-done.1, f32[8,2,256,256]{3,2,1,0:T(8,128)} %all-to-all-done.tiles_ref), custom_call_target="tpu_custom_call" | custom-call | flops 6442450944 | bytes 27262976 | tf_op jit(solution)/shard_map/schur/pallas_call | solution.py:593
  (3 shorter events, 0.0 us)
Async XLA Ops:
  0.6 1.7 copy-start
  115.1 2.4 %copy-start.2 = (f32[2,512,1280]{2,1,0:T(8,128)}, f32[2,512,1280]{2,1,0:T(8,128)S(1)}, u32[]{:S(2)}) copy-start(f32[2,512,1280]{2,1,0:T(8,128)S(1)} %get-tuple-element.7.pan_ref) | copy-start | bytes 15728644
  128.2 4.7 %copy-start.4 = (s32[8,16]{1,0:T(8,128)S(1)}, s32[8,16]{1,0:T(8,128)}, u32[]{:S(2)}) copy-start(s32[8,16]{1,0:T(8,128)} %param.7) | copy-start | bytes 1540
  128.2 54.3 %all-to-all-start = ((f32[8,2,256,256]{3,2,1,0:T(8,128)}), f32[8,2,256,256]{3,2,1,0:T(8,128)}, u32[]{:S(2)}, u32[]{:S(2)}) async-start(f32[8,2,256,256]{3,2,1,0:T(8,128)} %bitcast.10), calls=%async_computation | async-start | bytes 8388608 | tf_op jit(solution)/shard_map/all_to_all | solution.py:632
  134.4 2.5 %copy-start.3 = (f32[2,512,1280]{2,1,0:T(8,128)S(1)}, f32[2,512,1280]{2,1,0:T(8,128)}, u32[]{:S(2)}) copy-start(f32[2,512,1280]{2,1,0:T(8,128)} %copy-done.2) | copy-start | bytes 15728644
  170.7 1.3 copy-start.1

commit v4 on v3

--- a/solution.py
+++ b/solution.py
@@ -18,7 +18,6 @@
 COL_WIDTH = PCT * TILE
 SLICE = LEAD // COLS
 TOP_PIECES = 8
-TOP_OVERLAP = 8
 MESH = pl.DeviceIdType.MESH
 F32 = jnp.float32
 BF16 = jnp.bfloat16
@@ -57,81 +56,67 @@
     return lax.rem(value + 2 * SIDE, SIDE)
 
 
-def gather_kernel(own_ref, front_ref, all_ref, pan_ref, top_ref, send_sem, recv_sem, local_sem):
-    row = lax.axis_index("row")
-    col = lax.axis_index("col")
-    place_y = col // SIDE
-    place_z = lax.rem(col, SIDE)
-    chip = row // 2
-    core = lax.rem(row, 2)
-    counter = [0]
-
-    def fresh(count=1):
-        counter[0] += count
-        return counter[0] - count
-
-    def at(step_y, step_z):
-        return wrap(place_y + step_y) * SIDE + wrap(place_z + step_z)
-
-    def remote(src, dst, send, recv, to_row, to_col):
+class Wires:
+    def __init__(self, send_sem, recv_sem):
+        self.row = lax.axis_index("row")
+        self.col = lax.axis_index("col")
+        self.place_y = self.col // SIDE
+        self.place_z = lax.rem(self.col, SIDE)
+        self.chip = self.row // 2
+        self.core = lax.rem(self.row, 2)
+        self.send_sem = send_sem
+        self.recv_sem = recv_sem
+        self.used = 0
+        self.started = []
+
+    def fresh(self, count=1):
+        self.used += count
+        return self.used - count
+
+    def at(self, step_y, step_z):
+        return wrap(self.place_y + step_y) * SIDE + wrap(self.place_z + step_z)
+
+    def remote(self, src, dst, send, recv, to_row, to_col):
         return pltpu.make_async_remote_copy(
             src_ref=src,
             dst_ref=dst,
-            send_sem=send_sem.at[send],
-            recv_sem=recv_sem.at[recv],
+            send_sem=self.send_sem.at[send],
+            recv_sem=self.recv_sem.at[recv],
             device_id=(to_row, to_col),
             device_id_type=MESH,
         )
 
-    load_top = pltpu.make_async_copy(front_ref.at[pl.ds(0, LEAD)], top_ref, local_sem.at[0])
-
-    @pl.when(row == 0)
-    def _():
-        load_top.start()
-
-    keep_own = pltpu.make_async_copy(own_ref, all_ref.at[col], local_sem.at[1])
-    keep_own.start()
-
-    barrier = pltpu.get_barrier_semaphore()
-    greeted = [(row, lax.rem(col + k, COLS)) for k in range(1, COLS)]
-    greeted += [
-        (row + 1 - 2 * core, col),
-        (lax.rem(row + 2, ROWS), col),
-        (lax.rem(row + 6, ROWS), col),
-    ]
-    for who in greeted:
-        pl.semaphore_signal(barrier, inc=1, device_id=who, device_id_type=MESH)
-    pl.semaphore_wait(barrier, len(greeted))
-
-    started = []
-
-    def ring(half, piece, own):
+    def greet(self, devices):
+        barrier = pltpu.get_barrier_semaphore()
+        for who in devices:
+            pl.semaphore_signal(barrier, inc=1, device_id=who, device_id_type=MESH)
+        pl.semaphore_wait(barrier, len(devices))
+
+    def col_others(self):
+        return [(self.row, lax.rem(self.col + k, COLS)) for k in range(1, COLS)]
+
+    def ring(self, half, piece, own):
         if half == 0:
-            place = lambda i, j: at(j, i)
+            place = lambda i, j: self.at(j, i)
         else:
-            place = lambda i, j: at(i, j)
+            place = lambda i, j: self.at(i, j)
         sem = {}
 
         def key(name):
             if name not in sem:
-                sem[name] = fresh()
+                sem[name] = self.fresh()
             return sem[name]
 
         pending = {}
 
         def go(name, i, j, part, to_i, to_j):
             source = own if (i, j) == (0, 0) else piece(place(i, j), half, part)
-            copy = remote(
-                source,
-                piece(place(i, j), half, part),
-                key(name),
-                key(name),
-                row,
-                place(to_i, to_j),
-            )
+            target = piece(place(i, j), half, part)
+            number = key(name)
+            copy = self.remote(source, target, number, number, self.row, place(to_i, to_j))
             copy.start()
             pending[name] = copy
-            started.append((copy, None))
+            self.started.append(copy)
 
         def arrived(name):
             pending[name].wait_recv()
@@ -170,30 +155,48 @@
 
         return first, second, near, far, cross, last
 
-    def ring_steps(rings):
-        def each(index, *args):
-            return [lambda r=r: r[index](*args) for r in rings]
-
-        steps = each(0) + each(1) + each(2, 1) + each(2, -1) + each(4, 0) + each(3)
-        for i in (1, -1, 2):
-            steps += each(4, i)
-        for i in (0, 1, -1, 2):
-            steps += each(5, i)
-        return steps
+    def drain(self):
+        for copy in self.started:
+            copy.wait_send()
+
+
+def ring_steps(rings):
+    def each(index, *args):
+        return [lambda r=r: r[index](*args) for r in rings]
+
+    steps = each(0) + each(1) + each(2, 1) + each(2, -1) + each(4, 0) + each(3)
+    for i in (1, -1, 2):
+        steps += each(4, i)
+    for i in (0, 1, -1, 2):
+        steps += each(5, i)
+    return steps
+
+
+def gather_kernel(own_ref, front_ref, all_ref, top_ref, send_sem, recv_sem, local_sem):
+    wires = Wires(send_sem, recv_sem)
+    row, col, chip, core = wires.row, wires.col, wires.chip, wires.core
+    fresh, remote = wires.fresh, wires.remote
+    load_top = pltpu.make_async_copy(front_ref.at[pl.ds(0, LEAD)], top_ref, local_sem.at[0])
+
+    @pl.when(row == 0)
+    def _():
+        load_top.start()
+
+    keep_own = pltpu.make_async_copy(own_ref, all_ref.at[col], local_sem.at[1])
+    keep_own.start()
+    wires.greet(
+        [(row, wires.at(*step)) for step in ((1, 0), (-1, 0), (0, 1), (0, -1))]
+        + [
+            (row + 1 - 2 * core, col),
+            (lax.rem(row + 2, ROWS), col),
+            (lax.rem(row + 6, ROWS), col),
+        ]
+    )
 
     def factor_piece(slot, half, part):
         if part == 0:
             return all_ref.at[slot, pl.ds(half * 128, 128)]
         return all_ref.at[slot, pl.ds(half * 128 + 64 * (part - 1), 64)]
-
-    def panel_piece(slot, half, part):
-        if part == 0:
-            return pan_ref.at[half, pl.ds(slot * SLICE, SLICE)]
-        size = SLICE // 2
-        return pan_ref.at[half, pl.ds(slot * SLICE + size * (part - 1), size)]
-
-    factor_rings = [ring(h, factor_piece, own_ref.at[pl.ds(h * 128, 128)]) for h in range(2)]
-    panel_rings = [ring(h, panel_piece, panel_piece(col, h, 0)) for h in range(2)]
 
     top_size = LEAD // TOP_PIECES
     half_pieces = TOP_PIECES // 2
@@ -243,6 +246,39 @@
             @pl.when(core == 0)
             def _():
                 side.wait_send()
+
+    rings = [wires.ring(h, factor_piece, own_ref.at[pl.ds(h * 128, 128)]) for h in range(2)]
+    steps = ring_steps(rings)
+    for run in steps[:4]:
+        run()
+
+    @pl.when(row == 0)
+    def _():
+        load_top.wait()
+
+    for number in range(half_pieces + SIDE):
+        top_step(number)
+        for run in steps[4 + 2 * number : 6 + 2 * number]:
+            run()
+    for run in steps[4 + 2 * (half_pieces + SIDE) :]:
+        run()
+    keep_own.wait()
+    wires.drain()
+    for number in range(half_pieces):
+        top_drain(number)
+
+
+def spread_kernel(top_ref, pan_ref, send_sem, recv_sem, local_sem):
+    wires = Wires(send_sem, recv_sem)
+    row, col = wires.row, wires.col
+    fresh, remote = wires.fresh, wires.remote
+    wires.greet(wires.col_others())
+
+    def panel_piece(slot, half, part):
+        if part == 0:
+            return pan_ref.at[half, pl.ds(slot * SLICE, SLICE)]
+        size = SLICE // 2
+        return pan_ref.at[half, pl.ds(slot * SLICE + size * (part - 1), size)]
 
     spread = []
     for half in range(2):
@@ -271,7 +307,7 @@
         @pl.when(col == holder)
         def _():
             keep = pltpu.make_async_copy(
-                top_ref.at[rows, lanes], pan_ref.at[half, rows, to_lanes], local_sem.at[2 + index]
+                top_ref.at[rows, lanes], pan_ref.at[half, rows, to_lanes], local_sem.at[index]
             )
             keep.start()
 
@@ -293,33 +329,13 @@
             def _(step):
                 spread_copy(index, step).wait_send()
 
-    factor_steps = ring_steps(factor_rings)
-    panel_steps = ring_steps(panel_rings)
-    for run in factor_steps[:4]:
-        run()
-
-    @pl.when(row == 0)
-    def _():
-        load_top.wait()
-
-    top_steps = half_pieces + SIDE
-    for number in range(top_steps):
-        top_step(number)
-        if 4 + number < TOP_OVERLAP:
-            factor_steps[4 + number]()
     for number in (1, 3, 0, 2):
         spread_start(number)
-    for run in factor_steps[TOP_OVERLAP:]:
-        run()
     for number in range(len(spread)):
         spread_wait(number)
-    for run in panel_steps:
+    for run in ring_steps([wires.ring(h, panel_piece, panel_piece(col, h, 0)) for h in range(2)]):
         run()
-    keep_own.wait()
-    for copy, _ in started:
-        copy.wait_send()
-    for number in range(half_pieces):
-        top_drain(number)
+    wires.drain()
     for number in range(len(spread)):
         spread_drain(number)
 
@@ -331,21 +347,42 @@
         gather_kernel,
         out_shape=(
             jax.ShapeDtypeStruct((COLS, TILE, CW), F32),
-            jax.ShapeDtypeStruct((2, LEAD, COL_WIDTH + TILE), F32),
             jax.ShapeDtypeStruct((LEAD, COL_WIDTH), F32),
         ),
         in_specs=[vmem, anywhere],
-        out_specs=(vmem, vmem, vmem),
+        out_specs=(vmem, vmem),
         scratch_shapes=[
-            pltpu.SemaphoreType.DMA((192,)),
-            pltpu.SemaphoreType.DMA((192,)),
-            pltpu.SemaphoreType.DMA((6,)),
+            pltpu.SemaphoreType.DMA((104,)),
+            pltpu.SemaphoreType.DMA((104,)),
+            pltpu.SemaphoreType.DMA((2,)),
         ],
         compiler_params=pltpu.CompilerParams(
-            collective_id=0, has_side_effects=True, vmem_limit_bytes=40 * 2**20
+            collective_id=0, has_side_effects=True, vmem_limit_bytes=52 * 2**20
         ),
         name="gather",
     )(own_factor, front)
+
+
+def spread_panel(top):
+    vmem = pl.BlockSpec(memory_space=pltpu.VMEM)
+    return pl.pallas_call(
+        spread_kernel,
+        out_shape=jax.ShapeDtypeStruct((2, LEAD, COL_WIDTH + TILE), F32),
+        in_specs=[vmem],
+        out_specs=vmem,
+        scratch_shapes=[
+            pltpu.SemaphoreType.DMA((112,)),
+            pltpu.SemaphoreType.DMA((112,)),
+            pltpu.SemaphoreType.DMA((4,)),
+        ],
+        compiler_params=pltpu.CompilerParams(
+            collective_id=1, has_side_effects=True, vmem_limit_bytes=16 * 2**20
+        ),
+        cost_estimate=pl.CostEstimate(
+            flops=30 * 10**9, bytes_accessed=20 * 2**20, transcendentals=0
+        ),
+        name="spread",
+    )(top)
 
 
 BLOCK = 128
@@ -534,14 +571,17 @@
 PAIRS = COLS // 2
 
 
-def tiles_kernel(order_ref, first_ref, second_ref, right_ref, out_ref, high_ref, low_ref):
-    @pl.when(pl.program_id(0) == 0)
+def tiles_kernel(order_ref, all_ref, out_ref, high_ref, low_ref):
+    step = pl.program_id(0)
+
+    @pl.when(step == 0)
     def _():
-        high_ref[...], low_ref[...] = halves(right_ref[0])
+        high_ref[...], low_ref[...] = halves(all_ref[order_ref[COLS]])
 
     right = (high_ref[...], low_ref[...])
-    out_ref[0] = three_pass(halves(first_ref[0]), right, ((1,), (1,)))
-    out_ref[1] = three_pass(halves(second_ref[0]), right, ((1,), (1,)))
+    for part in range(2):
+        left = halves(all_ref[order_ref[2 * step + part]])
+        out_ref[part] = three_pass(left, right, ((1,), (1,)))
 
 
 def update_tiles(order, factors):
@@ -551,11 +591,7 @@
         grid_spec=pltpu.PrefetchScalarGridSpec(
             num_scalar_prefetch=1,
             grid=(PAIRS,),
-            in_specs=[
-                pl.BlockSpec((1, TILE, CW), lambda i, order: (order[2 * i], 0, 0)),
-                pl.BlockSpec((1, TILE, CW), lambda i, order: (order[2 * i + 1], 0, 0)),
-                pl.BlockSpec((1, TILE, CW), lambda i, order: (order[COLS], 0, 0)),
-            ],
+            in_specs=[pl.BlockSpec(memory_space=pltpu.VMEM)],
             out_specs=pl.BlockSpec((2, TILE, TILE), lambda i, order: (i, 0, 0)),
             scratch_shapes=[pltpu.VMEM((TILE, CW), BF16), pltpu.VMEM((TILE, CW), BF16)],
         ),
@@ -563,7 +599,7 @@
             flops=6 * COLS * TILE * TILE * CW, bytes_accessed=12 * 2**20, transcendentals=0
         ),
         name="tiles",
-    )(order, factors, factors, factors)
+    )(order, factors)
 
 
 def schur_kernel(
@@ -599,7 +635,7 @@
             in_specs=[
                 pl.BlockSpec((TILE, COL_WIDTH), lambda i, *_: (i, 0)),
                 pl.BlockSpec((TILE, LEAD), lambda i, *_: (i, 0)),
-                pl.BlockSpec((LEAD, COL_WIDTH), lambda i, *_: (0, 0)),
+                pl.BlockSpec(memory_space=pltpu.VMEM),
                 pl.BlockSpec((ROWS, 1, TILE, TILE), lambda i, *_: (0, i // PCT, 0, 0)),
             ],
             out_specs=pl.BlockSpec((TILE, COL_WIDTH), lambda i, *_: (i, 0)),
@@ -621,7 +657,7 @@
     here_row = lax.axis_index("row")
     here_col = lax.axis_index("col")
     own_factor = product_rows(child_panels[0], child_inverses[0])
-    factors, panel, top = gather_all(own_factor, parent_front)
+    factors, top = gather_all(own_factor, parent_front)
 
     block_of = parent_index // PCT
     my_blocks = lax.dynamic_index_in_dim(block_of, here_row, 0, keepdims=False)
@@ -629,6 +665,7 @@
     wanted = jnp.concatenate([ids, here_col[None].astype(jnp.int32)])
     order = jnp.sum(jnp.where(my_blocks[None, :] == wanted[:, None], ids[None, :], 0), axis=1)
     outgoing = update_tiles(order, factors).reshape(ROWS, 2, TILE, TILE)
+    outgoing, top = lax.optimization_barrier((outgoing, top))
     tiles = lax.all_to_all(outgoing, "row", split_axis=0, concat_axis=0, tiled=True)
 
     row_blocks = 2 * here_row + jnp.arange(2, dtype=jnp.int32)
@@ -645,7 +682,7 @@
         jnp.sum(jnp.where(block_of == here_col, parent_index, 0), axis=1) - here_col * PCT
     )
 
-    panel_out, top_out = factor_panel(panel, top)
+    panel_out, top_out = factor_panel(spread_panel(top), top)
     schur = schur_update(
         row_places.astype(jnp.int32),
         col_places.astype(jnp.int32),

time: 200 us -> 192 us (0.960)
  waiting for transfers between devices: 10.6 us -> 0.01 us
  Pallas kernels: 172 us -> 180 us
  local copies, waits for them, and re-layouts: 6.26 us -> 1.43 us
    pallas_call x0 -> x1, Pallas kernels: none -> 62.7 us  [spread_panel(): pl.pallas_call(spread_kernel, out_shape=jax.ShapeDtypeStruct((2, LEAD, CO...]
    pallas_call x1, Pallas kernels: 111 us -> 55.8 us  [gather_all(): pl.pallas_call(gather_kernel, out_shape=(jax.ShapeDtypeStruct((COLS, TILE...]
    all_to_all x1, waiting for transfers between devices: 10.6 us -> 0.01 us  [per_device(): lax.all_to_all(outgoing, 'row', split_axis=0, concat_axis=0, tiled=True)]
    unnamed x10 -> x8, local copies, waits for them, and re-layouts: 6.17 us -> 1.34 us
  transfers between devices with their start and end apart: 1 -> 1, of which waited for: 1 -> 0; matrix products, arithmetic and copies ran while one was open for 1% -> 1% of each run, Pallas kernels for 17% -> 50%
where the time goes in v4:
time: 192 us; the launch traced here: 191 us
  Pallas kernels  180 us (94%)
  starting transfers between devices  4.67 us (2%)
  other arithmetic  2.93 us (2%)
  matrix products  2.1 us (1%)
    pallas_call x1, Pallas kernels, spread_panel(): pl.pallas_call(spread_kernel, out_shape=jax.ShapeDtypeStruct((2, LEAD, CO...  62.7 us
    pallas_call x1, Pallas kernels, gather_all(): pl.pallas_call(gather_kernel, out_shape=(jax.ShapeDtypeStruct((COLS, TILE...  55.8 us
    pallas_call x1, Pallas kernels, factor_panel(): pl.pallas_call(panel_kernel, out_shape=(jax.ShapeDtypeStruct((PANEL_ROWS,...  33.8 us
    pallas_call x1, Pallas kernels, schur_update(): pl.pallas_call(schur_kernel, out_shape=jax.ShapeDtypeStruct((PANEL_ROWS,...  16.9 us
    pallas_call x1, Pallas kernels, update_tiles(): pl.pallas_call(tiles_kernel, out_shape=jax.ShapeDtypeStruct((COLS, TILE,...  10.4 us
    all_to_all x1, starting transfers between devices, per_device(): lax.all_to_all(outgoing, 'row', split_axis=0, concat_axis=0, tiled=True)  4.67 us
  transfers between devices with their start and end apart: 1, of which 0 were waited for; matrix products, arithmetic and copies ran while one was open for 1% of the time, Pallas kernels for 50%

profile of v4, /device:TPU:0, one launch (start us, length us, event | category | flops | bytes accessed | tf_op | source)
XLA Modules:
  0.0 191.4 jit_solution(5488268361927292566)
XLA Ops:
  0.6 0.0 copy-start
  0.7 0.9 select_reduce_fusion.2
  1.5 0.1 pad_add_fusion
  1.6 0.6 select_reduce_fusion.1.order_ref
  2.2 0.0 copy-done
  2.2 2.1 %fusion.own_ref = f32[256,512]{1,0:T(8,128)S(1)} fusion(f32[1,512,512]{2,1,0:T(8,128)S(1)} %copy-done, f32[1,256,512]{2,1,0:T(8,128)} %param.5), kind=kOutput, calls=%fused_computation | convolution fusion | flops 805306368 | bytes 2097152 | tf_op jit(solution)/shard_map/dot_general | solution.py:33
  4.3 55.8 %gather.1 = (f32[16,256,512]{2,1,0:T(8,128)}, f32[512,1024]{1,0:T(8,128)}) custom-call(f32[256,512]{1,0:T(8,128)S(1)} %fusion.own_ref, f32[2048,1024]{1,0:T(8,128)} %front_ref.3), custom_call_target="tpu_custom_call" | custom-call | tf_op jit(solution)/shard_map/gather/pallas_call | solution.py:346
  60.1 10.4 %tiles.1 = f32[16,256,256]{2,1,0:T(8,128)} custom-call(s32[17]{0:T(128)} %select_reduce_fusion.1.order_ref, f32[16,256,512]{2,1,0:T(8,128)} %get-tuple-element.8.all_ref), custom_call_target="tpu_custom_call" | custom-call | flops 3221225472 | bytes 12582912 | tf_op jit(solution)/shard_map/tiles/pallas_call | solution.py:588
  70.5 0.0 copy-start.3
  70.5 0.0 copy-start.2
  70.5 4.7 %all-to-all-start = ((f32[8,2,256,256]{3,2,1,0:T(8,128)}), f32[8,2,256,256]{3,2,1,0:T(8,128)}, u32[]{:S(2)}, u32[]{:S(2)}) async-start(f32[8,2,256,256]{3,2,1,0:T(8,128)} %bitcast.10), calls=%async_computation | async-start | bytes 8388608 | tf_op jit(solution)/shard_map/all_to_all | solution.py:669
  75.2 0.0 copy-done.3
  75.3 0.2 select_reduce_fusion
  75.5 0.1 copy.6
  75.5 0.0 copy-done.2
  75.5 62.7 %spread.1.pan_ref = f32[2,512,1280]{2,1,0:T(8,128)S(1)} custom-call(f32[512,1024]{1,0:T(8,128)S(1)} %copy-done.2), custom_call_target="tpu_custom_call" | custom-call | flops 30000001024 | bytes 20971520 | tf_op jit(solution)/shard_map/spread/pallas_call | solution.py:368
  138.2 0.6 broadcast_subtract_fusion.1.cols_ref
  138.8 0.6 broadcast_subtract_fusion.rows_ref
  139.4 33.8 %panel.1 = (f32[2048,512]{1,0:T(8,128)}, f32[512,1024]{1,0:T(8,128)S(1)}) custom-call(f32[2,512,1280]{2,1,0:T(8,128)S(1)} %spread.1.pan_ref, f32[512,1024]{1,0:T(8,128)S(1)} %copy-done.2), custom_call_target="tpu_custom_call" | custom-call | flops 60000002048 | bytes 14680064 | tf_op jit(solution)/shard_map/panel/pallas_call | solution.py:546
  173.2 0.0 copy-start.1
  173.2 1.3 copy-done.1
  174.5 0.0 all-to-all-done.tiles_ref
  174.5 16.9 %schur.1 = f32[2048,1024]{1,0:T(8,128)} custom-call(s32[8,2]{1,0:T(8,128)} %broadcast_subtract_fusion.rows_ref, s32[8]{0:T(128)} %broadcast_subtract_fusion.1.cols_ref, f32[2048,1024]{1,0:T(8,128)} %front_ref.3, f32[2048,512]{1,0:T(8,128)} %get-tuple-element.6.panel_ref, f32[512,1024]{1,0:T(8,128)} %copy-done.1, f32[8,2,256,256]{3,2,1,0:T(8,128)} %all-to-all-done.tiles_ref), custom_call_target="tpu_custom_call" | custom-call | flops 6442450944 | bytes 27262976 | tf_op jit(solution)/shard_map/schur/pallas_call | solution.py:629
  (3 shorter events, 0.0 us)
Async XLA Ops:
  0.6 1.6 copy-start
  70.5 4.7 %copy-start.3 = (s32[8,16]{1,0:T(8,128)S(1)}, s32[8,16]{1,0:T(8,128)}, u32[]{:S(2)}) copy-start(s32[8,16]{1,0:T(8,128)} %param.7) | copy-start | bytes 1540
  70.5 5.0 %copy-start.2 = (f32[512,1024]{1,0:T(8,128)S(1)}, f32[512,1024]{1,0:T(8,128)}, u32[]{:S(2)}) copy-start(f32[512,1024]{1,0:T(8,128)} %get-tuple-element.10.top_ref) | copy-start | bytes 6291460
  70.5 104.0 %all-to-all-start = ((f32[8,2,256,256]{3,2,1,0:T(8,128)}), f32[8,2,256,256]{3,2,1,0:T(8,128)}, u32[]{:S(2)}, u32[]{:S(2)}) async-start(f32[8,2,256,256]{3,2,1,0:T(8,128)} %bitcast.10), calls=%async_computation | async-start | bytes 8388608 | tf_op jit(solution)/shard_map/all_to_all | solution.py:669
  173.2 1.3 copy-start.1

commit v5 on v4

--- a/solution.py
+++ b/solution.py
@@ -110,16 +110,20 @@
         pending = {}
 
         def go(name, i, j, part, to_i, to_j):
-            source = own if (i, j) == (0, 0) else piece(place(i, j), half, part)
-            target = piece(place(i, j), half, part)
             number = key(name)
-            copy = self.remote(source, target, number, number, self.row, place(to_i, to_j))
-            copy.start()
-            pending[name] = copy
-            self.started.append(copy)
+
+            def build():
+                mine = (i, j) == (0, 0)
+                source = own() if mine else piece(place(i, j), half, part)
+                target = piece(place(i, j), half, part)
+                return self.remote(source, target, number, number, self.row, place(to_i, to_j))
+
+            build().start()
+            pending[name] = build
+            self.started.append(build)
 
         def arrived(name):
-            pending[name].wait_recv()
+            pending[name]().wait_recv()
 
         def quarter(d):
             return 1 if d == 1 else 2
@@ -156,8 +160,8 @@
         return first, second, near, far, cross, last
 
     def drain(self):
-        for copy in self.started:
-            copy.wait_send()
+        for build in self.started:
+            build().wait_send()
 
 
 def ring_steps(rings):
@@ -172,7 +176,9 @@
     return steps
 
 
-def gather_kernel(own_ref, front_ref, all_ref, top_ref, send_sem, recv_sem, local_sem):
+def gather_kernel(
+    own_ref, front_ref, all_ref, top_ref, lead_ref, send_sem, recv_sem, local_sem
+):
     wires = Wires(send_sem, recv_sem)
     row, col, chip, core = wires.row, wires.col, wires.chip, wires.core
     fresh, remote = wires.fresh, wires.remote
@@ -185,7 +191,7 @@
     keep_own = pltpu.make_async_copy(own_ref, all_ref.at[col], local_sem.at[1])
     keep_own.start()
     wires.greet(
-        [(row, wires.at(*step)) for step in ((1, 0), (-1, 0), (0, 1), (0, -1))]
+        wires.col_others()
         + [
             (row + 1 - 2 * core, col),
             (lax.rem(row + 2, ROWS), col),
@@ -247,8 +253,57 @@
             def _():
                 side.wait_send()
 
-    rings = [wires.ring(h, factor_piece, own_ref.at[pl.ds(h * 128, 128)]) for h in range(2)]
+    lead_recv = fresh()
+    lead_send = fresh(COLS)
+
+    def lead_copy(step):
+        to_col = lax.rem(col + step, COLS)
+        rows = pl.ds(to_col * SLICE, SLICE)
+        return remote(
+            top_ref.at[rows, pl.ds(0, LEAD)],
+            lead_ref.at[rows],
+            lead_send + step,
+            lead_recv,
+            row,
+            to_col,
+        )
+
+    def lead_piece(slot, half, part):
+        size = SLICE // 2
+        if part == 0:
+            return lead_ref.at[pl.ds(slot * SLICE + half * size, size)]
+        base = slot * SLICE + half * size + (size // 2) * (part - 1)
+        return lead_ref.at[pl.ds(base, size // 2)]
+
+    def lead_start():
+        @pl.when(col == 0)
+        def _():
+            keep = pltpu.make_async_copy(
+                top_ref.at[pl.ds(0, SLICE), pl.ds(0, LEAD)],
+                lead_ref.at[pl.ds(0, SLICE)],
+                local_sem.at[2],
+            )
+            keep.start()
+
+            @pl.loop(1, COLS)
+            def _(step):
+                lead_copy(step).start()
+
+            keep.wait()
+
+    def lead_wait():
+        @pl.when(col != 0)
+        def _():
+            lead_copy(1).wait_recv()
+
+    rings = [
+        wires.ring(h, factor_piece, lambda h=h: own_ref.at[pl.ds(h * 128, 128)]) for h in range(2)
+    ]
+    lead_rings = [
+        wires.ring(h, lead_piece, lambda h=h: lead_piece(col, h, 0)) for h in range(2)
+    ]
     steps = ring_steps(rings)
+    lead_steps = ring_steps(lead_rings)
     for run in steps[:4]:
         run()
 
@@ -256,19 +311,42 @@
     def _():
         load_top.wait()
 
-    for number in range(half_pieces + SIDE):
+    top_steps = half_pieces + SIDE
+    for number in range(top_steps):
         top_step(number)
-        for run in steps[4 + 2 * number : 6 + 2 * number]:
+        for run in steps[4 + number : 5 + number]:
             run()
-    for run in steps[4 + 2 * (half_pieces + SIDE) :]:
-        run()
+    lead_start()
+    rest = steps[4 + top_steps :]
+    rest[0]()
+    rest[1]()
+    lead_wait()
+    for number in range(max(len(rest) - 2, len(lead_steps) // 2 + 1)):
+        for run in lead_steps[2 * number : 2 * number + 2] + rest[number + 2 : number + 3]:
+            run()
     keep_own.wait()
     wires.drain()
     for number in range(half_pieces):
         top_drain(number)
 
-
-def spread_kernel(top_ref, pan_ref, send_sem, recv_sem, local_sem):
+    @pl.when(col == 0)
+    def _():
+        @pl.loop(1, COLS)
+        def _(step):
+            lead_copy(step).wait_send()
+
+
+BLOCK = 128
+GROUP = 8
+GROUPS = BLOCK // GROUP
+NEAR = slice(0, BLOCK)
+AWAY = slice(BLOCK, TILE)
+
+
+def spread_kernel(
+    top_ref, lead_ref, pan_ref, upper_ref, side_ref, full_ref, low_ref,
+    block_ref, inv_ref, work_ref, send_sem, recv_sem, local_sem,
+):
     wires = Wires(send_sem, recv_sem)
     row, col = wires.row, wires.col
     fresh, remote = wires.fresh, wires.remote
@@ -283,7 +361,6 @@
     spread = []
     for half in range(2):
         spread.append((half, 2 * row + half, pl.ds(0, COL_WIDTH), pl.ds(0, COL_WIDTH)))
-        spread.append((half, 0, pl.ds(half * TILE, TILE), pl.ds(COL_WIDTH, TILE)))
     spread_recv = [fresh() for _ in spread]
     spread_send = [fresh(COLS) for _ in spread]
 
@@ -329,14 +406,64 @@
             def _(step):
                 spread_copy(index, step).wait_send()
 
-    for number in (1, 3, 0, 2):
+    for number in range(2):
         spread_start(number)
-    for number in range(len(spread)):
-        spread_wait(number)
-    for run in ring_steps([wires.ring(h, panel_piece, panel_piece(col, h, 0)) for h in range(2)]):
+    steps = ring_steps(
+        [wires.ring(h, panel_piece, lambda h=h: panel_piece(col, h, 0)) for h in range(2)]
+    )
+
+    def join_inverse(tile):
+        first, second, side = inv_ref[2 * tile], inv_ref[2 * tile + 1], side_ref[tile]
+        full_ref[tile, NEAR, NEAR] = first
+        full_ref[tile, NEAR, AWAY] = jnp.zeros((BLOCK, BLOCK), F32)
+        full_ref[tile, AWAY, NEAR] = -product(second, product(side, first))
+        full_ref[tile, AWAY, AWAY] = second
+
+    def second_half(tile, below, corner):
+        side = product_rows(below, inv_ref[2 * tile])
+        side_ref[tile] = side
+        block_ref[...] = corner - product_rows(side, side)
+
+    def body(number, carry):
+        @pl.when(number == 0)
+        def _():
+            block_ref[...] = lead_ref[NEAR, NEAR]
+
+        @pl.when(number == 1)
+        def _():
+            for index in range(2):
+                spread_wait(index)
+            for run in steps[:4]:
+                run()
+            second_half(0, lead_ref[AWAY, NEAR], lead_ref[AWAY, AWAY])
+
+        @pl.when(number == 2)
+        def _():
+            for run in steps[4:8]:
+                run()
+            join_inverse(0)
+            low = product_rows(lead_ref[TILE:, :TILE], full_ref[0])
+            low_ref[...] = low
+            work_ref[...] = lead_ref[TILE:, TILE:] - product_rows(low, low)
+            block_ref[...] = work_ref[NEAR, NEAR]
+
+        @pl.when(number == 3)
+        def _():
+            for run in steps[8:12]:
+                run()
+            second_half(1, work_ref[AWAY, NEAR], work_ref[AWAY, AWAY])
+
+        eliminate(block_ref, upper_ref.at[number], inv_ref.at[number])
+        return carry
+
+    lax.fori_loop(0, 4, body, 0)
+    for run in steps[12:16]:
+        run()
+    join_inverse(1)
+    for run in steps[16:]:
         run()
     wires.drain()
-    for number in range(len(spread)):
+    for number in range(2):
         spread_drain(number)
 
 
@@ -348,46 +475,51 @@
         out_shape=(
             jax.ShapeDtypeStruct((COLS, TILE, CW), F32),
             jax.ShapeDtypeStruct((LEAD, COL_WIDTH), F32),
+            jax.ShapeDtypeStruct((LEAD, LEAD), F32),
         ),
         in_specs=[vmem, anywhere],
-        out_specs=(vmem, vmem),
+        out_specs=(vmem, vmem, vmem),
         scratch_shapes=[
-            pltpu.SemaphoreType.DMA((104,)),
-            pltpu.SemaphoreType.DMA((104,)),
+            pltpu.SemaphoreType.DMA((128,)),
+            pltpu.SemaphoreType.DMA((128,)),
+            pltpu.SemaphoreType.DMA((3,)),
+        ],
+        compiler_params=pltpu.CompilerParams(
+            collective_id=0, has_side_effects=True, vmem_limit_bytes=52 * 2**20
+        ),
+        name="gather",
+    )(own_factor, front)
+
+
+def spread_panel(top, lead):
+    vmem = pl.BlockSpec(memory_space=pltpu.VMEM)
+    return pl.pallas_call(
+        spread_kernel,
+        out_shape=(
+            jax.ShapeDtypeStruct((2, LEAD, COL_WIDTH), F32),
+            jax.ShapeDtypeStruct((4, BLOCK, BLOCK), F32),
+            jax.ShapeDtypeStruct((2, BLOCK, BLOCK), F32),
+            jax.ShapeDtypeStruct((2, TILE, TILE), F32),
+            jax.ShapeDtypeStruct((TILE, TILE), F32),
+        ),
+        in_specs=[vmem, vmem],
+        out_specs=(vmem,) * 5,
+        scratch_shapes=[
+            pltpu.VMEM((BLOCK, BLOCK), F32),
+            pltpu.VMEM((4, BLOCK, BLOCK), F32),
+            pltpu.VMEM((TILE, TILE), F32),
+            pltpu.SemaphoreType.DMA((80,)),
+            pltpu.SemaphoreType.DMA((80,)),
             pltpu.SemaphoreType.DMA((2,)),
         ],
         compiler_params=pltpu.CompilerParams(
-            collective_id=0, has_side_effects=True, vmem_limit_bytes=52 * 2**20
-        ),
-        name="gather",
-    )(own_factor, front)
-
-
-def spread_panel(top):
-    vmem = pl.BlockSpec(memory_space=pltpu.VMEM)
-    return pl.pallas_call(
-        spread_kernel,
-        out_shape=jax.ShapeDtypeStruct((2, LEAD, COL_WIDTH + TILE), F32),
-        in_specs=[vmem],
-        out_specs=vmem,
-        scratch_shapes=[
-            pltpu.SemaphoreType.DMA((112,)),
-            pltpu.SemaphoreType.DMA((112,)),
-            pltpu.SemaphoreType.DMA((4,)),
-        ],
-        compiler_params=pltpu.CompilerParams(
-            collective_id=1, has_side_effects=True, vmem_limit_bytes=16 * 2**20
+            collective_id=1, has_side_effects=True, vmem_limit_bytes=24 * 2**20
         ),
         cost_estimate=pl.CostEstimate(
             flops=30 * 10**9, bytes_accessed=20 * 2**20, transcendentals=0
         ),
         name="spread",
-    )(top)
-
-
-BLOCK = 128
-GROUP = 8
-GROUPS = BLOCK // GROUP
+    )(top, lead)
 
 
 def eliminate(block_ref, upper_ref, inverse_ref):
@@ -441,54 +573,10 @@
 
 
 def panel_kernel(
-    pan_ref, top_ref, panel_ref, cols_ref, block_ref, upper_ref, inv_ref, side_ref, low_ref,
-    work_ref, full_ref,
+    pan_ref, top_ref, upper_ref, side_ref, full_ref, low_ref, panel_ref, cols_ref
 ):
     row = lax.axis_index("row")
     col = lax.axis_index("col")
-    lead = [pan_ref.at[h, :, pl.ds(COL_WIDTH, TILE)] for h in range(2)]
-    near = slice(0, BLOCK)
-    away = slice(BLOCK, TILE)
-
-    def join_inverse(tile):
-        first, second, side = inv_ref[2 * tile], inv_ref[2 * tile + 1], side_ref[tile]
-        full_ref[tile, near, near] = first
-        full_ref[tile, near, away] = jnp.zeros((BLOCK, BLOCK), F32)
-        full_ref[tile, away, near] = -product(second, product(side, first))
-        full_ref[tile, away, away] = second
-
-    def second_half(tile, below, corner):
-        side = product_rows(below, inv_ref[2 * tile])
-        side_ref[tile] = side
-        block_ref[...] = corner - product_rows(side, side)
-
-    def body(number, carry):
-        @pl.when(number == 0)
-        def _():
-            block_ref[...] = lead[0][near, near]
-
-        @pl.when(number == 1)
-        def _():
-            second_half(0, lead[0][away, near], lead[0][away, away])
-
-        @pl.when(number == 2)
-        def _():
-            join_inverse(0)
-            low = product_rows(lead[0][TILE:, :], full_ref[0])
-            low_ref[...] = low
-            work_ref[...] = lead[1][TILE:, :] - product_rows(low, low)
-            block_ref[...] = work_ref[near, near]
-
-        @pl.when(number == 3)
-        def _():
-            second_half(1, work_ref[away, near], work_ref[away, away])
-
-        eliminate(block_ref, upper_ref.at[number], inv_ref.at[number])
-        return carry
-
-    lax.fori_loop(0, 4, body, 0)
-    join_inverse(1)
-
     inverses = [halves(full_ref[t]) for t in range(2)]
     low = halves(low_ref[...])
 
@@ -541,7 +629,7 @@
         panel_ref[:TILE, TILE:] = jnp.zeros((TILE, TILE), F32)
 
 
-def factor_panel(pan, top):
+def factor_panel(pan, top, upper, side, full, low):
     vmem = pl.BlockSpec(memory_space=pltpu.VMEM)
     return pl.pallas_call(
         panel_kernel,
@@ -549,23 +637,14 @@
             jax.ShapeDtypeStruct((PANEL_ROWS, LEAD), F32),
             jax.ShapeDtypeStruct((LEAD, COL_WIDTH), F32),
         ),
-        in_specs=[vmem, vmem],
+        in_specs=[vmem] * 6,
         out_specs=(vmem, vmem),
-        scratch_shapes=[
-            pltpu.VMEM((BLOCK, BLOCK), F32),
-            pltpu.VMEM((4, BLOCK, BLOCK), F32),
-            pltpu.VMEM((4, BLOCK, BLOCK), F32),
-            pltpu.VMEM((2, BLOCK, BLOCK), F32),
-            pltpu.VMEM((TILE, TILE), F32),
-            pltpu.VMEM((TILE, TILE), F32),
-            pltpu.VMEM((2, TILE, TILE), F32),
-        ],
-        compiler_params=pltpu.CompilerParams(vmem_limit_bytes=40 * 2**20),
+        compiler_params=pltpu.CompilerParams(vmem_limit_bytes=32 * 2**20),
         cost_estimate=pl.CostEstimate(
-            flops=60 * 10**9, bytes_accessed=14 * 2**20, transcendentals=0
+            flops=10 * 10**9, bytes_accessed=14 * 2**20, transcendentals=0
         ),
         name="panel",
-    )(pan, top)
+    )(pan, top, upper, side, full, low)
 
 
 PAIRS = COLS // 2
@@ -657,7 +736,7 @@
     here_row = lax.axis_index("row")
     here_col = lax.axis_index("col")
     own_factor = product_rows(child_panels[0], child_inverses[0])
-    factors, top = gather_all(own_factor, parent_front)
+    factors, top, lead = gather_all(own_factor, parent_front)
 
     block_of = parent_index // PCT
     my_blocks = lax.dynamic_index_in_dim(block_of, here_row, 0, keepdims=False)
@@ -665,7 +744,7 @@
     wanted = jnp.concatenate([ids, here_col[None].astype(jnp.int32)])
     order = jnp.sum(jnp.where(my_blocks[None, :] == wanted[:, None], ids[None, :], 0), axis=1)
     outgoing = update_tiles(order, factors).reshape(ROWS, 2, TILE, TILE)
-    outgoing, top = lax.optimization_barrier((outgoing, top))
+    outgoing, top, lead = lax.optimization_barrier((outgoing, top, lead))
     tiles = lax.all_to_all(outgoing, "row", split_axis=0, concat_axis=0, tiled=True)
 
     row_blocks = 2 * here_row + jnp.arange(2, dtype=jnp.int32)
@@ -682,7 +761,8 @@
         jnp.sum(jnp.where(block_of == here_col, parent_index, 0), axis=1) - here_col * PCT
     )
 
-    panel_out, top_out = factor_panel(spread_panel(top), top)
+    panel, upper, side, full, low = spread_panel(top, lead)
+    panel_out, top_out = factor_panel(panel, top, upper, side, full, low)
     schur = schur_update(
         row_places.astype(jnp.int32),
         col_places.astype(jnp.int32),

time: 192 us -> 188 us (0.979)
  Pallas kernels: 180 us -> 170 us
  local copies, waits for them, and re-layouts: 1.43 us -> 3.61 us
  starting transfers between devices: 4.67 us -> 6.63 us
    pallas_call x1, Pallas kernels: 55.8 us -> 76.4 us  [gather_all(): pl.pallas_call(gather_kernel, out_shape=(jax.ShapeDtypeStruct((COLS, TILE...]
    pallas_call x1, Pallas kernels: 33.8 us -> 13.9 us  [factor_panel(): pl.pallas_call(panel_kernel, out_shape=(jax.ShapeDtypeStruct((PANEL_ROWS,...]
    pallas_call x1, Pallas kernels: 62.7 us -> 52.6 us  [spread_panel(): pl.pallas_call(spread_kernel, out_shape=(jax.ShapeDtypeStruct((2, LEAD, C...]
    unnamed x8 -> x12, local copies, waits for them, and re-layouts: 1.34 us -> 3.52 us
    all_to_all x1, starting transfers between devices: 4.67 us -> 6.63 us  [per_device(): lax.all_to_all(outgoing, 'row', split_axis=0, concat_axis=0, tiled=True)]
  transfers between devices with their start and end apart: 1 -> 1, of which waited for: 0 -> 0; matrix products, arithmetic and copies ran while one was open for 1% -> 1% of each run, Pallas kernels for 50% -> 36%
where the time goes in v5:
time: 188 us; the launch traced here: 186 us
  Pallas kernels  170 us (90%)
  starting transfers between devices  6.63 us (4%)
  local copies, waits for them, and re-layouts  3.61 us (2%)
  other arithmetic  2.98 us (2%)
  matrix products  2.09 us (1%)
    pallas_call x1, Pallas kernels, gather_all(): pl.pallas_call(gather_kernel, out_shape=(jax.ShapeDtypeStruct((COLS, TILE...  76.4 us
    pallas_call x1, Pallas kernels, spread_panel(): pl.pallas_call(spread_kernel, out_shape=(jax.ShapeDtypeStruct((2, LEAD, C...  52.6 us
    pallas_call x1, Pallas kernels, schur_update(): pl.pallas_call(schur_kernel, out_shape=jax.ShapeDtypeStruct((PANEL_ROWS,...  16.9 us
    pallas_call x1, Pallas kernels, factor_panel(): pl.pallas_call(panel_kernel, out_shape=(jax.ShapeDtypeStruct((PANEL_ROWS,...  13.9 us
    pallas_call x1, Pallas kernels, update_tiles(): pl.pallas_call(tiles_kernel, out_shape=jax.ShapeDtypeStruct((COLS, TILE,...  10.4 us
    all_to_all x1, starting transfers between devices, per_device(): lax.all_to_all(outgoing, 'row', split_axis=0, concat_axis=0, tiled=True)  6.63 us
  transfers between devices with their start and end apart: 1, of which 0 were waited for; matrix products, arithmetic and copies ran while one was open for 1% of the time, Pallas kernels for 36%

profile of v5, /device:TPU:0, one launch (start us, length us, event | category | flops | bytes accessed | tf_op | source)
XLA Modules:
  0.0 186.2 jit_solution(14448495943216769013)
XLA Ops:
  0.6 0.0 copy-start
  0.7 0.9 select_reduce_fusion.2
  1.5 0.1 pad_add_fusion
  1.6 0.6 select_reduce_fusion.1.order_ref
  2.2 0.0 copy-done
  2.2 2.1 %fusion.own_ref = f32[256,512]{1,0:T(8,128)S(1)} fusion(f32[1,512,512]{2,1,0:T(8,128)S(1)} %copy-done, f32[1,256,512]{2,1,0:T(8,128)} %param.5), kind=kOutput, calls=%fused_computation | convolution fusion | flops 805306368 | bytes 2097152 | tf_op jit(solution)/shard_map/dot_general | solution.py:33
  4.3 76.4 %gather.1 = (f32[16,256,512]{2,1,0:T(8,128)}, f32[512,1024]{1,0:T(8,128)}, f32[512,512]{1,0:T(8,128)S(1)}) custom-call(f32[256,512]{1,0:T(8,128)S(1)} %fusion.own_ref, f32[2048,1024]{1,0:T(8,128)} %front_ref.3), custom_call_target="tpu_custom_call" | custom-call | tf_op jit(solution)/shard_map/gather/pallas_call | solution.py:473
  80.7 0.0 copy-start.3
  80.7 1.0 copy-done.3
  81.7 10.4 %tiles.1 = f32[16,256,256]{2,1,0:T(8,128)} custom-call(s32[17]{0:T(128)} %select_reduce_fusion.1.order_ref, f32[16,256,512]{2,1,0:T(8,128)} %get-tuple-element.15.all_ref), custom_call_target="tpu_custom_call" | custom-call | flops 3221225472 | bytes 12582912 | tf_op jit(solution)/shard_map/tiles/pallas_call | solution.py:667
  92.1 0.0 copy-start.5
  92.1 0.0 copy-start.2
  92.1 6.6 %all-to-all-start = ((f32[8,2,256,256]{3,2,1,0:T(8,128)}), f32[8,2,256,256]{3,2,1,0:T(8,128)}, u32[]{:S(2)}, u32[]{:S(2)}) async-start(f32[8,2,256,256]{3,2,1,0:T(8,128)} %bitcast.10), calls=%async_computation | async-start | bytes 8388608 | tf_op jit(solution)/shard_map/all_to_all | solution.py:748
  98.8 0.0 copy-done.5
  98.8 0.2 select_reduce_fusion
  99.0 0.1 copy.6
  99.1 0.6 broadcast_subtract_fusion.1.cols_ref
  99.7 0.6 broadcast_subtract_fusion.rows_ref
  100.3 0.0 copy-done.2
  100.3 0.0 copy-start.4
  100.3 1.2 copy-done.4
  101.5 52.6 %spread.1 = (f32[2,512,1024]{2,1,0:T(8,128)S(1)}, f32[4,128,128]{2,1,0:T(8,128)S(1)}, f32[2,128,128]{2,1,0:T(8,128)S(1)}, f32[2,256,256]{2,1,0:T(8,128)S(1)}, f32[256,256]{1,0:T(8,128)S(1)}) custom-call(f32[512,1024]{1,0:T(8,128)S(1)} %copy-done.2, f32[512,512]{1,0:T(8,128)S(1)} %copy-done.4), custom_call_target="tpu_custom_call" | custom-call | flops 30000001024 | bytes 20971520 | tf_op jit(solution)/shard_map/spread/pallas_call | solution.py:496
  154.1 13.9 %panel.1 = (f32[2048,512]{1,0:T(8,128)}, f32[512,1024]{1,0:T(8,128)S(1)}) custom-call(f32[2,512,1024]{2,1,0:T(8,128)S(1)} %get-tuple-element.20.pan_ref, f32[512,1024]{1,0:T(8,128)S(1)} %copy-done.2, f32[4,128,128]{2,1,0:T(8,128)S(1)} %get-tuple-element.21.upper_ref, f32[2,128,128]{2,1,0:T(8,128)S(1)} %get-tuple-element.22.side_ref, ...), custom_call_target="tpu_custom_call" | custom-call | flops 10000000000 | bytes 14680064 | tf_op jit(solution)/shard_map/panel/pallas_call | solution.py:634
  168.0 0.0 copy-start.1
  168.0 1.3 copy-done.1
  169.3 0.0 all-to-all-done.tiles_ref
  169.3 16.9 %schur.1 = f32[2048,1024]{1,0:T(8,128)} custom-call(s32[8,2]{1,0:T(8,128)} %broadcast_subtract_fusion.rows_ref, s32[8]{0:T(128)} %broadcast_subtract_fusion.1.cols_ref, f32[2048,1024]{1,0:T(8,128)} %front_ref.3, f32[2048,512]{1,0:T(8,128)} %get-tuple-element.13.panel_ref, f32[512,1024]{1,0:T(8,128)} %copy-done.1, f32[8,2,256,256]{3,2,1,0:T(8,128)} %all-to-all-done.tiles_ref), custom_call_target="tpu_custom_call" | custom-call | flops 6442450944 | bytes 27262976 | tf_op jit(solution)/shard_map/schur/pallas_call | solution.py:708
  (3 shorter events, 0.0 us)
Async XLA Ops:
  0.6 1.6 copy-start
  80.7 1.0 copy-start.3
  92.1 6.6 %copy-start.5 = (s32[8,16]{1,0:T(8,128)S(1)}, s32[8,16]{1,0:T(8,128)}, u32[]{:S(2)}) copy-start(s32[8,16]{1,0:T(8,128)} %param.7) | copy-start | bytes 1540
  92.1 8.1 %copy-start.2 = (f32[512,1024]{1,0:T(8,128)S(1)}, f32[512,1024]{1,0:T(8,128)}, u32[]{:S(2)}) copy-start(f32[512,1024]{1,0:T(8,128)} %get-tuple-element.18.top_ref) | copy-start | bytes 6291460
  92.1 77.2 %all-to-all-start = ((f32[8,2,256,256]{3,2,1,0:T(8,128)}), f32[8,2,256,256]{3,2,1,0:T(8,128)}, u32[]{:S(2)}, u32[]{:S(2)}) async-start(f32[8,2,256,256]{3,2,1,0:T(8,128)} %bitcast.10), calls=%async_computation | async-start | bytes 8388608 | tf_op jit(solution)/shard_map/all_to_all | solution.py:748
  100.3 1.2 copy-start.4
  168.0 1.3 copy-start.1

commit v6 on v5

--- a/solution.py
+++ b/solution.py
@@ -177,7 +177,7 @@
 
 
 def gather_kernel(
-    own_ref, front_ref, all_ref, top_ref, lead_ref, send_sem, recv_sem, local_sem
+    own_ref, front_ref, all_ref, top_ref, piece_ref, lead_ref, send_sem, recv_sem, local_sem
 ):
     wires = Wires(send_sem, recv_sem)
     row, col, chip, core = wires.row, wires.col, wires.chip, wires.core
@@ -253,57 +253,58 @@
             def _():
                 side.wait_send()
 
-    lead_recv = fresh()
-    lead_send = fresh(COLS)
-
-    def lead_copy(step):
+    spread = [
+        (0, pl.ds(0, LEAD), lead_ref),
+        (2 * row, pl.ds(0, COL_WIDTH), piece_ref.at[0]),
+        (2 * row + 1, pl.ds(0, COL_WIDTH), piece_ref.at[1]),
+    ]
+    spread_recv = fresh(len(spread))
+    spread_send = fresh(len(spread) * COLS)
+
+    def spread_copy(index, step):
+        _, lanes, target = spread[index]
         to_col = lax.rem(col + step, COLS)
-        rows = pl.ds(to_col * SLICE, SLICE)
         return remote(
-            top_ref.at[rows, pl.ds(0, LEAD)],
-            lead_ref.at[rows],
-            lead_send + step,
-            lead_recv,
+            top_ref.at[pl.ds(to_col * SLICE, SLICE), lanes],
+            target,
+            spread_send + index * COLS + step,
+            spread_recv + index,
             row,
             to_col,
         )
 
-    def lead_piece(slot, half, part):
-        size = SLICE // 2
-        if part == 0:
-            return lead_ref.at[pl.ds(slot * SLICE + half * size, size)]
-        base = slot * SLICE + half * size + (size // 2) * (part - 1)
-        return lead_ref.at[pl.ds(base, size // 2)]
-
-    def lead_start():
-        @pl.when(col == 0)
+    def spread_start(index):
+        holder, lanes, target = spread[index]
+
+        @pl.when(col == holder)
         def _():
             keep = pltpu.make_async_copy(
-                top_ref.at[pl.ds(0, SLICE), pl.ds(0, LEAD)],
-                lead_ref.at[pl.ds(0, SLICE)],
-                local_sem.at[2],
+                top_ref.at[pl.ds(col * SLICE, SLICE), lanes], target, local_sem.at[2 + index]
             )
             keep.start()
 
             @pl.loop(1, COLS)
             def _(step):
-                lead_copy(step).start()
+                spread_copy(index, step).start()
 
             keep.wait()
 
-    def lead_wait():
-        @pl.when(col != 0)
+    def spread_wait(index):
+        @pl.when(col != spread[index][0])
         def _():
-            lead_copy(1).wait_recv()
+            spread_copy(index, 1).wait_recv()
+
+    def spread_drain(index):
+        @pl.when(col == spread[index][0])
+        def _():
+            @pl.loop(1, COLS)
+            def _(step):
+                spread_copy(index, step).wait_send()
 
     rings = [
         wires.ring(h, factor_piece, lambda h=h: own_ref.at[pl.ds(h * 128, 128)]) for h in range(2)
     ]
-    lead_rings = [
-        wires.ring(h, lead_piece, lambda h=h: lead_piece(col, h, 0)) for h in range(2)
-    ]
     steps = ring_steps(rings)
-    lead_steps = ring_steps(lead_rings)
     for run in steps[:4]:
         run()
 
@@ -316,24 +317,18 @@
         top_step(number)
         for run in steps[4 + number : 5 + number]:
             run()
-    lead_start()
-    rest = steps[4 + top_steps :]
-    rest[0]()
-    rest[1]()
-    lead_wait()
-    for number in range(max(len(rest) - 2, len(lead_steps) // 2 + 1)):
-        for run in lead_steps[2 * number : 2 * number + 2] + rest[number + 2 : number + 3]:
-            run()
+    for index in range(len(spread)):
+        spread_start(index)
+    for run in steps[4 + top_steps :]:
+        run()
+    for index in range(len(spread)):
+        spread_wait(index)
     keep_own.wait()
     wires.drain()
     for number in range(half_pieces):
         top_drain(number)
-
-    @pl.when(col == 0)
-    def _():
-        @pl.loop(1, COLS)
-        def _(step):
-            lead_copy(step).wait_send()
+    for index in range(len(spread)):
+        spread_drain(index)
 
 
 BLOCK = 128
@@ -343,74 +338,10 @@
 AWAY = slice(BLOCK, TILE)
 
 
-def spread_kernel(
-    top_ref, lead_ref, pan_ref, upper_ref, side_ref, full_ref, low_ref,
-    block_ref, inv_ref, work_ref, send_sem, recv_sem, local_sem,
+def factor_kernel(
+    pieces_ref, upper_ref, side_ref, full_ref, low_ref, block_ref, inv_ref, work_ref, lead_ref
 ):
-    wires = Wires(send_sem, recv_sem)
-    row, col = wires.row, wires.col
-    fresh, remote = wires.fresh, wires.remote
-    wires.greet(wires.col_others())
-
-    def panel_piece(slot, half, part):
-        if part == 0:
-            return pan_ref.at[half, pl.ds(slot * SLICE, SLICE)]
-        size = SLICE // 2
-        return pan_ref.at[half, pl.ds(slot * SLICE + size * (part - 1), size)]
-
-    spread = []
-    for half in range(2):
-        spread.append((half, 2 * row + half, pl.ds(0, COL_WIDTH), pl.ds(0, COL_WIDTH)))
-    spread_recv = [fresh() for _ in spread]
-    spread_send = [fresh(COLS) for _ in spread]
-
-    def spread_copy(index, step):
-        half, _, lanes, to_lanes = spread[index]
-        to_col = lax.rem(col + step, COLS)
-        rows = pl.ds(to_col * SLICE, SLICE)
-        return remote(
-            top_ref.at[rows, lanes],
-            pan_ref.at[half, rows, to_lanes],
-            spread_send[index] + step,
-            spread_recv[index],
-            row,
-            to_col,
-        )
-
-    def spread_start(index):
-        half, holder, lanes, to_lanes = spread[index]
-        rows = pl.ds(col * SLICE, SLICE)
-
-        @pl.when(col == holder)
-        def _():
-            keep = pltpu.make_async_copy(
-                top_ref.at[rows, lanes], pan_ref.at[half, rows, to_lanes], local_sem.at[index]
-            )
-            keep.start()
-
-            @pl.loop(1, COLS)
-            def _(step):
-                spread_copy(index, step).start()
-
-            keep.wait()
-
-    def spread_wait(index):
-        @pl.when(col != spread[index][1])
-        def _():
-            spread_copy(index, 1).wait_recv()
-
-    def spread_drain(index):
-        @pl.when(col == spread[index][1])
-        def _():
-            @pl.loop(1, COLS)
-            def _(step):
-                spread_copy(index, step).wait_send()
-
-    for number in range(2):
-        spread_start(number)
-    steps = ring_steps(
-        [wires.ring(h, panel_piece, lambda h=h: panel_piece(col, h, 0)) for h in range(2)]
-    )
+    lead_ref[...] = pieces_ref[...].reshape(LEAD, LEAD)
 
     def join_inverse(tile):
         first, second, side = inv_ref[2 * tile], inv_ref[2 * tile + 1], side_ref[tile]
@@ -431,16 +362,10 @@
 
         @pl.when(number == 1)
         def _():
-            for index in range(2):
-                spread_wait(index)
-            for run in steps[:4]:
-                run()
             second_half(0, lead_ref[AWAY, NEAR], lead_ref[AWAY, AWAY])
 
         @pl.when(number == 2)
         def _():
-            for run in steps[4:8]:
-                run()
             join_inverse(0)
             low = product_rows(lead_ref[TILE:, :TILE], full_ref[0])
             low_ref[...] = low
@@ -449,22 +374,13 @@
 
         @pl.when(number == 3)
         def _():
-            for run in steps[8:12]:
-                run()
             second_half(1, work_ref[AWAY, NEAR], work_ref[AWAY, AWAY])
 
         eliminate(block_ref, upper_ref.at[number], inv_ref.at[number])
         return carry
 
     lax.fori_loop(0, 4, body, 0)
-    for run in steps[12:16]:
-        run()
     join_inverse(1)
-    for run in steps[16:]:
-        run()
-    wires.drain()
-    for number in range(2):
-        spread_drain(number)
 
 
 def gather_all(own_factor, front):
@@ -475,14 +391,15 @@
         out_shape=(
             jax.ShapeDtypeStruct((COLS, TILE, CW), F32),
             jax.ShapeDtypeStruct((LEAD, COL_WIDTH), F32),
-            jax.ShapeDtypeStruct((LEAD, LEAD), F32),
+            jax.ShapeDtypeStruct((2, SLICE, COL_WIDTH), F32),
+            jax.ShapeDtypeStruct((SLICE, LEAD), F32),
         ),
         in_specs=[vmem, anywhere],
-        out_specs=(vmem, vmem, vmem),
+        out_specs=(vmem,) * 4,
         scratch_shapes=[
             pltpu.SemaphoreType.DMA((128,)),
             pltpu.SemaphoreType.DMA((128,)),
-            pltpu.SemaphoreType.DMA((3,)),
+            pltpu.SemaphoreType.DMA((5,)),
         ],
         compiler_params=pltpu.CompilerParams(
             collective_id=0, has_side_effects=True, vmem_limit_bytes=52 * 2**20
@@ -491,35 +408,29 @@
     )(own_factor, front)
 
 
-def spread_panel(top, lead):
+def factor_lead(pieces):
     vmem = pl.BlockSpec(memory_space=pltpu.VMEM)
     return pl.pallas_call(
-        spread_kernel,
+        factor_kernel,
         out_shape=(
-            jax.ShapeDtypeStruct((2, LEAD, COL_WIDTH), F32),
             jax.ShapeDtypeStruct((4, BLOCK, BLOCK), F32),
             jax.ShapeDtypeStruct((2, BLOCK, BLOCK), F32),
             jax.ShapeDtypeStruct((2, TILE, TILE), F32),
             jax.ShapeDtypeStruct((TILE, TILE), F32),
         ),
-        in_specs=[vmem, vmem],
-        out_specs=(vmem,) * 5,
+        in_specs=[vmem],
+        out_specs=(vmem,) * 4,
         scratch_shapes=[
             pltpu.VMEM((BLOCK, BLOCK), F32),
             pltpu.VMEM((4, BLOCK, BLOCK), F32),
             pltpu.VMEM((TILE, TILE), F32),
-            pltpu.SemaphoreType.DMA((80,)),
-            pltpu.SemaphoreType.DMA((80,)),
-            pltpu.SemaphoreType.DMA((2,)),
+            pltpu.VMEM((LEAD, LEAD), F32),
         ],
-        compiler_params=pltpu.CompilerParams(
-            collective_id=1, has_side_effects=True, vmem_limit_bytes=24 * 2**20
-        ),
         cost_estimate=pl.CostEstimate(
-            flops=30 * 10**9, bytes_accessed=20 * 2**20, transcendentals=0
-        ),
-        name="spread",
-    )(top, lead)
+            flops=15 * 10**9, bytes_accessed=20 * 2**20, transcendentals=0
+        ),
+        name="factor",
+    )(pieces)
 
 
 def eliminate(block_ref, upper_ref, inverse_ref):
@@ -580,15 +491,15 @@
     inverses = [halves(full_ref[t]) for t in range(2)]
     low = halves(low_ref[...])
 
-    def chunk(source, lanes):
-        first = three_pass(inverses[0], halves(source[:TILE, lanes]), ((1,), (0,)))
-        rest = source[TILE:, lanes] - three_pass(low, halves(first), ((1,), (0,)))
+    def chunk(block):
+        first = three_pass(inverses[0], halves(block[:TILE]), ((1,), (0,)))
+        rest = block[TILE:] - three_pass(low, halves(first), ((1,), (0,)))
         return first, three_pass(inverses[1], halves(rest), ((1,), (0,)))
 
     @pl.loop(0, PCT)
     def _(part):
         lanes = pl.ds(pl.multiple_of(part * TILE, TILE), TILE)
-        first, second = chunk(top_ref, lanes)
+        first, second = chunk(top_ref[:, lanes])
         cols_ref[:TILE, lanes] = first
         cols_ref[TILE:, lanes] = second
 
@@ -596,7 +507,8 @@
     def _(part):
         lanes = pl.ds(pl.multiple_of(lax.rem(part, PCT) * TILE, TILE), TILE)
         rows = pl.ds(pl.multiple_of(part * TILE, TILE), TILE)
-        first, second = chunk(pan_ref.at[part // PCT], lanes)
+        block = pan_ref[:, part // PCT, :, lanes].reshape(LEAD, TILE)
+        first, second = chunk(block)
         panel_ref[rows, :TILE] = first.T
         panel_ref[rows, TILE:] = second.T
 
@@ -736,7 +648,9 @@
     here_row = lax.axis_index("row")
     here_col = lax.axis_index("col")
     own_factor = product_rows(child_panels[0], child_inverses[0])
-    factors, top, lead = gather_all(own_factor, parent_front)
+    factors, top, piece, lead = gather_all(own_factor, parent_front)
+    lead = lax.all_gather(lead, "col", axis=0)
+    panel = lax.all_gather(piece, "col", axis=0)
 
     block_of = parent_index // PCT
     my_blocks = lax.dynamic_index_in_dim(block_of, here_row, 0, keepdims=False)
@@ -744,7 +658,6 @@
     wanted = jnp.concatenate([ids, here_col[None].astype(jnp.int32)])
     order = jnp.sum(jnp.where(my_blocks[None, :] == wanted[:, None], ids[None, :], 0), axis=1)
     outgoing = update_tiles(order, factors).reshape(ROWS, 2, TILE, TILE)
-    outgoing, top, lead = lax.optimization_barrier((outgoing, top, lead))
     tiles = lax.all_to_all(outgoing, "row", split_axis=0, concat_axis=0, tiled=True)
 
     row_blocks = 2 * here_row + jnp.arange(2, dtype=jnp.int32)
@@ -761,7 +674,7 @@
         jnp.sum(jnp.where(block_of == here_col, parent_index, 0), axis=1) - here_col * PCT
     )
 
-    panel, upper, side, full, low = spread_panel(top, lead)
+    upper, side, full, low = factor_lead(lead)
     panel_out, top_out = factor_panel(panel, top, upper, side, full, low)
     schur = schur_update(
         row_places.astype(jnp.int32),

time: 188 us -> 227 us (1.21)
  waiting for transfers between devices: 0.01 us -> 52.1 us
  Pallas kernels: 170 us -> 142 us
  between operations: 0.7 us -> 14.1 us
  local copies, waits for them, and re-layouts: 3.61 us -> 8.64 us
    all_gather x0 -> x2, waiting for transfers between devices: none -> 51.4 us  [the longest x1 30.9 us: per_device(): panel = lax.all_gather(piece, 'col', axis=0)]
    pallas_call x1, Pallas kernels: 52.6 us -> 22.3 us  [factor_lead(): pl.pallas_call(factor_kernel, out_shape=(jax.ShapeDtypeStruct((4, BLOCK,...]
    unnamed x12 -> x18, local copies, waits for them, and re-layouts: 3.52 us -> 8.54 us
  transfers between devices with their start and end apart: 1 -> 3, of which waited for: 0 -> 2; matrix products, arithmetic and copies ran while one was open for 1% -> 1% of each run, Pallas kernels for 36% -> 21%
where the time goes in v6:
time: 227 us; the launch traced here: 225 us
  Pallas kernels  142 us (63%)
  waiting for transfers between devices  52.1 us (23%)
  between operations  14.1 us (6%)
  local copies, waits for them, and re-layouts  8.64 us (4%)
  starting transfers between devices  4.64 us (2%)
    pallas_call x1, Pallas kernels, gather_all(): pl.pallas_call(gather_kernel, out_shape=(jax.ShapeDtypeStruct((COLS, TILE...  78.1 us
    all_gather x1, waiting for transfers between devices, per_device(): panel = lax.all_gather(piece, 'col', axis=0)  30.9 us
    pallas_call x1, Pallas kernels, factor_lead(): pl.pallas_call(factor_kernel, out_shape=(jax.ShapeDtypeStruct((4, BLOCK,...  22.3 us
    all_gather x1, waiting for transfers between devices, per_device(): lead = lax.all_gather(lead, 'col', axis=0)  20.5 us
    pallas_call x1, Pallas kernels, schur_update(): pl.pallas_call(schur_kernel, out_shape=jax.ShapeDtypeStruct((PANEL_ROWS,...  16.9 us
    pallas_call x1, Pallas kernels, factor_panel(): pl.pallas_call(panel_kernel, out_shape=(jax.ShapeDtypeStruct((PANEL_ROWS,...  13.9 us
    pallas_call x1, Pallas kernels, update_tiles(): pl.pallas_call(tiles_kernel, out_shape=jax.ShapeDtypeStruct((COLS, TILE,...  10.5 us
    unnamed x18, local copies, waits for them, and re-layouts  8.54 us
  transfers between devices with their start and end apart: 3, of which 2 were waited for; matrix products, arithmetic and copies ran while one was open for 1% of the time, Pallas kernels for 21%

profile of v6, /device:TPU:0, one launch (start us, length us, event | category | flops | bytes accessed | tf_op | source)
XLA Modules:
  0.0 225.4 jit_solution(6364293688553969835)
XLA Ops:
  7.2 0.0 copy-start
  7.2 0.0 all-gather.7.cloned.1.call-start
  7.2 1.2 copy-done
  8.4 2.1 fusion.own_ref
  10.5 0.0 copy-start.8
  10.5 78.1 %gather.1 = (f32[16,256,512]{2,1,0:T(8,128)}, f32[512,1024]{1,0:T(8,128)}, f32[2,32,1024]{2,1,0:T(8,128)}, f32[32,512]{1,0:T(8,128)}) custom-call(f32[256,512]{1,0:T(8,128)S(1)} %fusion.own_ref, f32[2048,1024]{1,0:T(8,128)} %front_ref.3), custom_call_target="tpu_custom_call" | custom-call | tf_op jit(solution)/shard_map/gather/pallas_call | solution.py:389
  88.6 0.0 all-gather.7.cloned.1.call-update
  88.6 0.0 all-gather.5.cloned.1.call-start
  88.7 0.7 all-gather.5.cloned.1.call-update
  89.4 0.0 copy-done.8
  89.4 0.1 select_reduce_fusion.2
  89.5 0.1 pad_add_fusion
  89.6 0.6 select_reduce_fusion.order_ref
  90.2 10.5 %tiles.1 = f32[16,256,256]{2,1,0:T(8,128)} custom-call(s32[17]{0:T(128)} %select_reduce_fusion.order_ref, f32[16,256,512]{2,1,0:T(8,128)} %get-tuple-element.21.all_ref), custom_call_target="tpu_custom_call" | custom-call | flops 3221225472 | bytes 12582912 | tf_op jit(solution)/shard_map/tiles/pallas_call | solution.py:579
  100.7 4.6 %all-to-all-start = ((f32[8,2,256,256]{3,2,1,0:T(8,128)}), f32[8,2,256,256]{3,2,1,0:T(8,128)}, u32[]{:S(2)}, u32[]{:S(2)}) async-start(f32[8,2,256,256]{3,2,1,0:T(8,128)} %bitcast.13), calls=%async_computation | async-start | bytes 8388608 | tf_op jit(solution)/shard_map/all_to_all | solution.py:661
  105.3 0.2 select_reduce_fusion.1
  105.5 0.1 copy.6
  105.6 0.6 broadcast_subtract_fusion.1.cols_ref
  106.1 0.6 broadcast_subtract_fusion.rows_ref
  106.7 20.5 %all-gather.7.cloned.1.call-done = f32[512,512]{1,0:T(8,128)} async-done(((f32[32,512]{1,0:T(8,128)}), f32[512,512]{1,0:T(8,128)}) %all-gather.7.cloned.1.call-update) | async-done | bytes 1048592 | tf_op jit(solution)/shard_map/all_gather | solution.py:652
  127.2 0.0 copy-start.3
  127.2 22.3 %factor.1 = (f32[4,128,128]{2,1,0:T(8,128)}, f32[2,128,128]{2,1,0:T(8,128)}, f32[2,256,256]{2,1,0:T(8,128)}, f32[256,256]{1,0:T(8,128)}) custom-call(f32[16,32,512]{2,1,0:T(8,128)} %bitcast.14), custom_call_target="tpu_custom_call" | custom-call | flops 15000000512 | bytes 20971520 | tf_op jit(solution)/shard_map/factor/pallas_call | solution.py:413
  149.5 30.9 %all-gather.5.cloned.1.call-done = f32[32,32,1024]{2,1,0:T(8,128)} async-done(((f32[2,32,1024]{2,1,0:T(8,128)}), f32[32,32,1024]{2,1,0:T(8,128)}) %all-gather.5.cloned.1.call-update) | async-done | bytes 4194320 | tf_op jit(solution)/shard_map/all_gather | solution.py:653
  180.4 0.0 copy-done.3
  180.4 0.0 copy-start.2
  180.4 2.2 copy-done.2
  182.6 0.0 copy-start.4
  182.6 1.0 copy-done.4
  183.6 0.0 copy-start.5
  183.6 0.9 copy-done.5
  184.6 0.0 copy-start.6
  184.6 0.9 copy-done.6
  185.5 0.0 copy-start.7
  185.5 0.9 copy-done.7
  186.4 13.9 %panel.1 = (f32[2048,512]{1,0:T(8,128)}, f32[512,1024]{1,0:T(8,128)S(1)}) custom-call(f32[16,2,32,1024]{3,2,1,0:T(8,128)S(1)} %bitcast.12, f32[512,1024]{1,0:T(8,128)S(1)} %copy-done.3, f32[4,128,128]{2,1,0:T(8,128)S(1)} %copy-done.5, f32[2,128,128]{2,1,0:T(8,128)S(1)} %copy-done.7, f32[2,256,256]{2,1,0:T(8,128)S(1)} %copy-done.4, f32[256,256]{1,0:T(8,128)S(1)} %copy-done.6), custom_call_target="tpu_custom_call" | custom-call | flops 10000000000 | bytes 14680064 | tf_op jit(solution)/shard_map/panel/pallas_call | solution.py:546
  200.3 0.0 copy-start.1
  200.3 1.3 copy-done.1
  201.6 0.0 all-to-all-done.tiles_ref
  201.6 16.9 %schur.1 = f32[2048,1024]{1,0:T(8,128)} custom-call(s32[8,2]{1,0:T(8,128)} %broadcast_subtract_fusion.rows_ref, s32[8]{0:T(128)} %broadcast_subtract_fusion.1.cols_ref, f32[2048,1024]{1,0:T(8,128)} %front_ref.3, f32[2048,512]{1,0:T(8,128)} %get-tuple-element.10.panel_ref, f32[512,1024]{1,0:T(8,128)} %copy-done.1, f32[8,2,256,256]{3,2,1,0:T(8,128)} %all-to-all-done.tiles_ref), custom_call_target="tpu_custom_call" | custom-call | flops 6442450944 | bytes 27262976 | tf_op jit(solution)/shard_map/schur/pallas_call | solution.py:620
  (3 shorter events, 0.0 us)
Async XLA Ops:
  7.2 1.2 copy-start
  7.2 120.0 %all-gather.7.cloned.1.call-start = ((), (), s32[]{:S(2)}) async-start(), calls=%async_computation.2 | async-start | bytes 1114112 | tf_op jit(solution)/shard_map/all_gather | solution.py:652
  10.5 78.9 %copy-start.8 = (s32[8,16]{1,0:T(8,128)S(1)}, s32[8,16]{1,0:T(8,128)}, u32[]{:S(2)}) copy-start(s32[8,16]{1,0:T(8,128)} %param.7) | copy-start | bytes 1540
  88.6 91.8 %all-gather.5.cloned.1.call-start = ((), (), s32[]{:S(2)}) async-start(), calls=%async_computation.1 | async-start | bytes 4456448 | tf_op jit(solution)/shard_map/all_gather | solution.py:653
  100.7 101.0 %all-to-all-start = ((f32[8,2,256,256]{3,2,1,0:T(8,128)}), f32[8,2,256,256]{3,2,1,0:T(8,128)}, u32[]{:S(2)}, u32[]{:S(2)}) async-start(f32[8,2,256,256]{3,2,1,0:T(8,128)} %bitcast.13), calls=%async_computation | async-start | bytes 8388608 | tf_op jit(solution)/shard_map/all_to_all | solution.py:661
  127.2 53.2 %copy-start.3 = (f32[512,1024]{1,0:T(8,128)S(1)}, f32[512,1024]{1,0:T(8,128)}, u32[]{:S(2)}) copy-start(f32[512,1024]{1,0:T(8,128)} %get-tuple-element.13.top_ref) | copy-start | bytes 6291460
  180.4 2.2 copy-start.2
  182.6 1.0 copy-start.4
  183.6 0.9 copy-start.5
  184.6 0.9 copy-start.6
  185.5 0.9 copy-start.7
  200.3 1.3 copy-start.1
Sparse Core Ops, SparseCore 0:
  88.7 38.4 all-gather.6
  129.3 50.9 all-gather.4

commit v7 on v5

--- a/solution.py
+++ b/solution.py
@@ -177,7 +177,8 @@
 
 
 def gather_kernel(
-    own_ref, front_ref, all_ref, top_ref, lead_ref, send_sem, recv_sem, local_sem
+    order_ref, own_ref, front_ref, tiles_ref, top_ref,
+    all_ref, high_ref, low_ref, send_sem, recv_sem, local_sem,
 ):
     wires = Wires(send_sem, recv_sem)
     row, col, chip, core = wires.row, wires.col, wires.chip, wires.core
@@ -191,7 +192,7 @@
     keep_own = pltpu.make_async_copy(own_ref, all_ref.at[col], local_sem.at[1])
     keep_own.start()
     wires.greet(
-        wires.col_others()
+        [(row, wires.at(*step)) for step in ((1, 0), (-1, 0), (0, 1), (0, -1))]
         + [
             (row + 1 - 2 * core, col),
             (lax.rem(row + 2, ROWS), col),
@@ -253,57 +254,10 @@
             def _():
                 side.wait_send()
 
-    lead_recv = fresh()
-    lead_send = fresh(COLS)
-
-    def lead_copy(step):
-        to_col = lax.rem(col + step, COLS)
-        rows = pl.ds(to_col * SLICE, SLICE)
-        return remote(
-            top_ref.at[rows, pl.ds(0, LEAD)],
-            lead_ref.at[rows],
-            lead_send + step,
-            lead_recv,
-            row,
-            to_col,
-        )
-
-    def lead_piece(slot, half, part):
-        size = SLICE // 2
-        if part == 0:
-            return lead_ref.at[pl.ds(slot * SLICE + half * size, size)]
-        base = slot * SLICE + half * size + (size // 2) * (part - 1)
-        return lead_ref.at[pl.ds(base, size // 2)]
-
-    def lead_start():
-        @pl.when(col == 0)
-        def _():
-            keep = pltpu.make_async_copy(
-                top_ref.at[pl.ds(0, SLICE), pl.ds(0, LEAD)],
-                lead_ref.at[pl.ds(0, SLICE)],
-                local_sem.at[2],
-            )
-            keep.start()
-
-            @pl.loop(1, COLS)
-            def _(step):
-                lead_copy(step).start()
-
-            keep.wait()
-
-    def lead_wait():
-        @pl.when(col != 0)
-        def _():
-            lead_copy(1).wait_recv()
-
     rings = [
         wires.ring(h, factor_piece, lambda h=h: own_ref.at[pl.ds(h * 128, 128)]) for h in range(2)
     ]
-    lead_rings = [
-        wires.ring(h, lead_piece, lambda h=h: lead_piece(col, h, 0)) for h in range(2)
-    ]
     steps = ring_steps(rings)
-    lead_steps = ring_steps(lead_rings)
     for run in steps[:4]:
         run()
 
@@ -311,29 +265,23 @@
     def _():
         load_top.wait()
 
-    top_steps = half_pieces + SIDE
-    for number in range(top_steps):
+    for number in range(half_pieces + SIDE):
         top_step(number)
-        for run in steps[4 + number : 5 + number]:
+        for run in steps[4 + 2 * number : 6 + 2 * number]:
             run()
-    lead_start()
-    rest = steps[4 + top_steps :]
-    rest[0]()
-    rest[1]()
-    lead_wait()
-    for number in range(max(len(rest) - 2, len(lead_steps) // 2 + 1)):
-        for run in lead_steps[2 * number : 2 * number + 2] + rest[number + 2 : number + 3]:
-            run()
+    for run in steps[4 + 2 * (half_pieces + SIDE) :]:
+        run()
     keep_own.wait()
+    high_ref[...], low_ref[...] = halves(all_ref[order_ref[COLS]])
+
+    @pl.loop(0, COLS)
+    def _(number):
+        left = halves(all_ref[order_ref[number]])
+        tiles_ref[number] = three_pass(left, (high_ref[...], low_ref[...]), ((1,), (1,)))
+
     wires.drain()
     for number in range(half_pieces):
         top_drain(number)
-
-    @pl.when(col == 0)
-    def _():
-        @pl.loop(1, COLS)
-        def _(step):
-            lead_copy(step).wait_send()
 
 
 BLOCK = 128
@@ -344,8 +292,8 @@
 
 
 def spread_kernel(
-    top_ref, lead_ref, pan_ref, upper_ref, side_ref, full_ref, low_ref,
-    block_ref, inv_ref, work_ref, send_sem, recv_sem, local_sem,
+    top_ref, pan_ref, upper_ref, side_ref, full_ref, low_ref,
+    block_ref, inv_ref, work_ref, lead_ref, send_sem, recv_sem, local_sem,
 ):
     wires = Wires(send_sem, recv_sem)
     row, col = wires.row, wires.col
@@ -406,11 +354,61 @@
             def _(step):
                 spread_copy(index, step).wait_send()
 
+    lead_recv = fresh()
+    lead_send = fresh(COLS)
+
+    def lead_copy(step):
+        to_col = lax.rem(col + step, COLS)
+        rows = pl.ds(to_col * SLICE, SLICE)
+        return remote(
+            top_ref.at[rows, pl.ds(0, LEAD)],
+            lead_ref.at[rows],
+            lead_send + step,
+            lead_recv,
+            row,
+            to_col,
+        )
+
+    def lead_piece(slot, half, part):
+        size = SLICE // 2
+        if part == 0:
+            return lead_ref.at[pl.ds(slot * SLICE + half * size, size)]
+        base = slot * SLICE + half * size + (size // 2) * (part - 1)
+        return lead_ref.at[pl.ds(base, size // 2)]
+
+    def lead_start():
+        @pl.when(col == 0)
+        def _():
+            keep = pltpu.make_async_copy(
+                top_ref.at[pl.ds(0, SLICE), pl.ds(0, LEAD)],
+                lead_ref.at[pl.ds(0, SLICE)],
+                local_sem.at[2],
+            )
+            keep.start()
+
+            @pl.loop(1, COLS)
+            def _(step):
+                lead_copy(step).start()
+
+            keep.wait()
+
+    def lead_wait():
+        @pl.when(col != 0)
+        def _():
+            lead_copy(1).wait_recv()
+
+    lead_start()
     for number in range(2):
         spread_start(number)
+    lead_rings = [
+        wires.ring(h, lead_piece, lambda h=h: lead_piece(col, h, 0)) for h in range(2)
+    ]
     steps = ring_steps(
         [wires.ring(h, panel_piece, lambda h=h: panel_piece(col, h, 0)) for h in range(2)]
     )
+    lead_wait()
+    for run in ring_steps(lead_rings):
+        run()
 
     def join_inverse(tile):
         first, second, side = inv_ref[2 * tile], inv_ref[2 * tile + 1], side_ref[tile]
@@ -427,19 +425,21 @@
     def body(number, carry):
         @pl.when(number == 0)
         def _():
-            block_ref[...] = lead_ref[NEAR, NEAR]
-
-        @pl.when(number == 1)
-        def _():
             for index in range(2):
                 spread_wait(index)
             for run in steps[:4]:
                 run()
+            block_ref[...] = lead_ref[NEAR, NEAR]
+
+        @pl.when(number == 1)
+        def _():
+            for run in steps[4:8]:
+                run()
             second_half(0, lead_ref[AWAY, NEAR], lead_ref[AWAY, AWAY])
 
         @pl.when(number == 2)
         def _():
-            for run in steps[4:8]:
+            for run in steps[8:12]:
                 run()
             join_inverse(0)
             low = product_rows(lead_ref[TILE:, :TILE], full_ref[0])
@@ -449,7 +449,7 @@
 
         @pl.when(number == 3)
         def _():
-            for run in steps[8:12]:
+            for run in steps[12:16]:
                 run()
             second_half(1, work_ref[AWAY, NEAR], work_ref[AWAY, AWAY])
 
@@ -457,8 +457,6 @@
         return carry
 
     lax.fori_loop(0, 4, body, 0)
-    for run in steps[12:16]:
-        run()
     join_inverse(1)
     for run in steps[16:]:
         run()
@@ -466,32 +464,40 @@
     for number in range(2):
         spread_drain(number)
 
-
-def gather_all(own_factor, front):
+    @pl.when(col == 0)
+    def _():
+        @pl.loop(1, COLS)
+        def _(step):
+            lead_copy(step).wait_send()
+
+
+def gather_tiles(order, own_factor, front):
     anywhere = pl.BlockSpec(memory_space=pl.ANY)
     vmem = pl.BlockSpec(memory_space=pltpu.VMEM)
     return pl.pallas_call(
         gather_kernel,
         out_shape=(
-            jax.ShapeDtypeStruct((COLS, TILE, CW), F32),
+            jax.ShapeDtypeStruct((COLS, TILE, TILE), F32),
             jax.ShapeDtypeStruct((LEAD, COL_WIDTH), F32),
-            jax.ShapeDtypeStruct((LEAD, LEAD), F32),
         ),
-        in_specs=[vmem, anywhere],
-        out_specs=(vmem, vmem, vmem),
+        in_specs=[pl.BlockSpec(memory_space=pltpu.SMEM), vmem, anywhere],
+        out_specs=(vmem, vmem),
         scratch_shapes=[
-            pltpu.SemaphoreType.DMA((128,)),
-            pltpu.SemaphoreType.DMA((128,)),
-            pltpu.SemaphoreType.DMA((3,)),
+            pltpu.VMEM((COLS, TILE, CW), F32),
+            pltpu.VMEM((TILE, CW), BF16),
+            pltpu.VMEM((TILE, CW), BF16),
+            pltpu.SemaphoreType.DMA((72,)),
+            pltpu.SemaphoreType.DMA((72,)),
+            pltpu.SemaphoreType.DMA((2,)),
         ],
         compiler_params=pltpu.CompilerParams(
-            collective_id=0, has_side_effects=True, vmem_limit_bytes=52 * 2**20
+            collective_id=0, has_side_effects=True, vmem_limit_bytes=56 * 2**20
         ),
         name="gather",
-    )(own_factor, front)
-
-
-def spread_panel(top, lead):
+    )(order, own_factor, front)
+
+
+def spread_panel(top):
     vmem = pl.BlockSpec(memory_space=pltpu.VMEM)
     return pl.pallas_call(
         spread_kernel,
@@ -502,24 +508,25 @@
             jax.ShapeDtypeStruct((2, TILE, TILE), F32),
             jax.ShapeDtypeStruct((TILE, TILE), F32),
         ),
-        in_specs=[vmem, vmem],
+        in_specs=[vmem],
         out_specs=(vmem,) * 5,
         scratch_shapes=[
             pltpu.VMEM((BLOCK, BLOCK), F32),
             pltpu.VMEM((4, BLOCK, BLOCK), F32),
             pltpu.VMEM((TILE, TILE), F32),
-            pltpu.SemaphoreType.DMA((80,)),
-            pltpu.SemaphoreType.DMA((80,)),
-            pltpu.SemaphoreType.DMA((2,)),
+            pltpu.VMEM((LEAD, LEAD), F32),
+            pltpu.SemaphoreType.DMA((136,)),
+            pltpu.SemaphoreType.DMA((136,)),
+            pltpu.SemaphoreType.DMA((3,)),
         ],
         compiler_params=pltpu.CompilerParams(
-            collective_id=1, has_side_effects=True, vmem_limit_bytes=24 * 2**20
+            collective_id=1, has_side_effects=True, vmem_limit_bytes=56 * 2**20
         ),
         cost_estimate=pl.CostEstimate(
             flops=30 * 10**9, bytes_accessed=20 * 2**20, transcendentals=0
         ),
         name="spread",
-    )(top, lead)
+    )(top)
 
 
 def eliminate(block_ref, upper_ref, inverse_ref):
@@ -572,129 +579,67 @@
         inverse_ref[base : base + GROUP, :] = new_r * scale
 
 
-def panel_kernel(
-    pan_ref, top_ref, upper_ref, side_ref, full_ref, low_ref, panel_ref, cols_ref
+def final_kernel(
+    rows_ref, cols_ref, front_ref, pan_ref, top_ref, upper_ref, side_ref, full_ref, low_ref,
+    tiles_ref, panel_ref, out_ref, right_ref, high_ref, small_ref,
 ):
     row = lax.axis_index("row")
     col = lax.axis_index("col")
+    step = pl.program_id(0)
     inverses = [halves(full_ref[t]) for t in range(2)]
     low = halves(low_ref[...])
-
-    def chunk(source, lanes):
-        first = three_pass(inverses[0], halves(source[:TILE, lanes]), ((1,), (0,)))
-        rest = source[TILE:, lanes] - three_pass(low, halves(first), ((1,), (0,)))
+    blank = jnp.zeros((BLOCK, BLOCK), F32)
+
+    def chunk(block):
+        first = three_pass(inverses[0], halves(block[:TILE]), ((1,), (0,)))
+        rest = block[TILE:] - three_pass(low, halves(first), ((1,), (0,)))
         return first, three_pass(inverses[1], halves(rest), ((1,), (0,)))
 
-    @pl.loop(0, PCT)
-    def _(part):
-        lanes = pl.ds(pl.multiple_of(part * TILE, TILE), TILE)
-        first, second = chunk(top_ref, lanes)
-        cols_ref[:TILE, lanes] = first
-        cols_ref[TILE:, lanes] = second
-
-    @pl.loop(0, RT)
-    def _(part):
-        lanes = pl.ds(pl.multiple_of(lax.rem(part, PCT) * TILE, TILE), TILE)
-        rows = pl.ds(pl.multiple_of(part * TILE, TILE), TILE)
-        first, second = chunk(pan_ref.at[part // PCT], lanes)
-        panel_ref[rows, :TILE] = first.T
-        panel_ref[rows, TILE:] = second.T
-
-    blank = jnp.zeros((BLOCK, BLOCK), F32)
-
-    @pl.when(col == 0)
+    @pl.when(step == 0)
     def _():
-        for t in range(2):
-            for r, c, value in (
-                (0, 0, upper_ref[2 * t]),
-                (0, 1, side_ref[t].T),
-                (1, 0, blank),
-                (1, 1, upper_ref[2 * t + 1]),
-            ):
-                r0, c0 = t * TILE + r * BLOCK, t * TILE + c * BLOCK
-                cols_ref[r0 : r0 + BLOCK, c0 : c0 + BLOCK] = value
-        cols_ref[TILE:, :TILE] = jnp.zeros((TILE, TILE), F32)
-
-    @pl.when(row == 0)
-    def _():
-        for t in range(2):
+        for part in range(PCT):
+            lanes = slice(part * TILE, (part + 1) * TILE)
+            right_ref[:TILE, lanes], right_ref[TILE:, lanes] = chunk(top_ref[:, lanes])
+
+        @pl.when(col == 0)
+        def _():
+            for t in range(2):
+                for r, c, value in (
+                    (0, 0, upper_ref[2 * t]),
+                    (0, 1, side_ref[t].T),
+                    (1, 0, blank),
+                    (1, 1, upper_ref[2 * t + 1]),
+                ):
+                    r0, c0 = t * TILE + r * BLOCK, t * TILE + c * BLOCK
+                    right_ref[r0 : r0 + BLOCK, c0 : c0 + BLOCK] = value
+            right_ref[TILE:, :TILE] = jnp.zeros((TILE, TILE), F32)
+
+        high_ref[...], small_ref[...] = halves(right_ref[...])
+
+    first, second = chunk(pan_ref[0])
+    panel_ref[:, :TILE] = first.T
+    panel_ref[:, TILE:] = second.T
+
+    for t in range(2):
+
+        @pl.when((row == 0) & (step == t))
+        def _(t=t):
             for r, c, value in (
                 (0, 0, upper_ref[2 * t].T),
                 (0, 1, blank),
                 (1, 0, side_ref[t]),
                 (1, 1, upper_ref[2 * t + 1].T),
             ):
-                r0, c0 = t * TILE + r * BLOCK, t * TILE + c * BLOCK
+                r0, c0 = r * BLOCK, t * TILE + c * BLOCK
                 panel_ref[r0 : r0 + BLOCK, c0 : c0 + BLOCK] = value
-        panel_ref[:TILE, TILE:] = jnp.zeros((TILE, TILE), F32)
-
-
-def factor_panel(pan, top, upper, side, full, low):
-    vmem = pl.BlockSpec(memory_space=pltpu.VMEM)
-    return pl.pallas_call(
-        panel_kernel,
-        out_shape=(
-            jax.ShapeDtypeStruct((PANEL_ROWS, LEAD), F32),
-            jax.ShapeDtypeStruct((LEAD, COL_WIDTH), F32),
-        ),
-        in_specs=[vmem] * 6,
-        out_specs=(vmem, vmem),
-        compiler_params=pltpu.CompilerParams(vmem_limit_bytes=32 * 2**20),
-        cost_estimate=pl.CostEstimate(
-            flops=10 * 10**9, bytes_accessed=14 * 2**20, transcendentals=0
-        ),
-        name="panel",
-    )(pan, top, upper, side, full, low)
-
-
-PAIRS = COLS // 2
-
-
-def tiles_kernel(order_ref, all_ref, out_ref, high_ref, low_ref):
-    step = pl.program_id(0)
-
-    @pl.when(step == 0)
-    def _():
-        high_ref[...], low_ref[...] = halves(all_ref[order_ref[COLS]])
-
-    right = (high_ref[...], low_ref[...])
-    for part in range(2):
-        left = halves(all_ref[order_ref[2 * step + part]])
-        out_ref[part] = three_pass(left, right, ((1,), (1,)))
-
-
-def update_tiles(order, factors):
-    return pl.pallas_call(
-        tiles_kernel,
-        out_shape=jax.ShapeDtypeStruct((COLS, TILE, TILE), F32),
-        grid_spec=pltpu.PrefetchScalarGridSpec(
-            num_scalar_prefetch=1,
-            grid=(PAIRS,),
-            in_specs=[pl.BlockSpec(memory_space=pltpu.VMEM)],
-            out_specs=pl.BlockSpec((2, TILE, TILE), lambda i, order: (i, 0, 0)),
-            scratch_shapes=[pltpu.VMEM((TILE, CW), BF16), pltpu.VMEM((TILE, CW), BF16)],
-        ),
-        cost_estimate=pl.CostEstimate(
-            flops=6 * COLS * TILE * TILE * CW, bytes_accessed=12 * 2**20, transcendentals=0
-        ),
-        name="tiles",
-    )(order, factors)
-
-
-def schur_kernel(
-    rows_ref, cols_ref, front_ref, panel_ref, top_ref, tiles_ref, out_ref, high_ref, low_ref
-):
-    step = pl.program_id(0)
-
-    @pl.when(step == 0)
-    def _():
-        high_ref[...], low_ref[...] = halves(top_ref[...])
+            if t == 0:
+                panel_ref[:, TILE:] = jnp.zeros((TILE, TILE), F32)
 
     left = halves(panel_ref[...])
     for part in range(PCT):
-        lanes = slice(part * TILE, (part + 1) * TILE)
-        right = (high_ref[:, lanes], low_ref[:, lanes])
-        out_ref[:, lanes] = front_ref[:, lanes] - three_pass(left, right, ((1,), (0,)))
+        span = slice(part * TILE, (part + 1) * TILE)
+        right = (high_ref[:, span], small_ref[:, span])
+        out_ref[:, span] = front_ref[:, span] - three_pass(left, right, ((1,), (0,)))
     block = step // PCT
     for child in range(ROWS):
 
@@ -704,47 +649,57 @@
             out_ref[:, pl.ds(start, TILE)] -= tiles_ref[child, 0]
 
 
-def schur_update(row_places, col_places, front, panel, top, tiles):
+def finish(row_places, col_places, front, pan, top, upper, side, full, low, tiles):
     return pl.pallas_call(
-        schur_kernel,
-        out_shape=jax.ShapeDtypeStruct((PANEL_ROWS, COL_WIDTH), F32),
+        final_kernel,
+        out_shape=(
+            jax.ShapeDtypeStruct((PANEL_ROWS, LEAD), F32),
+            jax.ShapeDtypeStruct((PANEL_ROWS, COL_WIDTH), F32),
+        ),
         grid_spec=pltpu.PrefetchScalarGridSpec(
             num_scalar_prefetch=2,
             grid=(RT,),
             in_specs=[
                 pl.BlockSpec((TILE, COL_WIDTH), lambda i, *_: (i, 0)),
-                pl.BlockSpec((TILE, LEAD), lambda i, *_: (i, 0)),
-                pl.BlockSpec(memory_space=pltpu.VMEM),
+                pl.BlockSpec((1, LEAD, TILE), lambda i, *_: (i // PCT, 0, lax.rem(i, PCT))),
+                pl.BlockSpec((LEAD, COL_WIDTH), lambda i, *_: (0, 0)),
+                pl.BlockSpec((4, BLOCK, BLOCK), lambda i, *_: (0, 0, 0)),
+                pl.BlockSpec((2, BLOCK, BLOCK), lambda i, *_: (0, 0, 0)),
+                pl.BlockSpec((2, TILE, TILE), lambda i, *_: (0, 0, 0)),
+                pl.BlockSpec((TILE, TILE), lambda i, *_: (0, 0)),
                 pl.BlockSpec((ROWS, 1, TILE, TILE), lambda i, *_: (0, i // PCT, 0, 0)),
             ],
-            out_specs=pl.BlockSpec((TILE, COL_WIDTH), lambda i, *_: (i, 0)),
+            out_specs=(
+                pl.BlockSpec((TILE, LEAD), lambda i, *_: (i, 0)),
+                pl.BlockSpec((TILE, COL_WIDTH), lambda i, *_: (i, 0)),
+            ),
             scratch_shapes=[
+                pltpu.VMEM((LEAD, COL_WIDTH), F32),
                 pltpu.VMEM((LEAD, COL_WIDTH), BF16),
                 pltpu.VMEM((LEAD, COL_WIDTH), BF16),
             ],
         ),
+        compiler_params=pltpu.CompilerParams(vmem_limit_bytes=40 * 2**20),
         cost_estimate=pl.CostEstimate(
-            flops=6 * PANEL_ROWS * COL_WIDTH * LEAD,
-            bytes_accessed=26 * 2**20,
+            flops=9 * PANEL_ROWS * COL_WIDTH * LEAD,
+            bytes_accessed=30 * 2**20,
             transcendentals=0,
         ),
-        name="schur",
-    )(row_places, col_places, front, panel, top, tiles)
+        name="finish",
+    )(row_places, col_places, front, pan, top, upper, side, full, low, tiles)
 
 
 def per_device(parent_front, child_panels, child_inverses, parent_index):
     here_row = lax.axis_index("row")
     here_col = lax.axis_index("col")
     own_factor = product_rows(child_panels[0], child_inverses[0])
-    factors, top, lead = gather_all(own_factor, parent_front)
-
     block_of = parent_index // PCT
     my_blocks = lax.dynamic_index_in_dim(block_of, here_row, 0, keepdims=False)
     ids = jnp.arange(COLS, dtype=jnp.int32)
     wanted = jnp.concatenate([ids, here_col[None].astype(jnp.int32)])
     order = jnp.sum(jnp.where(my_blocks[None, :] == wanted[:, None], ids[None, :], 0), axis=1)
-    outgoing = update_tiles(order, factors).reshape(ROWS, 2, TILE, TILE)
-    outgoing, top, lead = lax.optimization_barrier((outgoing, top, lead))
+    outgoing, top = gather_tiles(order, own_factor, parent_front)
+    outgoing = outgoing.reshape(ROWS, 2, TILE, TILE)
     tiles = lax.all_to_all(outgoing, "row", split_axis=0, concat_axis=0, tiled=True)
 
     row_blocks = 2 * here_row + jnp.arange(2, dtype=jnp.int32)
@@ -761,14 +716,20 @@
         jnp.sum(jnp.where(block_of == here_col, parent_index, 0), axis=1) - here_col * PCT
     )
 
-    panel, upper, side, full, low = spread_panel(top, lead)
-    panel_out, top_out = factor_panel(panel, top, upper, side, full, low)
-    schur = schur_update(
-        row_places.astype(jnp.int32),
-        col_places.astype(jnp.int32),
+    top, row_places, col_places = lax.optimization_barrier(
+        (top, row_places.astype(jnp.int32), col_places.astype(jnp.int32))
+    )
+    pan, upper, side, full, low = spread_panel(top)
+    panel_out, schur = finish(
+        row_places,
+        col_places,
         parent_front,
-        panel_out,
-        top_out,
+        pan,
+        top,
+        upper,
+        side,
+        full,
+        low,
         tiles,
     )
     return (panel_out, schur)

time: 188 us -> 180 us (0.957)
  Pallas kernels: 170 us -> 163 us
  local copies, waits for them, and re-layouts: 3.61 us -> 6.14 us
  starting transfers between devices: 6.63 us -> 4.56 us
    pallas_call x4 -> x2, Pallas kernels: 118 us -> 86.9 us  [the longest x1 61.6 us: gather_tiles(): pl.pallas_call(gather_kernel, out_shape=(jax.ShapeDtypeStruct((COLS, TILE...]
    pallas_call x1, Pallas kernels: 52.6 us -> 76.3 us  [spread_panel(): pl.pallas_call(spread_kernel, out_shape=(jax.ShapeDtypeStruct((2, LEAD, C...]
    unnamed x12 -> x16, local copies, waits for them, and re-layouts: 3.52 us -> 6.04 us
    all_to_all x1, starting transfers between devices: 6.63 us -> 4.56 us  [per_device(): lax.all_to_all(outgoing, 'row', split_axis=0, concat_axis=0, tiled=True)]
  transfers between devices with their start and end apart: 1 -> 1, of which waited for: 0 -> 0; matrix products, arithmetic and copies ran while one was open for 1% -> 0% of each run, Pallas kernels for 36% -> 43%
where the time goes in v7:
time: 180 us; the launch traced here: 179 us
  Pallas kernels  163 us (91%)
  local copies, waits for them, and re-layouts  6.14 us (3%)
  starting transfers between devices  4.56 us (3%)
  matrix products  2.89 us (2%)
  other arithmetic  1.8 us (1%)
    pallas_call x1, Pallas kernels, spread_panel(): pl.pallas_call(spread_kernel, out_shape=(jax.ShapeDtypeStruct((2, LEAD, C...  76.3 us
    pallas_call x1, Pallas kernels, gather_tiles(): pl.pallas_call(gather_kernel, out_shape=(jax.ShapeDtypeStruct((COLS, TILE...  61.6 us
    pallas_call x1, Pallas kernels, finish(): pl.pallas_call(final_kernel, out_shape=(jax.ShapeDtypeStruct((PANEL_ROWS,...  25.3 us
    unnamed x16, local copies, waits for them, and re-layouts  6.04 us
    all_to_all x1, starting transfers between devices, per_device(): lax.all_to_all(outgoing, 'row', split_axis=0, concat_axis=0, tiled=True)  4.56 us
  transfers between devices with their start and end apart: 1, of which 0 were waited for; matrix products, arithmetic and copies ran while one was open for 0% of the time, Pallas kernels for 43%

profile of v7, /device:TPU:0, one launch (start us, length us, event | category | flops | bytes accessed | tf_op | source)
XLA Modules:
  0.0 179.3 jit_solution(14179762683429454760)
XLA Ops:
  0.6 0.0 copy-start
  0.7 0.9 select_reduce_fusion.2
  1.5 0.1 pad_add_fusion
  1.6 0.6 select_reduce_fusion.1.order_ref
  2.2 0.0 copy-done
  2.2 2.9 %fusion.own_ref = f32[256,512]{1,0:T(8,128)} fusion(f32[1,512,512]{2,1,0:T(8,128)S(1)} %copy-done, f32[1,256,512]{2,1,0:T(8,128)} %param.5), kind=kOutput, calls=%fused_computation | convolution fusion | flops 805306368 | bytes 2097152 | tf_op jit(solution)/shard_map/dot_general | solution.py:33
  5.1 61.6 %gather.1 = (f32[16,256,256]{2,1,0:T(8,128)}, f32[512,1024]{1,0:T(8,128)}) custom-call(s32[17]{0:T(128)} %select_reduce_fusion.1.order_ref, f32[256,512]{1,0:T(8,128)} %fusion.own_ref, f32[2048,1024]{1,0:T(8,128)} %front_ref.3), custom_call_target="tpu_custom_call" | custom-call | tf_op jit(solution)/shard_map/gather/pallas_call | solution.py:477
  66.7 0.0 copy-start.7
  66.7 4.6 %all-to-all-start = ((f32[8,2,256,256]{3,2,1,0:T(8,128)}), f32[8,2,256,256]{3,2,1,0:T(8,128)}, u32[]{:S(2)}, u32[]{:S(2)}) async-start(f32[8,2,256,256]{3,2,1,0:T(8,128)} %bitcast.10), calls=%async_computation | async-start | bytes 8388608 | tf_op jit(solution)/shard_map/all_to_all | solution.py:703
  71.3 0.0 copy-done.7
  71.3 0.2 select_reduce_fusion
  71.5 0.1 copy.6
  71.6 0.0 copy-start.1
  71.6 76.3 %spread.1 = (f32[2,512,1024]{2,1,0:T(8,128)}, f32[4,128,128]{2,1,0:T(8,128)}, f32[2,128,128]{2,1,0:T(8,128)}, f32[2,256,256]{2,1,0:T(8,128)}, f32[256,256]{1,0:T(8,128)}) custom-call(f32[512,1024]{1,0:T(8,128)} %get-tuple-element.15.top_ref), custom_call_target="tpu_custom_call" | custom-call | flops 30000001024 | bytes 20971520 | tf_op jit(solution)/shard_map/spread/pallas_call | solution.py:502
  148.0 0.0 all-to-all-done.tiles_ref
  148.0 0.0 copy-done.1
  148.0 0.0 copy-start.2
  148.0 2.2 %copy-done.2 = f32[2,512,1024]{2,1,0:T(8,128)S(1)} copy-done((f32[2,512,1024]{2,1,0:T(8,128)S(1)}, f32[2,512,1024]{2,1,0:T(8,128)}, u32[]{:S(2)}) %copy-start.2) | copy-done | bytes 4194328
  150.2 0.0 copy-start.3
  150.2 1.0 copy-done.3
  151.2 0.0 copy-start.4
  151.2 0.9 copy-done.4
  152.2 0.0 copy-start.5
  152.2 0.9 copy-done.5
  153.1 0.0 copy-start.6
  153.1 0.9 copy-done.6
  154.0 25.3 %finish.1 = (f32[2048,512]{1,0:T(8,128)}, f32[2048,1024]{1,0:T(8,128)}) custom-call(s32[8,2]{1,0:T(8,128)S(1)} %broadcast_subtract_fusion.rows_ref, s32[8]{0:T(128)S(1)} %broadcast_subtract_fusion.1.cols_ref, f32[2048,1024]{1,0:T(8,128)} %front_ref.3, f32[2,512,1024]{2,1,0:T(8,128)S(1)} %copy-done.2, f32[512,1024]{1,0:T(8,128)S(1)} %copy-done.1, ...), custom_call_target="tpu_custom_call" | custom-call | flops 9663676416 | bytes 31457280 | tf_op jit(solution)/shard_map/finish/pallas_call | solution.py:653
  (5 shorter events, 0.0 us)
Async XLA Ops:
  0.6 1.6 copy-start
  66.7 4.6 %copy-start.7 = (s32[8,16]{1,0:T(8,128)S(1)}, s32[8,16]{1,0:T(8,128)}, u32[]{:S(2)}) copy-start(s32[8,16]{1,0:T(8,128)} %param.7) | copy-start | bytes 1540
  66.7 81.2 %all-to-all-start = ((f32[8,2,256,256]{3,2,1,0:T(8,128)}), f32[8,2,256,256]{3,2,1,0:T(8,128)}, u32[]{:S(2)}, u32[]{:S(2)}) async-start(f32[8,2,256,256]{3,2,1,0:T(8,128)} %bitcast.10), calls=%async_computation | async-start | bytes 8388608 | tf_op jit(solution)/shard_map/all_to_all | solution.py:703
  71.6 76.3 %copy-start.1 = (f32[512,1024]{1,0:T(8,128)S(1)}, f32[512,1024]{1,0:T(8,128)}, u32[]{:S(2)}) copy-start(f32[512,1024]{1,0:T(8,128)} %get-tuple-element.15.top_ref) | copy-start | bytes 6291460
  148.0 2.2 %copy-start.2 = (f32[2,512,1024]{2,1,0:T(8,128)S(1)}, f32[2,512,1024]{2,1,0:T(8,128)}, u32[]{:S(2)}) copy-start(f32[2,512,1024]{2,1,0:T(8,128)} %get-tuple-element.16.pan_ref) | copy-start | bytes 12582916
  150.2 1.0 copy-start.3
  151.2 0.9 copy-start.4
  152.2 0.9 copy-start.5
  153.1 0.9 copy-start.6

commit v8 on v7

--- a/solution.py
+++ b/solution.py
@@ -177,7 +177,7 @@
 
 
 def gather_kernel(
-    order_ref, own_ref, front_ref, tiles_ref, top_ref,
+    order_ref, own_ref, front_ref, tiles_ref, top_ref, piece_ref, lead_ref,
     all_ref, high_ref, low_ref, send_sem, recv_sem, local_sem,
 ):
     wires = Wires(send_sem, recv_sem)
@@ -192,7 +192,7 @@
     keep_own = pltpu.make_async_copy(own_ref, all_ref.at[col], local_sem.at[1])
     keep_own.start()
     wires.greet(
-        [(row, wires.at(*step)) for step in ((1, 0), (-1, 0), (0, 1), (0, -1))]
+        wires.col_others()
         + [
             (row + 1 - 2 * core, col),
             (lax.rem(row + 2, ROWS), col),
@@ -254,6 +254,54 @@
             def _():
                 side.wait_send()
 
+    spread = [
+        (0, pl.ds(0, LEAD), lead_ref),
+        (2 * row, pl.ds(0, COL_WIDTH), piece_ref.at[0]),
+        (2 * row + 1, pl.ds(0, COL_WIDTH), piece_ref.at[1]),
+    ]
+    spread_recv = fresh(len(spread))
+    spread_send = fresh(len(spread) * COLS)
+
+    def spread_copy(index, step):
+        _, lanes, target = spread[index]
+        to_col = lax.rem(col + step, COLS)
+        return remote(
+            top_ref.at[pl.ds(to_col * SLICE, SLICE), lanes],
+            target,
+            spread_send + index * COLS + step,
+            spread_recv + index,
+            row,
+            to_col,
+        )
+
+    def spread_start(index):
+        holder, lanes, target = spread[index]
+
+        @pl.when(col == holder)
+        def _():
+            keep = pltpu.make_async_copy(
+                top_ref.at[pl.ds(col * SLICE, SLICE), lanes], target, local_sem.at[2 + index]
+            )
+            keep.start()
+
+            @pl.loop(1, COLS)
+            def _(step):
+                spread_copy(index, step).start()
+
+            keep.wait()
+
+    def spread_wait(index):
+        @pl.when(col != spread[index][0])
+        def _():
+            spread_copy(index, 1).wait_recv()
+
+    def spread_drain(index):
+        @pl.when(col == spread[index][0])
+        def _():
+            @pl.loop(1, COLS)
+            def _(step):
+                spread_copy(index, step).wait_send()
+
     rings = [
         wires.ring(h, factor_piece, lambda h=h: own_ref.at[pl.ds(h * 128, 128)]) for h in range(2)
     ]
@@ -271,6 +319,8 @@
             run()
     for run in steps[4 + 2 * (half_pieces + SIDE) :]:
         run()
+    for index in range(len(spread)):
+        spread_start(index)
     keep_own.wait()
     high_ref[...], low_ref[...] = halves(all_ref[order_ref[COLS]])
 
@@ -282,6 +332,9 @@
     wires.drain()
     for number in range(half_pieces):
         top_drain(number)
+    for index in range(len(spread)):
+        spread_wait(index)
+        spread_drain(index)
 
 
 BLOCK = 128
@@ -292,82 +345,26 @@
 
 
 def spread_kernel(
-    top_ref, pan_ref, upper_ref, side_ref, full_ref, low_ref,
+    piece_ref, corner_ref, pan_ref, upper_ref, side_ref, full_ref, low_ref,
     block_ref, inv_ref, work_ref, lead_ref, send_sem, recv_sem, local_sem,
 ):
     wires = Wires(send_sem, recv_sem)
     row, col = wires.row, wires.col
-    fresh, remote = wires.fresh, wires.remote
-    wires.greet(wires.col_others())
+    mine = pl.ds(col * SLICE, SLICE)
+    keeps = [
+        pltpu.make_async_copy(corner_ref, lead_ref.at[mine], local_sem.at[0]),
+        pltpu.make_async_copy(piece_ref.at[0], pan_ref.at[0, mine], local_sem.at[1]),
+        pltpu.make_async_copy(piece_ref.at[1], pan_ref.at[1, mine], local_sem.at[2]),
+    ]
+    for keep in keeps:
+        keep.start()
+    wires.greet([(row, wires.at(*step)) for step in ((1, 0), (-1, 0), (0, 1), (0, -1))])
 
     def panel_piece(slot, half, part):
         if part == 0:
             return pan_ref.at[half, pl.ds(slot * SLICE, SLICE)]
         size = SLICE // 2
         return pan_ref.at[half, pl.ds(slot * SLICE + size * (part - 1), size)]
-
-    spread = []
-    for half in range(2):
-        spread.append((half, 2 * row + half, pl.ds(0, COL_WIDTH), pl.ds(0, COL_WIDTH)))
-    spread_recv = [fresh() for _ in spread]
-    spread_send = [fresh(COLS) for _ in spread]
-
-    def spread_copy(index, step):
-        half, _, lanes, to_lanes = spread[index]
-        to_col = lax.rem(col + step, COLS)
-        rows = pl.ds(to_col * SLICE, SLICE)
-        return remote(
-            top_ref.at[rows, lanes],
-            pan_ref.at[half, rows, to_lanes],
-            spread_send[index] + step,
-            spread_recv[index],
-            row,
-            to_col,
-        )
-
-    def spread_start(index):
-        half, holder, lanes, to_lanes = spread[index]
-        rows = pl.ds(col * SLICE, SLICE)
-
-        @pl.when(col == holder)
-        def _():
-            keep = pltpu.make_async_copy(
-                top_ref.at[rows, lanes], pan_ref.at[half, rows, to_lanes], local_sem.at[index]
-            )
-            keep.start()
-
-            @pl.loop(1, COLS)
-            def _(step):
-                spread_copy(index, step).start()
-
-            keep.wait()
-
-    def spread_wait(index):
-        @pl.when(col != spread[index][1])
-        def _():
-            spread_copy(index, 1).wait_recv()
-
-    def spread_drain(index):
-        @pl.when(col == spread[index][1])
-        def _():
-            @pl.loop(1, COLS)
-            def _(step):
-                spread_copy(index, step).wait_send()
-
-    lead_recv = fresh()
-    lead_send = fresh(COLS)
-
-    def lead_copy(step):
-        to_col = lax.rem(col + step, COLS)
-        rows = pl.ds(to_col * SLICE, SLICE)
-        return remote(
-            top_ref.at[rows, pl.ds(0, LEAD)],
-            lead_ref.at[rows],
-            lead_send + step,
-            lead_recv,
-            row,
-            to_col,
-        )
 
     def lead_piece(slot, half, part):
         size = SLICE // 2
@@ -376,39 +373,20 @@
         base = slot * SLICE + half * size + (size // 2) * (part - 1)
         return lead_ref.at[pl.ds(base, size // 2)]
 
-    def lead_start():
-        @pl.when(col == 0)
-        def _():
-            keep = pltpu.make_async_copy(
-                top_ref.at[pl.ds(0, SLICE), pl.ds(0, LEAD)],
-                lead_ref.at[pl.ds(0, SLICE)],
-                local_sem.at[2],
-            )
-            keep.start()
-
-            @pl.loop(1, COLS)
-            def _(step):
-                lead_copy(step).start()
-
-            keep.wait()
-
-    def lead_wait():
-        @pl.when(col != 0)
-        def _():
-            lead_copy(1).wait_recv()
-
-    lead_start()
-    for number in range(2):
-        spread_start(number)
-    lead_rings = [
-        wires.ring(h, lead_piece, lambda h=h: lead_piece(col, h, 0)) for h in range(2)
-    ]
+    size = SLICE // 2
+    lead_steps = ring_steps(
+        [
+            wires.ring(h, lead_piece, lambda h=h: corner_ref.at[pl.ds(h * size, size)])
+            for h in range(2)
+        ]
+    )
     steps = ring_steps(
-        [wires.ring(h, panel_piece, lambda h=h: panel_piece(col, h, 0)) for h in range(2)]
-    )
-    lead_wait()
-    for run in ring_steps(lead_rings):
+        [wires.ring(h, panel_piece, lambda h=h: piece_ref.at[h]) for h in range(2)]
+    )
+    for run in lead_steps[:-8] + steps[:2] + lead_steps[-8:] + steps[2:4]:
         run()
+    for keep in keeps:
+        keep.wait()
 
     def join_inverse(tile):
         first, second, side = inv_ref[2 * tile], inv_ref[2 * tile + 1], side_ref[tile]
@@ -425,10 +403,6 @@
     def body(number, carry):
         @pl.when(number == 0)
         def _():
-            for index in range(2):
-                spread_wait(index)
-            for run in steps[:4]:
-                run()
             block_ref[...] = lead_ref[NEAR, NEAR]
 
         @pl.when(number == 1)
@@ -461,14 +435,6 @@
     for run in steps[16:]:
         run()
     wires.drain()
-    for number in range(2):
-        spread_drain(number)
-
-    @pl.when(col == 0)
-    def _():
-        @pl.loop(1, COLS)
-        def _(step):
-            lead_copy(step).wait_send()
 
 
 def gather_tiles(order, own_factor, front):
@@ -479,16 +445,18 @@
         out_shape=(
             jax.ShapeDtypeStruct((COLS, TILE, TILE), F32),
             jax.ShapeDtypeStruct((LEAD, COL_WIDTH), F32),
+            jax.ShapeDtypeStruct((2, SLICE, COL_WIDTH), F32),
+            jax.ShapeDtypeStruct((SLICE, LEAD), F32),
         ),
         in_specs=[pl.BlockSpec(memory_space=pltpu.SMEM), vmem, anywhere],
-        out_specs=(vmem, vmem),
+        out_specs=(vmem,) * 4,
         scratch_shapes=[
             pltpu.VMEM((COLS, TILE, CW), F32),
             pltpu.VMEM((TILE, CW), BF16),
             pltpu.VMEM((TILE, CW), BF16),
-            pltpu.SemaphoreType.DMA((72,)),
-            pltpu.SemaphoreType.DMA((72,)),
-            pltpu.SemaphoreType.DMA((2,)),
+            pltpu.SemaphoreType.DMA((120,)),
+            pltpu.SemaphoreType.DMA((120,)),
+            pltpu.SemaphoreType.DMA((5,)),
         ],
         compiler_params=pltpu.CompilerParams(
             collective_id=0, has_side_effects=True, vmem_limit_bytes=56 * 2**20
@@ -497,7 +465,7 @@
     )(order, own_factor, front)
 
 
-def spread_panel(top):
+def spread_panel(piece, corner):
     vmem = pl.BlockSpec(memory_space=pltpu.VMEM)
     return pl.pallas_call(
         spread_kernel,
@@ -508,15 +476,15 @@
             jax.ShapeDtypeStruct((2, TILE, TILE), F32),
             jax.ShapeDtypeStruct((TILE, TILE), F32),
         ),
-        in_specs=[vmem],
+        in_specs=[vmem, vmem],
         out_specs=(vmem,) * 5,
         scratch_shapes=[
             pltpu.VMEM((BLOCK, BLOCK), F32),
             pltpu.VMEM((4, BLOCK, BLOCK), F32),
             pltpu.VMEM((TILE, TILE), F32),
             pltpu.VMEM((LEAD, LEAD), F32),
-            pltpu.SemaphoreType.DMA((136,)),
-            pltpu.SemaphoreType.DMA((136,)),
+            pltpu.SemaphoreType.DMA((80,)),
+            pltpu.SemaphoreType.DMA((80,)),
             pltpu.SemaphoreType.DMA((3,)),
         ],
         compiler_params=pltpu.CompilerParams(
@@ -526,7 +494,7 @@
             flops=30 * 10**9, bytes_accessed=20 * 2**20, transcendentals=0
         ),
         name="spread",
-    )(top)
+    )(piece, corner)
 
 
 def eliminate(block_ref, upper_ref, inverse_ref):
@@ -679,7 +647,7 @@
                 pltpu.VMEM((LEAD, COL_WIDTH), BF16),
             ],
         ),
-        compiler_params=pltpu.CompilerParams(vmem_limit_bytes=40 * 2**20),
+        compiler_params=pltpu.CompilerParams(vmem_limit_bytes=58 * 2**20),
         cost_estimate=pl.CostEstimate(
             flops=9 * PANEL_ROWS * COL_WIDTH * LEAD,
             bytes_accessed=30 * 2**20,
@@ -698,7 +666,7 @@
     ids = jnp.arange(COLS, dtype=jnp.int32)
     wanted = jnp.concatenate([ids, here_col[None].astype(jnp.int32)])
     order = jnp.sum(jnp.where(my_blocks[None, :] == wanted[:, None], ids[None, :], 0), axis=1)
-    outgoing, top = gather_tiles(order, own_factor, parent_front)
+    outgoing, top, piece, corner = gather_tiles(order, own_factor, parent_front)
     outgoing = outgoing.reshape(ROWS, 2, TILE, TILE)
     tiles = lax.all_to_all(outgoing, "row", split_axis=0, concat_axis=0, tiled=True)
 
@@ -716,10 +684,10 @@
         jnp.sum(jnp.where(block_of == here_col, parent_index, 0), axis=1) - here_col * PCT
     )
 
-    top, row_places, col_places = lax.optimization_barrier(
-        (top, row_places.astype(jnp.int32), col_places.astype(jnp.int32))
-    )
-    pan, upper, side, full, low = spread_panel(top)
+    piece, corner, row_places, col_places = lax.optimization_barrier(
+        (piece, corner, row_places.astype(jnp.int32), col_places.astype(jnp.int32))
+    )
+    pan, upper, side, full, low = spread_panel(piece, corner)
     panel_out, schur = finish(
         row_places,
         col_places,

time: 180 us -> 169 us (0.939)
  local copies, waits for them, and re-layouts: 6.14 us -> 0.11 us
  Pallas kernels: 163 us -> 158 us
    pallas_call x1, Pallas kernels: 76.3 us -> 52.7 us  [spread_panel(): pl.pallas_call(spread_kernel, out_shape=(jax.ShapeDtypeStruct((2, LEAD, C...]
    pallas_call x1, Pallas kernels: 61.6 us -> 78.3 us  [gather_tiles(): pl.pallas_call(gather_kernel, out_shape=(jax.ShapeDtypeStruct((COLS, TILE...]
    unnamed x16 -> x4, local copies, waits for them, and re-layouts: 6.04 us -> 0.02 us
  transfers between devices with their start and end apart: 1 -> 1, of which waited for: 0 -> 0; matrix products, arithmetic and copies ran while one was open for 0% -> 1% of each run, Pallas kernels for 43% -> 31%
where the time goes in v8:
time: 169 us
  Pallas kernels  158 us (93%)
  starting transfers between devices  4.74 us (3%)
  other arithmetic  3.04 us (2%)
  matrix products  2.89 us (2%)
    pallas_call x1, Pallas kernels, gather_tiles(): pl.pallas_call(gather_kernel, out_shape=(jax.ShapeDtypeStruct((COLS, TILE...  78.3 us
    pallas_call x1, Pallas kernels, spread_panel(): pl.pallas_call(spread_kernel, out_shape=(jax.ShapeDtypeStruct((2, LEAD, C...  52.7 us
    pallas_call x1, Pallas kernels, finish(): pl.pallas_call(final_kernel, out_shape=(jax.ShapeDtypeStruct((PANEL_ROWS,...  26.6 us
    all_to_all x1, starting transfers between devices, per_device(): lax.all_to_all(outgoing, 'row', split_axis=0, concat_axis=0, tiled=True)  4.74 us
  transfers between devices with their start and end apart: 1, of which 0 were waited for; matrix products, arithmetic and copies ran while one was open for 1% of the time, Pallas kernels for 31%

profile of v8, /device:TPU:0, one launch (start us, length us, event | category | flops | bytes accessed | tf_op | source)
XLA Modules:
  0.0 169.1 jit_solution(6578263969586381992)
XLA Ops:
  0.6 0.0 copy-start
  0.7 0.9 select_reduce_fusion.2
  1.5 0.1 pad_add_fusion
  1.6 0.7 select_reduce_fusion.1.order_ref
  2.3 0.0 copy-done
  2.3 2.9 %fusion.own_ref = f32[256,512]{1,0:T(8,128)} fusion(f32[1,512,512]{2,1,0:T(8,128)S(1)} %copy-done, f32[1,256,512]{2,1,0:T(8,128)} %param.5), kind=kOutput, calls=%fused_computation | convolution fusion | flops 805306368 | bytes 2097152 | tf_op jit(solution)/shard_map/dot_general | solution.py:33
  5.2 78.3 %gather.1 = (f32[16,256,256]{2,1,0:T(8,128)}, f32[512,1024]{1,0:T(8,128)}, f32[2,32,1024]{2,1,0:T(8,128)}, f32[32,512]{1,0:T(8,128)}) custom-call(s32[17]{0:T(128)} %select_reduce_fusion.1.order_ref, f32[256,512]{1,0:T(8,128)} %fusion.own_ref, f32[2048,1024]{1,0:T(8,128)} %front_ref.3), custom_call_target="tpu_custom_call" | custom-call | tf_op jit(solution)/shard_map/gather/pallas_call | solution.py:443
  83.5 0.0 copy-start.1
  83.5 4.7 %all-to-all-start = ((f32[8,2,256,256]{3,2,1,0:T(8,128)}), f32[8,2,256,256]{3,2,1,0:T(8,128)}, u32[]{:S(2)}, u32[]{:S(2)}) async-start(f32[8,2,256,256]{3,2,1,0:T(8,128)} %bitcast.10), calls=%async_computation | async-start | bytes 8388608 | tf_op jit(solution)/shard_map/all_to_all | solution.py:671
  88.3 0.0 copy-done.1
  88.3 0.2 select_reduce_fusion
  88.5 0.1 copy.6
  88.6 0.6 broadcast_subtract_fusion.1.cols_ref
  89.2 0.6 broadcast_subtract_fusion.rows_ref
  89.8 52.7 %spread.1 = (f32[2,512,1024]{2,1,0:T(8,128)}, f32[4,128,128]{2,1,0:T(8,128)}, f32[2,128,128]{2,1,0:T(8,128)}, f32[2,256,256]{2,1,0:T(8,128)}, f32[256,256]{1,0:T(8,128)}) custom-call(f32[2,32,1024]{2,1,0:T(8,128)} %get-tuple-element.19.piece_ref, f32[32,512]{1,0:T(8,128)} %get-tuple-element.20.corner_ref), custom_call_target="tpu_custom_call" | custom-call | flops 30000001024 | bytes 20971520 | tf_op jit(solution)/shard_map/spread/pallas_call | solution.py:470
  142.5 0.0 all-to-all-done.tiles_ref
  142.5 26.6 %finish.1 = (f32[2048,512]{1,0:T(8,128)}, f32[2048,1024]{1,0:T(8,128)}) custom-call(s32[8,2]{1,0:T(8,128)} %broadcast_subtract_fusion.rows_ref, s32[8]{0:T(128)} %broadcast_subtract_fusion.1.cols_ref, f32[2048,1024]{1,0:T(8,128)} %front_ref.3, f32[2,512,1024]{2,1,0:T(8,128)} %get-tuple-element.21.pan_ref, f32[512,1024]{1,0:T(8,128)} %get-tuple-element.22.top_ref, ...), custom_call_target="tpu_custom_call" | custom-call | flops 9663676416 | bytes 31457280 | tf_op jit(solution)/shard_map/finish/pallas_call | solution.py:621
  (3 shorter events, 0.0 us)
Async XLA Ops:
  0.6 1.7 copy-start
  83.5 4.8 %copy-start.1 = (s32[8,16]{1,0:T(8,128)S(1)}, s32[8,16]{1,0:T(8,128)}, u32[]{:S(2)}) copy-start(s32[8,16]{1,0:T(8,128)} %param.7) | copy-start | bytes 1540
  83.5 59.0 %all-to-all-start = ((f32[8,2,256,256]{3,2,1,0:T(8,128)}), f32[8,2,256,256]{3,2,1,0:T(8,128)}, u32[]{:S(2)}, u32[]{:S(2)}) async-start(f32[8,2,256,256]{3,2,1,0:T(8,128)} %bitcast.10), calls=%async_computation | async-start | bytes 8388608 | tf_op jit(solution)/shard_map/all_to_all | solution.py:671

commit v9 on v7

--- a/solution.py
+++ b/solution.py
@@ -177,8 +177,8 @@
 
 
 def gather_kernel(
-    order_ref, own_ref, front_ref, tiles_ref, top_ref,
-    all_ref, high_ref, low_ref, send_sem, recv_sem, local_sem,
+    order_ref, own_ref, front_ref, tiles_ref, top_ref, lead_ref,
+    all_ref, high_ref, low_ref, corner_ref, send_sem, recv_sem, local_sem,
 ):
     wires = Wires(send_sem, recv_sem)
     row, col, chip, core = wires.row, wires.col, wires.chip, wires.core
@@ -192,11 +192,9 @@
     keep_own = pltpu.make_async_copy(own_ref, all_ref.at[col], local_sem.at[1])
     keep_own.start()
     wires.greet(
-        [(row, wires.at(*step)) for step in ((1, 0), (-1, 0), (0, 1), (0, -1))]
+        wires.col_others()
         + [
-            (row + 1 - 2 * core, col),
-            (lax.rem(row + 2, ROWS), col),
-            (lax.rem(row + 6, ROWS), col),
+            (lax.rem(row + k, ROWS), col) for k in range(1, ROWS)
         ]
     )
 
@@ -254,10 +252,80 @@
             def _():
                 side.wait_send()
 
+    corner_recv = fresh()
+    along = fresh(COLS)
+    down = fresh(ROWS)
+    load_corner = pltpu.make_async_copy(
+        front_ref.at[pl.ds(0, SLICE), pl.ds(0, LEAD)], corner_ref, local_sem.at[2]
+    )
+
+    def along_copy(step):
+        return remote(
+            front_ref.at[pl.ds(step * SLICE, SLICE), pl.ds(0, LEAD)],
+            corner_ref,
+            along + step,
+            corner_recv,
+            row,
+            step,
+        )
+
+    def down_copy(step):
+        return remote(corner_ref, corner_ref, down + step, corner_recv, step, col)
+
+    def each_along(act):
+        @pl.when((row == 0) & (col == 0))
+        def _():
+            @pl.loop(1, COLS)
+            def _(step):
+                act(along_copy(step))
+
+    def each_down(act):
+        @pl.when(row == 0)
+        def _():
+            @pl.loop(1, ROWS)
+            def _(step):
+                act(down_copy(step))
+
+    def corner_start():
+        each_along(lambda copy: copy.start())
+
+        @pl.when((row == 0) & (col == 0))
+        def _():
+            load_corner.start()
+
+    def corner_pass():
+        @pl.when((row == 0) & (col == 0))
+        def _():
+            load_corner.wait()
+
+        @pl.when((row == 0) & (col != 0))
+        def _():
+            down_copy(1).wait_recv()
+
+        each_down(lambda copy: copy.start())
+
+    def corner_wait():
+        @pl.when(row != 0)
+        def _():
+            down_copy(1).wait_recv()
+
+    def lead_piece(slot, half, part):
+        size = SLICE // 2
+        if part == 0:
+            return lead_ref.at[pl.ds(slot * SLICE + half * size, size)]
+        base = slot * SLICE + half * size + (size // 2) * (part - 1)
+        return lead_ref.at[pl.ds(base, size // 2)]
+
     rings = [
         wires.ring(h, factor_piece, lambda h=h: own_ref.at[pl.ds(h * 128, 128)]) for h in range(2)
     ]
+    size = SLICE // 2
+    lead_rings = [
+        wires.ring(h, lead_piece, lambda h=h: corner_ref.at[pl.ds(h * size, size)])
+        for h in range(2)
+    ]
     steps = ring_steps(rings)
+    corner_start()
     for run in steps[:4]:
         run()
 
@@ -267,21 +335,37 @@
 
     for number in range(half_pieces + SIDE):
         top_step(number)
+        if number == 2:
+            corner_pass()
         for run in steps[4 + 2 * number : 6 + 2 * number]:
             run()
     for run in steps[4 + 2 * (half_pieces + SIDE) :]:
         run()
+    corner_wait()
+    keep_corner = pltpu.make_async_copy(
+        corner_ref, lead_ref.at[pl.ds(col * SLICE, SLICE)], local_sem.at[3]
+    )
+    keep_corner.start()
     keep_own.wait()
+    lead_steps = ring_steps(lead_rings)
+    for run in lead_steps[:4]:
+        run()
     high_ref[...], low_ref[...] = halves(all_ref[order_ref[COLS]])
 
-    @pl.loop(0, COLS)
-    def _(number):
+    def tile(number):
         left = halves(all_ref[order_ref[number]])
         tiles_ref[number] = three_pass(left, (high_ref[...], low_ref[...]), ((1,), (1,)))
 
+    for part in range(COLS // 2):
+        pl.loop(2 * part, 2 * part + 2)(tile)
+        for run in lead_steps[4 + 4 * part : 8 + 4 * part]:
+            run()
+    keep_corner.wait()
     wires.drain()
     for number in range(half_pieces):
         top_drain(number)
+    each_along(lambda copy: copy.wait_send())
+    each_down(lambda copy: copy.wait_send())
 
 
 BLOCK = 128
@@ -292,8 +376,8 @@
 
 
 def spread_kernel(
-    top_ref, pan_ref, upper_ref, side_ref, full_ref, low_ref,
-    block_ref, inv_ref, work_ref, lead_ref, send_sem, recv_sem, local_sem,
+    top_ref, lead_ref, pan_ref, upper_ref, side_ref, full_ref, low_ref,
+    block_ref, inv_ref, work_ref, send_sem, recv_sem, local_sem,
 ):
     wires = Wires(send_sem, recv_sem)
     row, col = wires.row, wires.col
@@ -354,61 +438,11 @@
             def _(step):
                 spread_copy(index, step).wait_send()
 
-    lead_recv = fresh()
-    lead_send = fresh(COLS)
-
-    def lead_copy(step):
-        to_col = lax.rem(col + step, COLS)
-        rows = pl.ds(to_col * SLICE, SLICE)
-        return remote(
-            top_ref.at[rows, pl.ds(0, LEAD)],
-            lead_ref.at[rows],
-            lead_send + step,
-            lead_recv,
-            row,
-            to_col,
-        )
-
-    def lead_piece(slot, half, part):
-        size = SLICE // 2
-        if part == 0:
-            return lead_ref.at[pl.ds(slot * SLICE + half * size, size)]
-        base = slot * SLICE + half * size + (size // 2) * (part - 1)
-        return lead_ref.at[pl.ds(base, size // 2)]
-
-    def lead_start():
-        @pl.when(col == 0)
-        def _():
-            keep = pltpu.make_async_copy(
-                top_ref.at[pl.ds(0, SLICE), pl.ds(0, LEAD)],
-                lead_ref.at[pl.ds(0, SLICE)],
-                local_sem.at[2],
-            )
-            keep.start()
-
-            @pl.loop(1, COLS)
-            def _(step):
-                lead_copy(step).start()
-
-            keep.wait()
-
-    def lead_wait():
-        @pl.when(col != 0)
-        def _():
-            lead_copy(1).wait_recv()
-
-    lead_start()
-    for number in range(2):
-        spread_start(number)
-    lead_rings = [
-        wires.ring(h, lead_piece, lambda h=h: lead_piece(col, h, 0)) for h in range(2)
-    ]
+    for index in range(2):
+        spread_start(index)
     steps = ring_steps(
         [wires.ring(h, panel_piece, lambda h=h: panel_piece(col, h, 0)) for h in range(2)]
     )
-    lead_wait()
-    for run in ring_steps(lead_rings):
-        run()
 
     def join_inverse(tile):
         first, second, side = inv_ref[2 * tile], inv_ref[2 * tile + 1], side_ref[tile]
@@ -425,21 +459,17 @@
     def body(number, carry):
         @pl.when(number == 0)
         def _():
+            block_ref[...] = lead_ref[NEAR, NEAR]
+
+        @pl.when(number == 1)
+        def _():
+            second_half(0, lead_ref[AWAY, NEAR], lead_ref[AWAY, AWAY])
+
+        @pl.when(number == 2)
+        def _():
             for index in range(2):
                 spread_wait(index)
             for run in steps[:4]:
-                run()
-            block_ref[...] = lead_ref[NEAR, NEAR]
-
-        @pl.when(number == 1)
-        def _():
-            for run in steps[4:8]:
-                run()
-            second_half(0, lead_ref[AWAY, NEAR], lead_ref[AWAY, AWAY])
-
-        @pl.when(number == 2)
-        def _():
-            for run in steps[8:12]:
                 run()
             join_inverse(0)
             low = product_rows(lead_ref[TILE:, :TILE], full_ref[0])
@@ -449,7 +479,7 @@
 
         @pl.when(number == 3)
         def _():
-            for run in steps[12:16]:
+            for run in steps[4:8]:
                 run()
             second_half(1, work_ref[AWAY, NEAR], work_ref[AWAY, AWAY])
 
@@ -457,18 +487,14 @@
         return carry
 
     lax.fori_loop(0, 4, body, 0)
+    for run in steps[8:12]:
+        run()
     join_inverse(1)
-    for run in steps[16:]:
+    for run in steps[12:]:
         run()
     wires.drain()
-    for number in range(2):
-        spread_drain(number)
-
-    @pl.when(col == 0)
-    def _():
-        @pl.loop(1, COLS)
-        def _(step):
-            lead_copy(step).wait_send()
+    for index in range(2):
+        spread_drain(index)
 
 
 def gather_tiles(order, own_factor, front):
@@ -479,16 +505,18 @@
         out_shape=(
             jax.ShapeDtypeStruct((COLS, TILE, TILE), F32),
             jax.ShapeDtypeStruct((LEAD, COL_WIDTH), F32),
+            jax.ShapeDtypeStruct((LEAD, LEAD), F32),
         ),
         in_specs=[pl.BlockSpec(memory_space=pltpu.SMEM), vmem, anywhere],
-        out_specs=(vmem, vmem),
+        out_specs=(vmem,) * 3,
         scratch_shapes=[
             pltpu.VMEM((COLS, TILE, CW), F32),
             pltpu.VMEM((TILE, CW), BF16),
             pltpu.VMEM((TILE, CW), BF16),
-            pltpu.SemaphoreType.DMA((72,)),
-            pltpu.SemaphoreType.DMA((72,)),
-            pltpu.SemaphoreType.DMA((2,)),
+            pltpu.VMEM((SLICE, LEAD), F32),
+            pltpu.SemaphoreType.DMA((136,)),
+            pltpu.SemaphoreType.DMA((136,)),
+            pltpu.SemaphoreType.DMA((4,)),
         ],
         compiler_params=pltpu.CompilerParams(
             collective_id=0, has_side_effects=True, vmem_limit_bytes=56 * 2**20
@@ -497,7 +525,7 @@
     )(order, own_factor, front)
 
 
-def spread_panel(top):
+def spread_panel(top, lead):
     vmem = pl.BlockSpec(memory_space=pltpu.VMEM)
     return pl.pallas_call(
         spread_kernel,
@@ -508,15 +536,14 @@
             jax.ShapeDtypeStruct((2, TILE, TILE), F32),
             jax.ShapeDtypeStruct((TILE, TILE), F32),
         ),
-        in_specs=[vmem],
+        in_specs=[vmem, vmem],
         out_specs=(vmem,) * 5,
         scratch_shapes=[
             pltpu.VMEM((BLOCK, BLOCK), F32),
             pltpu.VMEM((4, BLOCK, BLOCK), F32),
             pltpu.VMEM((TILE, TILE), F32),
-            pltpu.VMEM((LEAD, LEAD), F32),
-            pltpu.SemaphoreType.DMA((136,)),
-            pltpu.SemaphoreType.DMA((136,)),
+            pltpu.SemaphoreType.DMA((80,)),
+            pltpu.SemaphoreType.DMA((80,)),
             pltpu.SemaphoreType.DMA((3,)),
         ],
         compiler_params=pltpu.CompilerParams(
@@ -526,7 +553,7 @@
             flops=30 * 10**9, bytes_accessed=20 * 2**20, transcendentals=0
         ),
         name="spread",
-    )(top)
+    )(top, lead)
 
 
 def eliminate(block_ref, upper_ref, inverse_ref):
@@ -679,7 +706,7 @@
                 pltpu.VMEM((LEAD, COL_WIDTH), BF16),
             ],
         ),
-        compiler_params=pltpu.CompilerParams(vmem_limit_bytes=40 * 2**20),
+        compiler_params=pltpu.CompilerParams(vmem_limit_bytes=58 * 2**20),
         cost_estimate=pl.CostEstimate(
             flops=9 * PANEL_ROWS * COL_WIDTH * LEAD,
             bytes_accessed=30 * 2**20,
@@ -698,7 +725,7 @@
     ids = jnp.arange(COLS, dtype=jnp.int32)
     wanted = jnp.concatenate([ids, here_col[None].astype(jnp.int32)])
     order = jnp.sum(jnp.where(my_blocks[None, :] == wanted[:, None], ids[None, :], 0), axis=1)
-    outgoing, top = gather_tiles(order, own_factor, parent_front)
+    outgoing, top, lead = gather_tiles(order, own_factor, parent_front)
     outgoing = outgoing.reshape(ROWS, 2, TILE, TILE)
     tiles = lax.all_to_all(outgoing, "row", split_axis=0, concat_axis=0, tiled=True)
 
@@ -716,10 +743,10 @@
         jnp.sum(jnp.where(block_of == here_col, parent_index, 0), axis=1) - here_col * PCT
     )
 
-    top, row_places, col_places = lax.optimization_barrier(
-        (top, row_places.astype(jnp.int32), col_places.astype(jnp.int32))
-    )
-    pan, upper, side, full, low = spread_panel(top)
+    top, lead, row_places, col_places = lax.optimization_barrier(
+        (top, lead, row_places.astype(jnp.int32), col_places.astype(jnp.int32))
+    )
+    pan, upper, side, full, low = spread_panel(top, lead)
     panel_out, schur = finish(
         row_places,
         col_places,

time: 180 us -> 168 us (0.933)
  Pallas kernels: 163 us -> 156 us
  local copies, waits for them, and re-layouts: 6.14 us -> 0.11 us
    pallas_call x1, Pallas kernels: 76.3 us -> 49.9 us  [spread_panel(): pl.pallas_call(spread_kernel, out_shape=(jax.ShapeDtypeStruct((2, LEAD, C...]
    pallas_call x1, Pallas kernels: 61.6 us -> 79.1 us  [gather_tiles(): pl.pallas_call(gather_kernel, out_shape=(jax.ShapeDtypeStruct((COLS, TILE...]
    unnamed x16 -> x4, local copies, waits for them, and re-layouts: 6.04 us -> 0.02 us
  transfers between devices with their start and end apart: 1 -> 1, of which waited for: 0 -> 0; matrix products, arithmetic and copies ran while one was open for 0% -> 1% of each run, Pallas kernels for 43% -> 30%
where the time goes in v9:
time: 168 us; the launch traced here: 167 us
  Pallas kernels  156 us (93%)
  starting transfers between devices  5.02 us (3%)
  matrix products  2.89 us (2%)
  other arithmetic  2.88 us (2%)
    pallas_call x1, Pallas kernels, gather_tiles(): pl.pallas_call(gather_kernel, out_shape=(jax.ShapeDtypeStruct((COLS, TILE...  79.1 us
    pallas_call x1, Pallas kernels, spread_panel(): pl.pallas_call(spread_kernel, out_shape=(jax.ShapeDtypeStruct((2, LEAD, C...  49.9 us
    pallas_call x1, Pallas kernels, finish(): pl.pallas_call(final_kernel, out_shape=(jax.ShapeDtypeStruct((PANEL_ROWS,...  26.6 us
    all_to_all x1, starting transfers between devices, per_device(): lax.all_to_all(outgoing, 'row', split_axis=0, concat_axis=0, tiled=True)  5.02 us
  transfers between devices with their start and end apart: 1, of which 0 were waited for; matrix products, arithmetic and copies ran while one was open for 1% of the time, Pallas kernels for 30%

profile of v9, /device:TPU:0, one launch (start us, length us, event | category | flops | bytes accessed | tf_op | source)
XLA Modules:
  0.0 167.2 jit_solution(12945599131461133807)
XLA Ops:
  0.6 0.0 copy-start
  0.7 0.9 select_reduce_fusion.2
  1.5 0.1 pad_add_fusion
  1.6 0.6 select_reduce_fusion.1.order_ref
  2.2 0.0 copy-done
  2.2 2.9 %fusion.own_ref = f32[256,512]{1,0:T(8,128)} fusion(f32[1,512,512]{2,1,0:T(8,128)S(1)} %copy-done, f32[1,256,512]{2,1,0:T(8,128)} %param.5), kind=kOutput, calls=%fused_computation | convolution fusion | flops 805306368 | bytes 2097152 | tf_op jit(solution)/shard_map/dot_general | solution.py:33
  5.1 79.1 %gather.1 = (f32[16,256,256]{2,1,0:T(8,128)}, f32[512,1024]{1,0:T(8,128)}, f32[512,512]{1,0:T(8,128)}) custom-call(s32[17]{0:T(128)} %select_reduce_fusion.1.order_ref, f32[256,512]{1,0:T(8,128)} %fusion.own_ref, f32[2048,1024]{1,0:T(8,128)} %front_ref.3), custom_call_target="tpu_custom_call" | custom-call | tf_op jit(solution)/shard_map/gather/pallas_call | solution.py:503
  84.3 0.0 copy-start.1
  84.3 5.0 %all-to-all-start = ((f32[8,2,256,256]{3,2,1,0:T(8,128)}), f32[8,2,256,256]{3,2,1,0:T(8,128)}, u32[]{:S(2)}, u32[]{:S(2)}) async-start(f32[8,2,256,256]{3,2,1,0:T(8,128)} %bitcast.10), calls=%async_computation | async-start | bytes 8388608 | tf_op jit(solution)/shard_map/all_to_all | solution.py:730
  89.3 0.0 copy-done.1
  89.3 0.2 select_reduce_fusion
  89.5 0.1 copy.6
  89.6 0.5 broadcast_subtract_fusion.1.cols_ref
  90.1 0.6 broadcast_subtract_fusion.rows_ref
  90.7 49.9 %spread.1 = (f32[2,512,1024]{2,1,0:T(8,128)}, f32[4,128,128]{2,1,0:T(8,128)}, f32[2,128,128]{2,1,0:T(8,128)}, f32[2,256,256]{2,1,0:T(8,128)}, f32[256,256]{1,0:T(8,128)}) custom-call(f32[512,1024]{1,0:T(8,128)} %get-tuple-element.18.top_ref, f32[512,512]{1,0:T(8,128)} %get-tuple-element.19.lead_ref), custom_call_target="tpu_custom_call" | custom-call | flops 30000001024 | bytes 20971520 | tf_op jit(solution)/shard_map/spread/pallas_call | solution.py:530
  140.6 0.0 all-to-all-done.tiles_ref
  140.6 26.6 %finish.1 = (f32[2048,512]{1,0:T(8,128)}, f32[2048,1024]{1,0:T(8,128)}) custom-call(s32[8,2]{1,0:T(8,128)} %broadcast_subtract_fusion.rows_ref, s32[8]{0:T(128)} %broadcast_subtract_fusion.1.cols_ref, f32[2048,1024]{1,0:T(8,128)} %front_ref.3, f32[2,512,1024]{2,1,0:T(8,128)} %get-tuple-element.20.pan_ref, f32[512,1024]{1,0:T(8,128)} %get-tuple-element.18.top_ref, ...), custom_call_target="tpu_custom_call" | custom-call | flops 9663676416 | bytes 31457280 | tf_op jit(solution)/shard_map/finish/pallas_call | solution.py:680
  (3 shorter events, 0.0 us)
Async XLA Ops:
  0.6 1.6 copy-start
  84.3 5.0 %copy-start.1 = (s32[8,16]{1,0:T(8,128)S(1)}, s32[8,16]{1,0:T(8,128)}, u32[]{:S(2)}) copy-start(s32[8,16]{1,0:T(8,128)} %param.7) | copy-start | bytes 1540
  84.3 56.3 %all-to-all-start = ((f32[8,2,256,256]{3,2,1,0:T(8,128)}), f32[8,2,256,256]{3,2,1,0:T(8,128)}, u32[]{:S(2)}, u32[]{:S(2)}) async-start(f32[8,2,256,256]{3,2,1,0:T(8,128)} %bitcast.10), calls=%async_computation | async-start | bytes 8388608 | tf_op jit(solution)/shard_map/all_to_all | solution.py:730

commit v10 on v9

--- a/solution.py
+++ b/solution.py
@@ -270,7 +270,9 @@
         )
 
     def down_copy(step):
-        return remote(corner_ref, corner_ref, down + step, corner_recv, step, col)
+        start = pl.multiple_of(lax.rem(step, 2) * (SLICE // 2), SLICE // 2)
+        part = corner_ref.at[pl.ds(start, SLICE // 2)]
+        return remote(part, part, down + step, corner_recv, step, col)
 
     def each_along(act):
         @pl.when((row == 0) & (col == 0))
@@ -300,7 +302,7 @@
 
         @pl.when((row == 0) & (col != 0))
         def _():
-            down_copy(1).wait_recv()
+            along_copy(1).wait_recv()
 
         each_down(lambda copy: copy.start())
 
@@ -309,21 +311,26 @@
         def _():
             down_copy(1).wait_recv()
 
-    def lead_piece(slot, half, part):
-        size = SLICE // 2
+    half_slice = SLICE // 2
+
+    def lead_piece(slot, _, part):
         if part == 0:
-            return lead_ref.at[pl.ds(slot * SLICE + half * size, size)]
-        base = slot * SLICE + half * size + (size // 2) * (part - 1)
-        return lead_ref.at[pl.ds(base, size // 2)]
+            return lead_ref.at[slot, core]
+        return lead_ref.at[slot, core, pl.ds((half_slice // 2) * (part - 1), half_slice // 2)]
+
+    def own_corner():
+        return corner_ref.at[pl.ds(pl.multiple_of(core * half_slice, half_slice), half_slice)]
+
+    swap_sem = fresh()
+
+    def swap_copy():
+        mine = lead_ref.at[:, core]
+        return remote(mine, mine, swap_sem, swap_sem, row + 1 - 2 * core, col)
 
     rings = [
         wires.ring(h, factor_piece, lambda h=h: own_ref.at[pl.ds(h * 128, 128)]) for h in range(2)
     ]
-    size = SLICE // 2
-    lead_rings = [
-        wires.ring(h, lead_piece, lambda h=h: corner_ref.at[pl.ds(h * size, size)])
-        for h in range(2)
-    ]
+    lead_ring = wires.ring(0, lead_piece, own_corner)
     steps = ring_steps(rings)
     corner_start()
     for run in steps[:4]:
@@ -342,13 +349,11 @@
     for run in steps[4 + 2 * (half_pieces + SIDE) :]:
         run()
     corner_wait()
-    keep_corner = pltpu.make_async_copy(
-        corner_ref, lead_ref.at[pl.ds(col * SLICE, SLICE)], local_sem.at[3]
-    )
+    keep_corner = pltpu.make_async_copy(own_corner(), lead_ref.at[col, core], local_sem.at[3])
     keep_corner.start()
     keep_own.wait()
-    lead_steps = ring_steps(lead_rings)
-    for run in lead_steps[:4]:
+    lead_steps = ring_steps([lead_ring])
+    for run in lead_steps[:2]:
         run()
     high_ref[...], low_ref[...] = halves(all_ref[order_ref[COLS]])
 
@@ -358,9 +363,13 @@
 
     for part in range(COLS // 2):
         pl.loop(2 * part, 2 * part + 2)(tile)
-        for run in lead_steps[4 + 4 * part : 8 + 4 * part]:
+        for run in lead_steps[2 + 2 * part : 4 + 2 * part]:
             run()
-    keep_corner.wait()
+        if part == COLS // 2 - 2:
+            keep_corner.wait()
+            swap_copy().start()
+    swap_copy().wait_recv()
+    swap_copy().wait_send()
     wires.drain()
     for number in range(half_pieces):
         top_drain(number)
@@ -375,8 +384,14 @@
 AWAY = slice(BLOCK, TILE)
 
 
+def triangular(inverses, low, block):
+    first = three_pass(inverses[0], halves(block[:TILE]), ((1,), (0,)))
+    rest = block[TILE:] - three_pass(low, halves(first), ((1,), (0,)))
+    return first, three_pass(inverses[1], halves(rest), ((1,), (0,)))
+
+
 def spread_kernel(
-    top_ref, lead_ref, pan_ref, upper_ref, side_ref, full_ref, low_ref,
+    top_ref, lead_ref, pan_ref, upper_ref, side_ref, full_ref, low_ref, cols_ref,
     block_ref, inv_ref, work_ref, send_sem, recv_sem, local_sem,
 ):
     wires = Wires(send_sem, recv_sem)
@@ -490,7 +505,31 @@
     for run in steps[8:12]:
         run()
     join_inverse(1)
-    for run in steps[12:]:
+    inverses = [halves(full_ref[t]) for t in range(2)]
+    low = halves(low_ref[...])
+    blank = jnp.zeros((BLOCK, BLOCK), F32)
+    for part in range(PCT):
+        for run in steps[12 + 2 * part : 14 + 2 * part]:
+            run()
+        lanes = slice(part * TILE, (part + 1) * TILE)
+        first, second = triangular(inverses, low, top_ref[:, lanes])
+        cols_ref[:TILE, lanes] = first
+        cols_ref[TILE:, lanes] = second
+
+    @pl.when(col == 0)
+    def _():
+        for t in range(2):
+            for r, c, value in (
+                (0, 0, upper_ref[2 * t]),
+                (0, 1, side_ref[t].T),
+                (1, 0, blank),
+                (1, 1, upper_ref[2 * t + 1]),
+            ):
+                r0, c0 = t * TILE + r * BLOCK, t * TILE + c * BLOCK
+                cols_ref[r0 : r0 + BLOCK, c0 : c0 + BLOCK] = value
+        cols_ref[TILE:, :TILE] = jnp.zeros((TILE, TILE), F32)
+
+    for run in steps[20:]:
         run()
     wires.drain()
     for index in range(2):
@@ -505,7 +544,7 @@
         out_shape=(
             jax.ShapeDtypeStruct((COLS, TILE, TILE), F32),
             jax.ShapeDtypeStruct((LEAD, COL_WIDTH), F32),
-            jax.ShapeDtypeStruct((LEAD, LEAD), F32),
+            jax.ShapeDtypeStruct((COLS, 2, SLICE // 2, LEAD), F32),
         ),
         in_specs=[pl.BlockSpec(memory_space=pltpu.SMEM), vmem, anywhere],
         out_specs=(vmem,) * 3,
@@ -535,9 +574,10 @@
             jax.ShapeDtypeStruct((2, BLOCK, BLOCK), F32),
             jax.ShapeDtypeStruct((2, TILE, TILE), F32),
             jax.ShapeDtypeStruct((TILE, TILE), F32),
+            jax.ShapeDtypeStruct((LEAD, COL_WIDTH), F32),
         ),
         in_specs=[vmem, vmem],
-        out_specs=(vmem,) * 5,
+        out_specs=(vmem,) * 6,
         scratch_shapes=[
             pltpu.VMEM((BLOCK, BLOCK), F32),
             pltpu.VMEM((4, BLOCK, BLOCK), F32),
@@ -607,43 +647,20 @@
 
 
 def final_kernel(
-    rows_ref, cols_ref, front_ref, pan_ref, top_ref, upper_ref, side_ref, full_ref, low_ref,
-    tiles_ref, panel_ref, out_ref, right_ref, high_ref, small_ref,
+    rows_ref, cols_ref, front_ref, pan_ref, right_ref, upper_ref, side_ref, full_ref, low_ref,
+    tiles_ref, panel_ref, out_ref, high_ref, small_ref,
 ):
     row = lax.axis_index("row")
-    col = lax.axis_index("col")
     step = pl.program_id(0)
     inverses = [halves(full_ref[t]) for t in range(2)]
     low = halves(low_ref[...])
     blank = jnp.zeros((BLOCK, BLOCK), F32)
 
-    def chunk(block):
-        first = three_pass(inverses[0], halves(block[:TILE]), ((1,), (0,)))
-        rest = block[TILE:] - three_pass(low, halves(first), ((1,), (0,)))
-        return first, three_pass(inverses[1], halves(rest), ((1,), (0,)))
-
     @pl.when(step == 0)
     def _():
-        for part in range(PCT):
-            lanes = slice(part * TILE, (part + 1) * TILE)
-            right_ref[:TILE, lanes], right_ref[TILE:, lanes] = chunk(top_ref[:, lanes])
-
-        @pl.when(col == 0)
-        def _():
-            for t in range(2):
-                for r, c, value in (
-                    (0, 0, upper_ref[2 * t]),
-                    (0, 1, side_ref[t].T),
-                    (1, 0, blank),
-                    (1, 1, upper_ref[2 * t + 1]),
-                ):
-                    r0, c0 = t * TILE + r * BLOCK, t * TILE + c * BLOCK
-                    right_ref[r0 : r0 + BLOCK, c0 : c0 + BLOCK] = value
-            right_ref[TILE:, :TILE] = jnp.zeros((TILE, TILE), F32)
-
         high_ref[...], small_ref[...] = halves(right_ref[...])
 
-    first, second = chunk(pan_ref[0])
+    first, second = triangular(inverses, low, pan_ref[0])
     panel_ref[:, :TILE] = first.T
     panel_ref[:, TILE:] = second.T
 
@@ -701,7 +718,6 @@
                 pl.BlockSpec((TILE, COL_WIDTH), lambda i, *_: (i, 0)),
             ),
             scratch_shapes=[
-                pltpu.VMEM((LEAD, COL_WIDTH), F32),
                 pltpu.VMEM((LEAD, COL_WIDTH), BF16),
                 pltpu.VMEM((LEAD, COL_WIDTH), BF16),
             ],
@@ -726,6 +742,7 @@
     wanted = jnp.concatenate([ids, here_col[None].astype(jnp.int32)])
     order = jnp.sum(jnp.where(my_blocks[None, :] == wanted[:, None], ids[None, :], 0), axis=1)
     outgoing, top, lead = gather_tiles(order, own_factor, parent_front)
+    lead = lead.reshape(LEAD, LEAD)
     outgoing = outgoing.reshape(ROWS, 2, TILE, TILE)
     tiles = lax.all_to_all(outgoing, "row", split_axis=0, concat_axis=0, tiled=True)
 
@@ -746,13 +763,13 @@
     top, lead, row_places, col_places = lax.optimization_barrier(
         (top, lead, row_places.astype(jnp.int32), col_places.astype(jnp.int32))
     )
-    pan, upper, side, full, low = spread_panel(top, lead)
+    pan, upper, side, full, low, cols = spread_panel(top, lead)
     panel_out, schur = finish(
         row_places,
         col_places,
         parent_front,
         pan,
-        top,
+        cols,
         upper,
         side,
         full,

time: 168 us -> 165 us (0.982)
  Pallas kernels: 156 us -> 152 us
    pallas_call x1, Pallas kernels: 26.6 us -> 23.9 us  [finish(): pl.pallas_call(final_kernel, out_shape=(jax.ShapeDtypeStruct((PANEL_ROWS,...]
  transfers between devices with their start and end apart: 1 -> 1, of which waited for: 0 -> 0; matrix products, arithmetic and copies ran while one was open for 1% -> 1% of each run, Pallas kernels for 30% -> 31%
where the time goes in v10:
time: 165 us; the launch traced here: 163 us
  Pallas kernels  152 us (92%)
  starting transfers between devices  4.56 us (3%)
  other arithmetic  2.99 us (2%)
  matrix products  2.89 us (2%)
    pallas_call x1, Pallas kernels, gather_tiles(): pl.pallas_call(gather_kernel, out_shape=(jax.ShapeDtypeStruct((COLS, TILE...  77.6 us
    pallas_call x1, Pallas kernels, spread_panel(): pl.pallas_call(spread_kernel, out_shape=(jax.ShapeDtypeStruct((2, LEAD, C...  50.7 us
    pallas_call x1, Pallas kernels, finish(): pl.pallas_call(final_kernel, out_shape=(jax.ShapeDtypeStruct((PANEL_ROWS,...  23.9 us
    all_to_all x1, starting transfers between devices, per_device(): lax.all_to_all(outgoing, 'row', split_axis=0, concat_axis=0, tiled=True)  4.56 us
  transfers between devices with their start and end apart: 1, of which 0 were waited for; matrix products, arithmetic and copies ran while one was open for 1% of the time, Pallas kernels for 31%

profile of v10, /device:TPU:0, one launch (start us, length us, event | category | flops | bytes accessed | tf_op | source)
XLA Modules:
  0.0 163.4 jit_solution(2314662079181483308)
XLA Ops:
  0.6 0.0 copy-start
  0.7 0.9 select_reduce_fusion.2
  1.5 0.1 pad_add_fusion
  1.6 0.7 select_reduce_fusion.1.order_ref
  2.3 0.0 copy-done
  2.3 2.9 %fusion.own_ref = f32[256,512]{1,0:T(8,128)} fusion(f32[1,512,512]{2,1,0:T(8,128)S(1)} %copy-done, f32[1,256,512]{2,1,0:T(8,128)} %param.5), kind=kOutput, calls=%fused_computation | convolution fusion | flops 805306368 | bytes 2097152 | tf_op jit(solution)/shard_map/dot_general | solution.py:33
  5.2 77.6 %gather.1 = (f32[16,256,256]{2,1,0:T(8,128)}, f32[512,1024]{1,0:T(8,128)}, f32[16,2,16,512]{3,2,1,0:T(8,128)}) custom-call(s32[17]{0:T(128)} %select_reduce_fusion.1.order_ref, f32[256,512]{1,0:T(8,128)} %fusion.own_ref, f32[2048,1024]{1,0:T(8,128)} %front_ref.3), custom_call_target="tpu_custom_call" | custom-call | tf_op jit(solution)/shard_map/gather/pallas_call | solution.py:542
  82.8 0.0 copy-start.1
  82.8 4.6 %all-to-all-start = ((f32[8,2,256,256]{3,2,1,0:T(8,128)}), f32[8,2,256,256]{3,2,1,0:T(8,128)}, u32[]{:S(2)}, u32[]{:S(2)}) async-start(f32[8,2,256,256]{3,2,1,0:T(8,128)} %bitcast.11), calls=%async_computation | async-start | bytes 8388608 | tf_op jit(solution)/shard_map/all_to_all | solution.py:747
  87.4 0.0 copy-done.1
  87.4 0.2 select_reduce_fusion
  87.6 0.1 copy.6
  87.7 0.5 broadcast_subtract_fusion.1.cols_ref
  88.3 0.6 broadcast_subtract_fusion.rows_ref
  88.9 50.7 %spread.1 = (f32[2,512,1024]{2,1,0:T(8,128)}, f32[4,128,128]{2,1,0:T(8,128)}, f32[2,128,128]{2,1,0:T(8,128)}, f32[2,256,256]{2,1,0:T(8,128)}, f32[256,256]{1,0:T(8,128)}, /*index=5*/f32[512,1024]{1,0:T(8,128)}) custom-call(f32[512,1024]{1,0:T(8,128)} %get-tuple-element.19.top_ref, f32[512,512]{1,0:T(8,128)} %bitcast.12), custom_call_target="tpu_custom_call" | custom-call | flops 30000001024 | bytes 20971520 | tf_op jit(solution)/shard_map/spread/pallas_call | solution.py:569
  139.6 0.0 all-to-all-done.tiles_ref
  139.6 23.9 %finish.1 = (f32[2048,512]{1,0:T(8,128)}, f32[2048,1024]{1,0:T(8,128)}) custom-call(s32[8,2]{1,0:T(8,128)} %broadcast_subtract_fusion.rows_ref, s32[8]{0:T(128)} %broadcast_subtract_fusion.1.cols_ref, f32[2048,1024]{1,0:T(8,128)} %front_ref.3, f32[2,512,1024]{2,1,0:T(8,128)} %get-tuple-element.21.pan_ref, f32[512,1024]{1,0:T(8,128)} %get-tuple-element.22.right_ref, ...), custom_call_target="tpu_custom_call" | custom-call | flops 9663676416 | bytes 31457280 | tf_op jit(solution)/shard_map/finish/pallas_call | solution.py:697
  (3 shorter events, 0.0 us)
Async XLA Ops:
  0.6 1.7 %copy-start = (f32[1,512,512]{2,1,0:T(8,128)S(1)}, f32[1,512,512]{2,1,0:T(8,128)}, u32[]{:S(2)}) copy-start(f32[1,512,512]{2,1,0:T(8,128)} %param.6) | copy-start | bytes 3145732
  82.8 4.6 %copy-start.1 = (s32[8,16]{1,0:T(8,128)S(1)}, s32[8,16]{1,0:T(8,128)}, u32[]{:S(2)}) copy-start(s32[8,16]{1,0:T(8,128)} %param.7) | copy-start | bytes 1540
  82.8 56.7 %all-to-all-start = ((f32[8,2,256,256]{3,2,1,0:T(8,128)}), f32[8,2,256,256]{3,2,1,0:T(8,128)}, u32[]{:S(2)}, u32[]{:S(2)}) async-start(f32[8,2,256,256]{3,2,1,0:T(8,128)} %bitcast.11), calls=%async_computation | async-start | bytes 8388608 | tf_op jit(solution)/shard_map/all_to_all | solution.py:747

commit v11 on v10

--- a/solution.py
+++ b/solution.py
@@ -332,21 +332,23 @@
     ]
     lead_ring = wires.ring(0, lead_piece, own_corner)
     steps = ring_steps(rings)
-    corner_start()
     for run in steps[:4]:
         run()
+    corner_start()
 
     @pl.when(row == 0)
     def _():
         load_top.wait()
 
+    for run in steps[4:8]:
+        run()
     for number in range(half_pieces + SIDE):
         top_step(number)
-        if number == 2:
+        if number == 6:
             corner_pass()
-        for run in steps[4 + 2 * number : 6 + 2 * number]:
+        for run in steps[8 + 2 * number : 10 + 2 * number]:
             run()
-    for run in steps[4 + 2 * (half_pieces + SIDE) :]:
+    for run in steps[8 + 2 * (half_pieces + SIDE) :]:
         run()
     corner_wait()
     keep_corner = pltpu.make_async_copy(own_corner(), lead_ref.at[col, core], local_sem.at[3])

time: 165 us -> 169 us (1.024)
  starting transfers between devices: 4.56 us -> 7.92 us
    all_to_all x1, starting transfers between devices: 4.56 us -> 7.92 us  [per_device(): lax.all_to_all(outgoing, 'row', split_axis=0, concat_axis=0, tiled=True)]
where the time goes in v11:
time: 169 us; the launch traced here: 167 us
  Pallas kernels  152 us (90%)
  starting transfers between devices  7.92 us (5%)
  other arithmetic  2.99 us (2%)
  matrix products  2.89 us (2%)
    pallas_call x1, Pallas kernels, gather_tiles(): pl.pallas_call(gather_kernel, out_shape=(jax.ShapeDtypeStruct((COLS, TILE...  77.2 us
    pallas_call x1, Pallas kernels, spread_panel(): pl.pallas_call(spread_kernel, out_shape=(jax.ShapeDtypeStruct((2, LEAD, C...  51.3 us
    pallas_call x1, Pallas kernels, finish(): pl.pallas_call(final_kernel, out_shape=(jax.ShapeDtypeStruct((PANEL_ROWS,...  23.8 us
    all_to_all x1, starting transfers between devices, per_device(): lax.all_to_all(outgoing, 'row', split_axis=0, concat_axis=0, tiled=True)  7.92 us
  transfers between devices with their start and end apart: 1, of which 0 were waited for; matrix products, arithmetic and copies ran while one was open for 1% of the time, Pallas kernels for 31%

profile of v11, /device:TPU:0, one launch (start us, length us, event | category | flops | bytes accessed | tf_op | source)
XLA Modules:
  0.0 167.0 jit_solution(12262964561868460281)
XLA Ops:
  0.6 0.0 copy-start
  0.7 0.9 select_reduce_fusion.2
  1.5 0.1 pad_add_fusion
  1.6 0.7 select_reduce_fusion.1.order_ref
  2.3 0.0 copy-done
  2.3 2.9 %fusion.own_ref = f32[256,512]{1,0:T(8,128)} fusion(f32[1,512,512]{2,1,0:T(8,128)S(1)} %copy-done, f32[1,256,512]{2,1,0:T(8,128)} %param.5), kind=kOutput, calls=%fused_computation | convolution fusion | flops 805306368 | bytes 2097152 | tf_op jit(solution)/shard_map/dot_general | solution.py:33
  5.2 77.2 %gather.1 = (f32[16,256,256]{2,1,0:T(8,128)}, f32[512,1024]{1,0:T(8,128)}, f32[16,2,16,512]{3,2,1,0:T(8,128)}) custom-call(s32[17]{0:T(128)} %select_reduce_fusion.1.order_ref, f32[256,512]{1,0:T(8,128)} %fusion.own_ref, f32[2048,1024]{1,0:T(8,128)} %front_ref.3), custom_call_target="tpu_custom_call" | custom-call | tf_op jit(solution)/shard_map/gather/pallas_call | solution.py:544
  82.4 0.0 copy-start.1
  82.4 7.9 %all-to-all-start = ((f32[8,2,256,256]{3,2,1,0:T(8,128)}), f32[8,2,256,256]{3,2,1,0:T(8,128)}, u32[]{:S(2)}, u32[]{:S(2)}) async-start(f32[8,2,256,256]{3,2,1,0:T(8,128)} %bitcast.11), calls=%async_computation | async-start | bytes 8388608 | tf_op jit(solution)/shard_map/all_to_all | solution.py:749
  90.3 0.0 copy-done.1
  90.4 0.2 select_reduce_fusion
  90.6 0.1 copy.6
  90.7 0.5 broadcast_subtract_fusion.1.cols_ref
  91.2 0.6 broadcast_subtract_fusion.rows_ref
  91.8 51.3 %spread.1 = (f32[2,512,1024]{2,1,0:T(8,128)}, f32[4,128,128]{2,1,0:T(8,128)}, f32[2,128,128]{2,1,0:T(8,128)}, f32[2,256,256]{2,1,0:T(8,128)}, f32[256,256]{1,0:T(8,128)}, /*index=5*/f32[512,1024]{1,0:T(8,128)}) custom-call(f32[512,1024]{1,0:T(8,128)} %get-tuple-element.19.top_ref, f32[512,512]{1,0:T(8,128)} %bitcast.12), custom_call_target="tpu_custom_call" | custom-call | flops 30000001024 | bytes 20971520 | tf_op jit(solution)/shard_map/spread/pallas_call | solution.py:571
  143.1 0.0 all-to-all-done.tiles_ref
  143.1 23.8 %finish.1 = (f32[2048,512]{1,0:T(8,128)}, f32[2048,1024]{1,0:T(8,128)}) custom-call(s32[8,2]{1,0:T(8,128)} %broadcast_subtract_fusion.rows_ref, s32[8]{0:T(128)} %broadcast_subtract_fusion.1.cols_ref, f32[2048,1024]{1,0:T(8,128)} %front_ref.3, f32[2,512,1024]{2,1,0:T(8,128)} %get-tuple-element.21.pan_ref, f32[512,1024]{1,0:T(8,128)} %get-tuple-element.22.right_ref, ...), custom_call_target="tpu_custom_call" | custom-call | flops 9663676416 | bytes 31457280 | tf_op jit(solution)/shard_map/finish/pallas_call | solution.py:699
  (3 shorter events, 0.0 us)
Async XLA Ops:
  0.6 1.7 %copy-start = (f32[1,512,512]{2,1,0:T(8,128)S(1)}, f32[1,512,512]{2,1,0:T(8,128)}, u32[]{:S(2)}) copy-start(f32[1,512,512]{2,1,0:T(8,128)} %param.6) | copy-start | bytes 3145732
  82.4 7.9 %copy-start.1 = (s32[8,16]{1,0:T(8,128)S(1)}, s32[8,16]{1,0:T(8,128)}, u32[]{:S(2)}) copy-start(s32[8,16]{1,0:T(8,128)} %param.7) | copy-start | bytes 1540
  82.4 60.7 %all-to-all-start = ((f32[8,2,256,256]{3,2,1,0:T(8,128)}), f32[8,2,256,256]{3,2,1,0:T(8,128)}, u32[]{:S(2)}, u32[]{:S(2)}) async-start(f32[8,2,256,256]{3,2,1,0:T(8,128)} %bitcast.11), calls=%async_computation | async-start | bytes 8388608 | tf_op jit(solution)/shard_map/all_to_all | solution.py:749

commit v12 on v11

--- a/solution.py
+++ b/solution.py
@@ -332,9 +332,9 @@
     ]
     lead_ring = wires.ring(0, lead_piece, own_corner)
     steps = ring_steps(rings)
+    corner_start()
     for run in steps[:4]:
         run()
-    corner_start()
 
     @pl.when(row == 0)
     def _():
@@ -342,10 +342,9 @@
 
     for run in steps[4:8]:
         run()
+    corner_pass()
     for number in range(half_pieces + SIDE):
         top_step(number)
-        if number == 6:
-            corner_pass()
         for run in steps[8 + 2 * number : 10 + 2 * number]:
             run()
     for run in steps[8 + 2 * (half_pieces + SIDE) :]:

time: 169 us -> 169 us (level)
  no operation moved by 1% of the time
where the time goes in v12:
time: 169 us; the launch traced here: 167 us
  Pallas kernels  152 us (90%)
  starting transfers between devices  7.8 us (5%)
  other arithmetic  2.99 us (2%)
  matrix products  2.89 us (2%)
    pallas_call x1, Pallas kernels, gather_tiles(): pl.pallas_call(gather_kernel, out_shape=(jax.ShapeDtypeStruct((COLS, TILE...  76.9 us
    pallas_call x1, Pallas kernels, spread_panel(): pl.pallas_call(spread_kernel, out_shape=(jax.ShapeDtypeStruct((2, LEAD, C...  51.4 us
    pallas_call x1, Pallas kernels, finish(): pl.pallas_call(final_kernel, out_shape=(jax.ShapeDtypeStruct((PANEL_ROWS,...  23.8 us
    all_to_all x1, starting transfers between devices, per_device(): lax.all_to_all(outgoing, 'row', split_axis=0, concat_axis=0, tiled=True)  7.8 us
  transfers between devices with their start and end apart: 1, of which 0 were waited for; matrix products, arithmetic and copies ran while one was open for 1% of the time, Pallas kernels for 31%

profile of v12, /device:TPU:0, one launch (start us, length us, event | category | flops | bytes accessed | tf_op | source)
XLA Modules:
  0.0 166.5 jit_solution(11326639913686512824)
XLA Ops:
  0.6 0.0 copy-start
  0.7 0.9 select_reduce_fusion.2
  1.5 0.1 pad_add_fusion
  1.6 0.7 select_reduce_fusion.1.order_ref
  2.3 0.0 copy-done
  2.3 2.9 %fusion.own_ref = f32[256,512]{1,0:T(8,128)} fusion(f32[1,512,512]{2,1,0:T(8,128)S(1)} %copy-done, f32[1,256,512]{2,1,0:T(8,128)} %param.5), kind=kOutput, calls=%fused_computation | convolution fusion | flops 805306368 | bytes 2097152 | tf_op jit(solution)/shard_map/dot_general | solution.py:33
  5.2 76.9 %gather.1 = (f32[16,256,256]{2,1,0:T(8,128)}, f32[512,1024]{1,0:T(8,128)}, f32[16,2,16,512]{3,2,1,0:T(8,128)}) custom-call(s32[17]{0:T(128)} %select_reduce_fusion.1.order_ref, f32[256,512]{1,0:T(8,128)} %fusion.own_ref, f32[2048,1024]{1,0:T(8,128)} %front_ref.3), custom_call_target="tpu_custom_call" | custom-call | tf_op jit(solution)/shard_map/gather/pallas_call | solution.py:543
  82.1 0.0 copy-start.1
  82.1 7.8 %all-to-all-start = ((f32[8,2,256,256]{3,2,1,0:T(8,128)}), f32[8,2,256,256]{3,2,1,0:T(8,128)}, u32[]{:S(2)}, u32[]{:S(2)}) async-start(f32[8,2,256,256]{3,2,1,0:T(8,128)} %bitcast.11), calls=%async_computation | async-start | bytes 8388608 | tf_op jit(solution)/shard_map/all_to_all | solution.py:748
  89.9 0.0 copy-done.1
  89.9 0.2 select_reduce_fusion
  90.1 0.1 copy.6
  90.2 0.5 broadcast_subtract_fusion.1.cols_ref
  90.7 0.6 broadcast_subtract_fusion.rows_ref
  91.3 51.4 %spread.1 = (f32[2,512,1024]{2,1,0:T(8,128)}, f32[4,128,128]{2,1,0:T(8,128)}, f32[2,128,128]{2,1,0:T(8,128)}, f32[2,256,256]{2,1,0:T(8,128)}, f32[256,256]{1,0:T(8,128)}, /*index=5*/f32[512,1024]{1,0:T(8,128)}) custom-call(f32[512,1024]{1,0:T(8,128)} %get-tuple-element.19.top_ref, f32[512,512]{1,0:T(8,128)} %bitcast.12), custom_call_target="tpu_custom_call" | custom-call | flops 30000001024 | bytes 20971520 | tf_op jit(solution)/shard_map/spread/pallas_call | solution.py:570
  142.7 0.0 all-to-all-done.tiles_ref
  142.7 23.8 %finish.1 = (f32[2048,512]{1,0:T(8,128)}, f32[2048,1024]{1,0:T(8,128)}) custom-call(s32[8,2]{1,0:T(8,128)} %broadcast_subtract_fusion.rows_ref, s32[8]{0:T(128)} %broadcast_subtract_fusion.1.cols_ref, f32[2048,1024]{1,0:T(8,128)} %front_ref.3, f32[2,512,1024]{2,1,0:T(8,128)} %get-tuple-element.21.pan_ref, f32[512,1024]{1,0:T(8,128)} %get-tuple-element.22.right_ref, ...), custom_call_target="tpu_custom_call" | custom-call | flops 9663676416 | bytes 31457280 | tf_op jit(solution)/shard_map/finish/pallas_call | solution.py:698
  (3 shorter events, 0.0 us)
Async XLA Ops:
  0.6 1.7 %copy-start = (f32[1,512,512]{2,1,0:T(8,128)S(1)}, f32[1,512,512]{2,1,0:T(8,128)}, u32[]{:S(2)}) copy-start(f32[1,512,512]{2,1,0:T(8,128)} %param.6) | copy-start | bytes 3145732
  82.1 7.8 %copy-start.1 = (s32[8,16]{1,0:T(8,128)S(1)}, s32[8,16]{1,0:T(8,128)}, u32[]{:S(2)}) copy-start(s32[8,16]{1,0:T(8,128)} %param.7) | copy-start | bytes 1540
  82.1 60.6 %all-to-all-start = ((f32[8,2,256,256]{3,2,1,0:T(8,128)}), f32[8,2,256,256]{3,2,1,0:T(8,128)}, u32[]{:S(2)}, u32[]{:S(2)}) async-start(f32[8,2,256,256]{3,2,1,0:T(8,128)} %bitcast.11), calls=%async_computation | async-start | bytes 8388608 | tf_op jit(solution)/shard_map/all_to_all | solution.py:748
